TPU v7x, 128 devices: a whole 4x4x4 slice. The times are simulated.
128 devices in a mesh: row: 8 (over y_hi, z), col: 16 (over y_lo, x, core).
Axes of the slice: x: 4, y: 4 (y_hi: 2, y_lo: 2; y = y_hi * 2 + y_lo), z: 4, core: 2. Of those that a mesh axis runs over, the one named last changes fastest.
Arguments:
- a_blocks: float32 [8, 16, 32, 128, 128], P('row', 'col'), may hold values from -1 to 1
- a_rows: int32 [8, 16, 32], P('row', 'col'), may hold values from 0 to 127, as said below
- a_cols: int32 [8, 16, 32], P('row', 'col'), may hold values from 0 to 15, as said below
- a_counts: int32 [8, 16, 16], P('row', 'col'), may hold values from 0 to 2, as said below
- b_blocks: float32 [8, 16, 32, 128, 128], P('row', 'col'), may hold values from -1 to 1
- b_rows: int32 [8, 16, 32], P('row', 'col'), may hold values from 0 to 15, as said below
- b_cols: int32 [8, 16, 32], P('row', 'col'), may hold values from 0 to 63, as said below
- b_counts: int32 [8, 16, 16], P('row', 'col'), may hold values from 0 to 2, as said below
- out_mask: int32 [128, 64], P('row', 'col'), may hold values 0 or 1
Outputs:
- square: float32 [16384, 8192], P('row', 'col')
Inputs may be any that keep to these rules, and one draw needn't show every extreme that they name: a_counts[i, j, k] is the number of counted slots of device (i, j)'s list with inner block index k, at most 2; for every i and k some device (i, j) has exactly 2. The counted slots come first in the list, ordered by inner block index. `a_rows`: a device (i, j) lists only block rows from i * 16 to (i + 1) * 16 - 1; no block (r, k) is listed twice among counted slots. `a_cols`: on counted slots, the inner block index agrees with a_counts. b_counts[i, j, k] is the number of counted slots of device (i, j)'s list with inner block index k, at most 2; for every j and k some device (i, j) has exactly 2. The counted slots come first in the list, ordered by inner block index. `b_rows`: on counted slots, the inner block index agrees with b_counts. `b_cols`: a device (i, j) lists only block columns from j * 4 to (j + 1) * 4 - 1; no block (k, c) is listed twice among counted slots.
All inputs are finite; a program needn't handle non-finite values. No bound on the sum of `out_mask` on one device may be relied on, other than what follows from the above.
Results may differ from a plain program's by a relative error of at most 0.00007.
Values sent between devices are 32-bit elements; how exact they have to be, the bound alone decides.
No kernel may reach another device: no remote copies, remote signals or barrier semaphores. Data moves between devices by JAX's collectives and lax.ppermute only.
A program may use at most 64 MiB of HBM per device.

v0:
```python
import jax
import jax.numpy as jnp
from jax import lax
from jax.sharding import PartitionSpec as P

CAP = 2


def shifted(block, axis, distance):
    devices = range(lax.axis_size(axis))
    route = [((i - distance) % len(devices), i) for i in devices]
    return lax.ppermute(block, axis, route)


def table_pick(table, index):
    chosen = index[:, None] == jnp.arange(table.shape[0], dtype=jnp.int32)[None, :]
    return jnp.sum(jnp.where(chosen, table[None, :], 0), axis=1)


def segment_ranks(counts, inner_index, seg_width, seg_total):
    seg_counts = counts.reshape((seg_total, seg_width)).sum(axis=1)
    seg_starts = jnp.cumsum(seg_counts) - seg_counts
    slot_index = jnp.arange(inner_index.shape[0], dtype=jnp.int32)
    segment = inner_index // seg_width
    ranks = slot_index - table_pick(seg_starts, segment)
    usable = slot_index < jnp.sum(counts)
    return (segment, ranks, usable)


def fill_panel(received, where, panel_slots):
    block_width = received.shape[-1]
    flat_where = where.reshape(-1)
    flat_blocks = received.reshape((-1, block_width, block_width))
    target = jnp.where(flat_where >= 0, flat_where, panel_slots)
    empty = jnp.zeros((panel_slots, block_width, block_width), jnp.float32)
    return empty.at[target].set(flat_blocks, mode="drop")


def per_device(a_blocks, a_rows, a_cols, a_counts, b_blocks, b_rows, b_cols, b_counts, out_mask):
    n_row = lax.axis_size("row")
    n_col = lax.axis_size("col")
    row_id = lax.axis_index("row")
    col_id = lax.axis_index("col")
    block_width = a_blocks.shape[-1]
    inner_total = a_counts.shape[-1]
    rows_group = out_mask.shape[0]
    cols_group = out_mask.shape[1]
    seg_width = inner_total // n_col
    halves = n_col // n_row
    slots = seg_width * CAP
    a_list = a_blocks.reshape((-1, block_width, block_width))
    a_inner = a_cols.reshape(-1)
    a_owner = a_rows.reshape(-1)
    segment_a, ranks_a, usable_a = segment_ranks(a_counts.reshape(-1), a_inner, seg_width, n_col)
    target_col = (segment_a - row_id) % n_col
    place_a = (a_owner - row_id * rows_group) * seg_width + a_inner % seg_width
    a_send = jnp.zeros((n_col * slots, block_width, block_width), jnp.float32)
    a_where = jnp.full((n_col * slots,), -1, jnp.int32)
    target_a = jnp.where(usable_a, (target_col + 0) * slots + ranks_a, n_col * slots)
    a_send = a_send.at[target_a].set(a_list, mode="drop")
    a_where = a_where.at[target_a].set(place_a, mode="drop")
    a_got, a_got_where = (
        lax.all_to_all(
            a_send.reshape((n_col, slots, block_width, block_width)),
            "col",
            split_axis=0,
            concat_axis=0,
            tiled=True,
        ),
        lax.all_to_all(
            a_where.reshape((n_col, slots)), "col", split_axis=0, concat_axis=0, tiled=True
        ),
    )
    a_panel = fill_panel(a_got, a_got_where, rows_group * seg_width)
    a_matrix = a_panel.reshape((rows_group, seg_width, block_width, block_width)).transpose(
        (0, 2, 1, 3)
    )
    a_matrix = a_matrix.reshape((rows_group * block_width, seg_width * block_width))
    b_list = b_blocks.reshape((-1, block_width, block_width))
    b_inner = b_rows.reshape(-1)
    b_owner = b_cols.reshape(-1)
    segment_b, ranks_b, usable_b = segment_ranks(b_counts.reshape(-1), b_inner, seg_width, n_col)
    pair_b = segment_b % n_row
    half_b = segment_b // n_row
    target_row = (pair_b - col_id) % n_row
    per_row = halves * slots
    target_b = jnp.where(usable_b, target_row * per_row + half_b * slots + ranks_b, n_row * per_row)
    place_b = (
        half_b * seg_width * cols_group
        + b_inner % seg_width * cols_group
        + b_owner
        - col_id * cols_group
    )
    b_send = (
        jnp.zeros((n_row * per_row, block_width, block_width), jnp.float32)
        .at[target_b]
        .set(b_list, mode="drop")
    )
    b_where = jnp.full((n_row * per_row,), -1, jnp.int32).at[target_b].set(place_b, mode="drop")
    b_got, b_got_where = (
        lax.all_to_all(
            b_send.reshape((n_row, per_row, block_width, block_width)),
            "row",
            split_axis=0,
            concat_axis=0,
            tiled=True,
        ),
        lax.all_to_all(
            b_where.reshape((n_row, per_row)), "row", split_axis=0, concat_axis=0, tiled=True
        ),
    )
    b_panel = fill_panel(b_got, b_got_where, halves * seg_width * cols_group)
    b_matrix = b_panel.reshape((halves, seg_width, cols_group, block_width, block_width)).transpose(
        (0, 1, 3, 2, 4)
    )
    b_matrix = b_matrix.reshape((halves, seg_width * block_width, cols_group * block_width))

    def multiply(total_sum, a_current, b_current, turn_index):
        segment_now = (row_id + col_id + turn_index) % n_col
        half_now = segment_now // n_row
        b_used = lax.dynamic_index_in_dim(b_current, half_now, 0, keepdims=False)
        return total_sum + jnp.dot(
            a_current, b_used, precision=lax.Precision.HIGHEST, preferred_element_type=jnp.float32
        )

    def advance(turn_index, state_tuple):
        total_sum, a_current, b_current = state_tuple
        total_sum = multiply(total_sum, a_current, b_current, turn_index)
        a_current = shifted(a_current, "col", -1)
        b_current = shifted(b_current, "row", -1)
        return (total_sum, a_current, b_current)

    start_sum = jnp.zeros((rows_group * block_width, cols_group * block_width), jnp.float32)
    total_sum, a_current, b_current = lax.fori_loop(
        0, n_col - 1, advance, (start_sum, a_matrix, b_matrix)
    )
    total_sum = multiply(total_sum, a_current, b_current, n_col - 1)
    shaped = total_sum.reshape((rows_group, block_width, cols_group, block_width))
    shaped = shaped * out_mask.astype(jnp.float32)[:, None, :, None]
    return shaped.reshape((rows_group * block_width, cols_group * block_width))


def solution(mesh):
    in_specs = (
        P("row", "col", None, None, None),
        P("row", "col", None),
        P("row", "col", None),
        P("row", "col", None),
        P("row", "col", None, None, None),
        P("row", "col", None),
        P("row", "col", None),
        P("row", "col", None),
        P("row", "col"),
    )
    out_specs = P("row", "col")
    return jax.shard_map(
        per_device, mesh=mesh, in_specs=in_specs, out_specs=out_specs, check_vma=False
    )
```

profile of v0, /device:TPU:103, one launch (start us, length us, event | category | flops | bytes accessed | tf_op | source)
XLA Modules:
  0.0 518.3 jit_solution(8428561673365764052)
XLA Ops:
  33.3 7.2 %all-to-all-start.3 = ((f32[8,4,128,128]{3,2,1,0:T(8,128)}), f32[8,4,128,128]{3,2,1,0:T(8,128)S(1)}, u32[]{:S(2)}, u32[]{:S(2)}) async-start(f32[8,4,128,128]{3,2,1,0:T(8,128)} %bitcast.23), calls=%async_computation.3 | async-start | bytes 4194304 | tf_op jit(solution)/shard_map/all_to_all | solution.py:101
  48.3 18.2 %all-to-all-done.3 = f32[8,4,128,128]{3,2,1,0:T(8,128)S(1)} async-done(((f32[8,4,128,128]{3,2,1,0:T(8,128)}), f32[8,4,128,128]{3,2,1,0:T(8,128)S(1)}, u32[]{:S(2)}, u32[]{:S(2)}) %all-to-all-start.3) | async-done | bytes 2097184 | tf_op jit(solution)/shard_map/all_to_all | solution.py:101
  81.0 18.5 %all-to-all-done.1 = f32[16,2,128,128]{3,2,1,0:T(8,128)S(1)} async-done(((f32[16,2,128,128]{3,2,1,0:T(8,128)}), f32[16,2,128,128]{3,2,1,0:T(8,128)S(1)}, u32[]{:S(2)}, u32[]{:S(2)}) %all-to-all-start.1) | async-done | bytes 2097184 | tf_op jit(solution)/shard_map/all_to_all | solution.py:63
  105.0 400.5 %while.20 = (s32[]{:T(128)}, f32[2048,512]{0,1:T(8,128)}, f32[2048,128]{1,0:T(8,128)S(1)}, f32[2,128,512]{2,1,0:T(8,128)S(1)}, s32[]{:T(128)}, /*index=5*/s32[]{...) while((s32[]{:T(128)}, f32[2048,512]{0,1:T(8,128)}, ...), condition=%wide.region_13.14_spmd.clone, body=%wide.region_12.13_spmd.clone.sunk | while | flops 1612709888 | bytes 19137036 | solution.py:134
  111.4 23.2 %collective-permute-done.1 = f32[2,128,512]{2,1,0:T(8,128)S(1)} collective-permute-done((f32[2,128,512]{2,1,0:T(8,128)S(1)}, f32[2,128,512]{2,1,0:T(8,128)S(1)}, u32[]{:S(2)}, u32[]{:S(2)}) %collective-permute-start.1) | collective-permute-done | bytes 524320 | tf_op jit(solution)/shard_map/while/body/eval_jaxpr/ppermute | solution.py:12
  135.5 6.7 %bitcast_add_fusion.3 = f32[2048,512]{0,1:T(8,128)} fusion(f32[2048,512]{0,1:T(8,128)} %get-tuple-element.254, f32[2048,128]{1,0:T(8,128)S(1)} %copy.52, pred[]{:T(512)S(6)} %compare.52, f32[2,128,512]{2,1,0:T(8,128)S(1)} %copy.53, s32[]{:T(128)S(6)} %select_n.301), kind=kOutput, calls=%fused_computation.6.clone.1 | convolution fusion | flops 1612709888 | bytes 9699333 | tf_op jit(solution)/shard_map/while/body/eval_jaxpr/dot_general | solution.py:122
  142.2 19.0 %collective-permute-done.1 = f32[2,128,512]{2,1,0:T(8,128)S(1)} collective-permute-done((f32[2,128,512]{2,1,0:T(8,128)S(1)}, f32[2,128,512]{2,1,0:T(8,128)S(1)}, u32[]{:S(2)}, u32[]{:S(2)}) %collective-permute-start.1) | collective-permute-done | bytes 524320 | tf_op jit(solution)/shard_map/while/body/eval_jaxpr/ppermute | solution.py:12
  162.0 6.7 %bitcast_add_fusion.3 = f32[2048,512]{0,1:T(8,128)} fusion(f32[2048,512]{0,1:T(8,128)} %get-tuple-element.254, f32[2048,128]{1,0:T(8,128)S(1)} %copy.52, pred[]{:T(512)S(6)} %compare.52, f32[2,128,512]{2,1,0:T(8,128)S(1)} %copy.53, s32[]{:T(128)S(6)} %select_n.301), kind=kOutput, calls=%fused_computation.6.clone.1 | convolution fusion | flops 1612709888 | bytes 9699333 | tf_op jit(solution)/shard_map/while/body/eval_jaxpr/dot_general | solution.py:122
  168.7 18.8 %collective-permute-done.1 = f32[2,128,512]{2,1,0:T(8,128)S(1)} collective-permute-done((f32[2,128,512]{2,1,0:T(8,128)S(1)}, f32[2,128,512]{2,1,0:T(8,128)S(1)}, u32[]{:S(2)}, u32[]{:S(2)}) %collective-permute-start.1) | collective-permute-done | bytes 524320 | tf_op jit(solution)/shard_map/while/body/eval_jaxpr/ppermute | solution.py:12
  188.3 6.7 %bitcast_add_fusion.3 = f32[2048,512]{0,1:T(8,128)} fusion(f32[2048,512]{0,1:T(8,128)} %get-tuple-element.254, f32[2048,128]{1,0:T(8,128)S(1)} %copy.52, pred[]{:T(512)S(6)} %compare.52, f32[2,128,512]{2,1,0:T(8,128)S(1)} %copy.53, s32[]{:T(128)S(6)} %select_n.301), kind=kOutput, calls=%fused_computation.6.clone.1 | convolution fusion | flops 1612709888 | bytes 9699333 | tf_op jit(solution)/shard_map/while/body/eval_jaxpr/dot_general | solution.py:122
  195.0 19.2 %collective-permute-done.1 = f32[2,128,512]{2,1,0:T(8,128)S(1)} collective-permute-done((f32[2,128,512]{2,1,0:T(8,128)S(1)}, f32[2,128,512]{2,1,0:T(8,128)S(1)}, u32[]{:S(2)}, u32[]{:S(2)}) %collective-permute-start.1) | collective-permute-done | bytes 524320 | tf_op jit(solution)/shard_map/while/body/eval_jaxpr/ppermute | solution.py:12
  215.0 6.7 %bitcast_add_fusion.3 = f32[2048,512]{0,1:T(8,128)} fusion(f32[2048,512]{0,1:T(8,128)} %get-tuple-element.254, f32[2048,128]{1,0:T(8,128)S(1)} %copy.52, pred[]{:T(512)S(6)} %compare.52, f32[2,128,512]{2,1,0:T(8,128)S(1)} %copy.53, s32[]{:T(128)S(6)} %select_n.301), kind=kOutput, calls=%fused_computation.6.clone.1 | convolution fusion | flops 1612709888 | bytes 9699333 | tf_op jit(solution)/shard_map/while/body/eval_jaxpr/dot_general | solution.py:122
  221.7 18.8 %collective-permute-done.1 = f32[2,128,512]{2,1,0:T(8,128)S(1)} collective-permute-done((f32[2,128,512]{2,1,0:T(8,128)S(1)}, f32[2,128,512]{2,1,0:T(8,128)S(1)}, u32[]{:S(2)}, u32[]{:S(2)}) %collective-permute-start.1) | collective-permute-done | bytes 524320 | tf_op jit(solution)/shard_map/while/body/eval_jaxpr/ppermute | solution.py:12
  241.3 6.7 %bitcast_add_fusion.3 = f32[2048,512]{0,1:T(8,128)} fusion(f32[2048,512]{0,1:T(8,128)} %get-tuple-element.254, f32[2048,128]{1,0:T(8,128)S(1)} %copy.52, pred[]{:T(512)S(6)} %compare.52, f32[2,128,512]{2,1,0:T(8,128)S(1)} %copy.53, s32[]{:T(128)S(6)} %select_n.301), kind=kOutput, calls=%fused_computation.6.clone.1 | convolution fusion | flops 1612709888 | bytes 9699333 | tf_op jit(solution)/shard_map/while/body/eval_jaxpr/dot_general | solution.py:122
  248.0 19.2 %collective-permute-done.1 = f32[2,128,512]{2,1,0:T(8,128)S(1)} collective-permute-done((f32[2,128,512]{2,1,0:T(8,128)S(1)}, f32[2,128,512]{2,1,0:T(8,128)S(1)}, u32[]{:S(2)}, u32[]{:S(2)}) %collective-permute-start.1) | collective-permute-done | bytes 524320 | tf_op jit(solution)/shard_map/while/body/eval_jaxpr/ppermute | solution.py:12
  268.0 6.7 %bitcast_add_fusion.3 = f32[2048,512]{0,1:T(8,128)} fusion(f32[2048,512]{0,1:T(8,128)} %get-tuple-element.254, f32[2048,128]{1,0:T(8,128)S(1)} %copy.52, pred[]{:T(512)S(6)} %compare.52, f32[2,128,512]{2,1,0:T(8,128)S(1)} %copy.53, s32[]{:T(128)S(6)} %select_n.301), kind=kOutput, calls=%fused_computation.6.clone.1 | convolution fusion | flops 1612709888 | bytes 9699333 | tf_op jit(solution)/shard_map/while/body/eval_jaxpr/dot_general | solution.py:122
  274.7 18.8 %collective-permute-done.1 = f32[2,128,512]{2,1,0:T(8,128)S(1)} collective-permute-done((f32[2,128,512]{2,1,0:T(8,128)S(1)}, f32[2,128,512]{2,1,0:T(8,128)S(1)}, u32[]{:S(2)}, u32[]{:S(2)}) %collective-permute-start.1) | collective-permute-done | bytes 524320 | tf_op jit(solution)/shard_map/while/body/eval_jaxpr/ppermute | solution.py:12
  294.3 6.7 %bitcast_add_fusion.3 = f32[2048,512]{0,1:T(8,128)} fusion(f32[2048,512]{0,1:T(8,128)} %get-tuple-element.254, f32[2048,128]{1,0:T(8,128)S(1)} %copy.52, pred[]{:T(512)S(6)} %compare.52, f32[2,128,512]{2,1,0:T(8,128)S(1)} %copy.53, s32[]{:T(128)S(6)} %select_n.301), kind=kOutput, calls=%fused_computation.6.clone.1 | convolution fusion | flops 1612709888 | bytes 9699333 | tf_op jit(solution)/shard_map/while/body/eval_jaxpr/dot_general | solution.py:122
  301.0 19.2 %collective-permute-done.1 = f32[2,128,512]{2,1,0:T(8,128)S(1)} collective-permute-done((f32[2,128,512]{2,1,0:T(8,128)S(1)}, f32[2,128,512]{2,1,0:T(8,128)S(1)}, u32[]{:S(2)}, u32[]{:S(2)}) %collective-permute-start.1) | collective-permute-done | bytes 524320 | tf_op jit(solution)/shard_map/while/body/eval_jaxpr/ppermute | solution.py:12
  327.7 18.8 %collective-permute-done.1 = f32[2,128,512]{2,1,0:T(8,128)S(1)} collective-permute-done((f32[2,128,512]{2,1,0:T(8,128)S(1)}, f32[2,128,512]{2,1,0:T(8,128)S(1)}, u32[]{:S(2)}, u32[]{:S(2)}) %collective-permute-start.1) | collective-permute-done | bytes 524320 | tf_op jit(solution)/shard_map/while/body/eval_jaxpr/ppermute | solution.py:12
  347.3 6.7 %bitcast_add_fusion.3 = f32[2048,512]{0,1:T(8,128)} fusion(f32[2048,512]{0,1:T(8,128)} %get-tuple-element.254, f32[2048,128]{1,0:T(8,128)S(1)} %copy.52, pred[]{:T(512)S(6)} %compare.52, f32[2,128,512]{2,1,0:T(8,128)S(1)} %copy.53, s32[]{:T(128)S(6)} %select_n.301), kind=kOutput, calls=%fused_computation.6.clone.1 | convolution fusion | flops 1612709888 | bytes 9699333 | tf_op jit(solution)/shard_map/while/body/eval_jaxpr/dot_general | solution.py:122
  354.0 19.2 %collective-permute-done.1 = f32[2,128,512]{2,1,0:T(8,128)S(1)} collective-permute-done((f32[2,128,512]{2,1,0:T(8,128)S(1)}, f32[2,128,512]{2,1,0:T(8,128)S(1)}, u32[]{:S(2)}, u32[]{:S(2)}) %collective-permute-start.1) | collective-permute-done | bytes 524320 | tf_op jit(solution)/shard_map/while/body/eval_jaxpr/ppermute | solution.py:12
  374.0 6.7 %bitcast_add_fusion.3 = f32[2048,512]{0,1:T(8,128)} fusion(f32[2048,512]{0,1:T(8,128)} %get-tuple-element.254, f32[2048,128]{1,0:T(8,128)S(1)} %copy.52, pred[]{:T(512)S(6)} %compare.52, f32[2,128,512]{2,1,0:T(8,128)S(1)} %copy.53, s32[]{:T(128)S(6)} %select_n.301), kind=kOutput, calls=%fused_computation.6.clone.1 | convolution fusion | flops 1612709888 | bytes 9699333 | tf_op jit(solution)/shard_map/while/body/eval_jaxpr/dot_general | solution.py:122
  380.7 18.8 %collective-permute-done.1 = f32[2,128,512]{2,1,0:T(8,128)S(1)} collective-permute-done((f32[2,128,512]{2,1,0:T(8,128)S(1)}, f32[2,128,512]{2,1,0:T(8,128)S(1)}, u32[]{:S(2)}, u32[]{:S(2)}) %collective-permute-start.1) | collective-permute-done | bytes 524320 | tf_op jit(solution)/shard_map/while/body/eval_jaxpr/ppermute | solution.py:12
  400.3 6.7 %bitcast_add_fusion.3 = f32[2048,512]{0,1:T(8,128)} fusion(f32[2048,512]{0,1:T(8,128)} %get-tuple-element.254, f32[2048,128]{1,0:T(8,128)S(1)} %copy.52, pred[]{:T(512)S(6)} %compare.52, f32[2,128,512]{2,1,0:T(8,128)S(1)} %copy.53, s32[]{:T(128)S(6)} %select_n.301), kind=kOutput, calls=%fused_computation.6.clone.1 | convolution fusion | flops 1612709888 | bytes 9699333 | tf_op jit(solution)/shard_map/while/body/eval_jaxpr/dot_general | solution.py:122
  407.0 19.2 %collective-permute-done.1 = f32[2,128,512]{2,1,0:T(8,128)S(1)} collective-permute-done((f32[2,128,512]{2,1,0:T(8,128)S(1)}, f32[2,128,512]{2,1,0:T(8,128)S(1)}, u32[]{:S(2)}, u32[]{:S(2)}) %collective-permute-start.1) | collective-permute-done | bytes 524320 | tf_op jit(solution)/shard_map/while/body/eval_jaxpr/ppermute | solution.py:12
  427.0 6.7 %bitcast_add_fusion.3 = f32[2048,512]{0,1:T(8,128)} fusion(f32[2048,512]{0,1:T(8,128)} %get-tuple-element.254, f32[2048,128]{1,0:T(8,128)S(1)} %copy.52, pred[]{:T(512)S(6)} %compare.52, f32[2,128,512]{2,1,0:T(8,128)S(1)} %copy.53, s32[]{:T(128)S(6)} %select_n.301), kind=kOutput, calls=%fused_computation.6.clone.1 | convolution fusion | flops 1612709888 | bytes 9699333 | tf_op jit(solution)/shard_map/while/body/eval_jaxpr/dot_general | solution.py:122
  433.7 18.8 %collective-permute-done.1 = f32[2,128,512]{2,1,0:T(8,128)S(1)} collective-permute-done((f32[2,128,512]{2,1,0:T(8,128)S(1)}, f32[2,128,512]{2,1,0:T(8,128)S(1)}, u32[]{:S(2)}, u32[]{:S(2)}) %collective-permute-start.1) | collective-permute-done | bytes 524320 | tf_op jit(solution)/shard_map/while/body/eval_jaxpr/ppermute | solution.py:12
  453.3 6.7 %bitcast_add_fusion.3 = f32[2048,512]{0,1:T(8,128)} fusion(f32[2048,512]{0,1:T(8,128)} %get-tuple-element.254, f32[2048,128]{1,0:T(8,128)S(1)} %copy.52, pred[]{:T(512)S(6)} %compare.52, f32[2,128,512]{2,1,0:T(8,128)S(1)} %copy.53, s32[]{:T(128)S(6)} %select_n.301), kind=kOutput, calls=%fused_computation.6.clone.1 | convolution fusion | flops 1612709888 | bytes 9699333 | tf_op jit(solution)/shard_map/while/body/eval_jaxpr/dot_general | solution.py:122
  460.0 19.2 %collective-permute-done.1 = f32[2,128,512]{2,1,0:T(8,128)S(1)} collective-permute-done((f32[2,128,512]{2,1,0:T(8,128)S(1)}, f32[2,128,512]{2,1,0:T(8,128)S(1)}, u32[]{:S(2)}, u32[]{:S(2)}) %collective-permute-start.1) | collective-permute-done | bytes 524320 | tf_op jit(solution)/shard_map/while/body/eval_jaxpr/ppermute | solution.py:12
  480.0 6.7 %bitcast_add_fusion.3 = f32[2048,512]{0,1:T(8,128)} fusion(f32[2048,512]{0,1:T(8,128)} %get-tuple-element.254, f32[2048,128]{1,0:T(8,128)S(1)} %copy.52, pred[]{:T(512)S(6)} %compare.52, f32[2,128,512]{2,1,0:T(8,128)S(1)} %copy.53, s32[]{:T(128)S(6)} %select_n.301), kind=kOutput, calls=%fused_computation.6.clone.1 | convolution fusion | flops 1612709888 | bytes 9699333 | tf_op jit(solution)/shard_map/while/body/eval_jaxpr/dot_general | solution.py:122
  486.7 18.8 %collective-permute-done.1 = f32[2,128,512]{2,1,0:T(8,128)S(1)} collective-permute-done((f32[2,128,512]{2,1,0:T(8,128)S(1)}, f32[2,128,512]{2,1,0:T(8,128)S(1)}, u32[]{:S(2)}, u32[]{:S(2)}) %collective-permute-start.1) | collective-permute-done | bytes 524320 | tf_op jit(solution)/shard_map/while/body/eval_jaxpr/ppermute | solution.py:12
  (135 shorter events, 96.7 us)
Async XLA Ops:
  33.3 33.2 %all-to-all-start.3 = ((f32[8,4,128,128]{3,2,1,0:T(8,128)}), f32[8,4,128,128]{3,2,1,0:T(8,128)S(1)}, u32[]{:S(2)}, u32[]{:S(2)}) async-start(f32[8,4,128,128]{3,2,1,0:T(8,128)} %bitcast.23), calls=%async_computation.3 | async-start | bytes 4194304 | tf_op jit(solution)/shard_map/all_to_all | solution.py:101
  67.8 31.7 %all-to-all-start.1 = ((f32[16,2,128,128]{3,2,1,0:T(8,128)}), f32[16,2,128,128]{3,2,1,0:T(8,128)S(1)}, u32[]{:S(2)}, u32[]{:S(2)}) async-start(f32[16,2,128,128]{3,2,1,0:T(8,128)} %bitcast.10), calls=%async_computation.1 | async-start | bytes 4194304 | tf_op jit(solution)/shard_map/all_to_all | solution.py:63
  105.1 29.5 %collective-permute-start = (f32[2048,128]{1,0:T(8,128)S(1)}, f32[2048,128]{1,0:T(8,128)S(1)}, u32[]{:S(2)}, u32[]{:S(2)}) collective-permute-start(f32[2048,128]{1,0:T(8,128)S(1)} %copy.52), channel_id=1, source_target_pairs={{1,0},{2,1},{3,2},{4,3},{5,4},{6,5},{7,6},{8,7},{9,8},{10,9},{11,1... | collective-permute-start | bytes 3145736 | tf_op jit(solution)/shard_map/while/body/eval_jaxpr/ppermute | solution.py:12
  106.0 28.6 %collective-permute-start.1 = (f32[2,128,512]{2,1,0:T(8,128)S(1)}, f32[2,128,512]{2,1,0:T(8,128)S(1)}, u32[]{:S(2)}, u32[]{:S(2)}) collective-permute-start(f32[2,128,512]{2,1,0:T(8,128)S(1)} %copy.53), channel_id=1, source_target_pairs={{16,0},{32,16},{48,32},{64,48},{80,64},{96,80},{112,96},{0,112},{1... | collective-permute-start | bytes 1572872 | tf_op jit(solution)/shard_map/while/body/eval_jaxpr/ppermute | solution.py:12
  134.6 26.6 %collective-permute-start = (f32[2048,128]{1,0:T(8,128)S(1)}, f32[2048,128]{1,0:T(8,128)S(1)}, u32[]{:S(2)}, u32[]{:S(2)}) collective-permute-start(f32[2048,128]{1,0:T(8,128)S(1)} %copy.52), channel_id=1, source_target_pairs={{1,0},{2,1},{3,2},{4,3},{5,4},{6,5},{7,6},{8,7},{9,8},{10,9},{11,1... | collective-permute-start | bytes 3145736 | tf_op jit(solution)/shard_map/while/body/eval_jaxpr/ppermute | solution.py:12
  135.4 25.8 %collective-permute-start.1 = (f32[2,128,512]{2,1,0:T(8,128)S(1)}, f32[2,128,512]{2,1,0:T(8,128)S(1)}, u32[]{:S(2)}, u32[]{:S(2)}) collective-permute-start(f32[2,128,512]{2,1,0:T(8,128)S(1)} %copy.53), channel_id=1, source_target_pairs={{16,0},{32,16},{48,32},{64,48},{80,64},{96,80},{112,96},{0,112},{1... | collective-permute-start | bytes 1572872 | tf_op jit(solution)/shard_map/while/body/eval_jaxpr/ppermute | solution.py:12
  161.3 26.2 %collective-permute-start = (f32[2048,128]{1,0:T(8,128)S(1)}, f32[2048,128]{1,0:T(8,128)S(1)}, u32[]{:S(2)}, u32[]{:S(2)}) collective-permute-start(f32[2048,128]{1,0:T(8,128)S(1)} %copy.52), channel_id=1, source_target_pairs={{1,0},{2,1},{3,2},{4,3},{5,4},{6,5},{7,6},{8,7},{9,8},{10,9},{11,1... | collective-permute-start | bytes 3145736 | tf_op jit(solution)/shard_map/while/body/eval_jaxpr/ppermute | solution.py:12
  161.8 25.7 %collective-permute-start.1 = (f32[2,128,512]{2,1,0:T(8,128)S(1)}, f32[2,128,512]{2,1,0:T(8,128)S(1)}, u32[]{:S(2)}, u32[]{:S(2)}) collective-permute-start(f32[2,128,512]{2,1,0:T(8,128)S(1)} %copy.53), channel_id=1, source_target_pairs={{16,0},{32,16},{48,32},{64,48},{80,64},{96,80},{112,96},{0,112},{1... | collective-permute-start | bytes 1572872 | tf_op jit(solution)/shard_map/while/body/eval_jaxpr/ppermute | solution.py:12
  187.6 26.6 %collective-permute-start = (f32[2048,128]{1,0:T(8,128)S(1)}, f32[2048,128]{1,0:T(8,128)S(1)}, u32[]{:S(2)}, u32[]{:S(2)}) collective-permute-start(f32[2048,128]{1,0:T(8,128)S(1)} %copy.52), channel_id=1, source_target_pairs={{1,0},{2,1},{3,2},{4,3},{5,4},{6,5},{7,6},{8,7},{9,8},{10,9},{11,1... | collective-permute-start | bytes 3145736 | tf_op jit(solution)/shard_map/while/body/eval_jaxpr/ppermute | solution.py:12
  188.2 26.1 %collective-permute-start.1 = (f32[2,128,512]{2,1,0:T(8,128)S(1)}, f32[2,128,512]{2,1,0:T(8,128)S(1)}, u32[]{:S(2)}, u32[]{:S(2)}) collective-permute-start(f32[2,128,512]{2,1,0:T(8,128)S(1)} %copy.53), channel_id=1, source_target_pairs={{16,0},{32,16},{48,32},{64,48},{80,64},{96,80},{112,96},{0,112},{1... | collective-permute-start | bytes 1572872 | tf_op jit(solution)/shard_map/while/body/eval_jaxpr/ppermute | solution.py:12
  214.3 26.2 %collective-permute-start = (f32[2048,128]{1,0:T(8,128)S(1)}, f32[2048,128]{1,0:T(8,128)S(1)}, u32[]{:S(2)}, u32[]{:S(2)}) collective-permute-start(f32[2048,128]{1,0:T(8,128)S(1)} %copy.52), channel_id=1, source_target_pairs={{1,0},{2,1},{3,2},{4,3},{5,4},{6,5},{7,6},{8,7},{9,8},{10,9},{11,1... | collective-permute-start | bytes 3145736 | tf_op jit(solution)/shard_map/while/body/eval_jaxpr/ppermute | solution.py:12
  214.8 25.7 %collective-permute-start.1 = (f32[2,128,512]{2,1,0:T(8,128)S(1)}, f32[2,128,512]{2,1,0:T(8,128)S(1)}, u32[]{:S(2)}, u32[]{:S(2)}) collective-permute-start(f32[2,128,512]{2,1,0:T(8,128)S(1)} %copy.53), channel_id=1, source_target_pairs={{16,0},{32,16},{48,32},{64,48},{80,64},{96,80},{112,96},{0,112},{1... | collective-permute-start | bytes 1572872 | tf_op jit(solution)/shard_map/while/body/eval_jaxpr/ppermute | solution.py:12
  240.6 26.6 %collective-permute-start = (f32[2048,128]{1,0:T(8,128)S(1)}, f32[2048,128]{1,0:T(8,128)S(1)}, u32[]{:S(2)}, u32[]{:S(2)}) collective-permute-start(f32[2048,128]{1,0:T(8,128)S(1)} %copy.52), channel_id=1, source_target_pairs={{1,0},{2,1},{3,2},{4,3},{5,4},{6,5},{7,6},{8,7},{9,8},{10,9},{11,1... | collective-permute-start | bytes 3145736 | tf_op jit(solution)/shard_map/while/body/eval_jaxpr/ppermute | solution.py:12
  241.2 26.1 %collective-permute-start.1 = (f32[2,128,512]{2,1,0:T(8,128)S(1)}, f32[2,128,512]{2,1,0:T(8,128)S(1)}, u32[]{:S(2)}, u32[]{:S(2)}) collective-permute-start(f32[2,128,512]{2,1,0:T(8,128)S(1)} %copy.53), channel_id=1, source_target_pairs={{16,0},{32,16},{48,32},{64,48},{80,64},{96,80},{112,96},{0,112},{1... | collective-permute-start | bytes 1572872 | tf_op jit(solution)/shard_map/while/body/eval_jaxpr/ppermute | solution.py:12
  267.3 26.2 %collective-permute-start = (f32[2048,128]{1,0:T(8,128)S(1)}, f32[2048,128]{1,0:T(8,128)S(1)}, u32[]{:S(2)}, u32[]{:S(2)}) collective-permute-start(f32[2048,128]{1,0:T(8,128)S(1)} %copy.52), channel_id=1, source_target_pairs={{1,0},{2,1},{3,2},{4,3},{5,4},{6,5},{7,6},{8,7},{9,8},{10,9},{11,1... | collective-permute-start | bytes 3145736 | tf_op jit(solution)/shard_map/while/body/eval_jaxpr/ppermute | solution.py:12
  267.8 25.7 %collective-permute-start.1 = (f32[2,128,512]{2,1,0:T(8,128)S(1)}, f32[2,128,512]{2,1,0:T(8,128)S(1)}, u32[]{:S(2)}, u32[]{:S(2)}) collective-permute-start(f32[2,128,512]{2,1,0:T(8,128)S(1)} %copy.53), channel_id=1, source_target_pairs={{16,0},{32,16},{48,32},{64,48},{80,64},{96,80},{112,96},{0,112},{1... | collective-permute-start | bytes 1572872 | tf_op jit(solution)/shard_map/while/body/eval_jaxpr/ppermute | solution.py:12
  293.6 26.6 %collective-permute-start = (f32[2048,128]{1,0:T(8,128)S(1)}, f32[2048,128]{1,0:T(8,128)S(1)}, u32[]{:S(2)}, u32[]{:S(2)}) collective-permute-start(f32[2048,128]{1,0:T(8,128)S(1)} %copy.52), channel_id=1, source_target_pairs={{1,0},{2,1},{3,2},{4,3},{5,4},{6,5},{7,6},{8,7},{9,8},{10,9},{11,1... | collective-permute-start | bytes 3145736 | tf_op jit(solution)/shard_map/while/body/eval_jaxpr/ppermute | solution.py:12
  294.2 26.1 %collective-permute-start.1 = (f32[2,128,512]{2,1,0:T(8,128)S(1)}, f32[2,128,512]{2,1,0:T(8,128)S(1)}, u32[]{:S(2)}, u32[]{:S(2)}) collective-permute-start(f32[2,128,512]{2,1,0:T(8,128)S(1)} %copy.53), channel_id=1, source_target_pairs={{16,0},{32,16},{48,32},{64,48},{80,64},{96,80},{112,96},{0,112},{1... | collective-permute-start | bytes 1572872 | tf_op jit(solution)/shard_map/while/body/eval_jaxpr/ppermute | solution.py:12
  320.3 26.2 %collective-permute-start = (f32[2048,128]{1,0:T(8,128)S(1)}, f32[2048,128]{1,0:T(8,128)S(1)}, u32[]{:S(2)}, u32[]{:S(2)}) collective-permute-start(f32[2048,128]{1,0:T(8,128)S(1)} %copy.52), channel_id=1, source_target_pairs={{1,0},{2,1},{3,2},{4,3},{5,4},{6,5},{7,6},{8,7},{9,8},{10,9},{11,1... | collective-permute-start | bytes 3145736 | tf_op jit(solution)/shard_map/while/body/eval_jaxpr/ppermute | solution.py:12
  320.8 25.7 %collective-permute-start.1 = (f32[2,128,512]{2,1,0:T(8,128)S(1)}, f32[2,128,512]{2,1,0:T(8,128)S(1)}, u32[]{:S(2)}, u32[]{:S(2)}) collective-permute-start(f32[2,128,512]{2,1,0:T(8,128)S(1)} %copy.53), channel_id=1, source_target_pairs={{16,0},{32,16},{48,32},{64,48},{80,64},{96,80},{112,96},{0,112},{1... | collective-permute-start | bytes 1572872 | tf_op jit(solution)/shard_map/while/body/eval_jaxpr/ppermute | solution.py:12
  346.6 26.6 %collective-permute-start = (f32[2048,128]{1,0:T(8,128)S(1)}, f32[2048,128]{1,0:T(8,128)S(1)}, u32[]{:S(2)}, u32[]{:S(2)}) collective-permute-start(f32[2048,128]{1,0:T(8,128)S(1)} %copy.52), channel_id=1, source_target_pairs={{1,0},{2,1},{3,2},{4,3},{5,4},{6,5},{7,6},{8,7},{9,8},{10,9},{11,1... | collective-permute-start | bytes 3145736 | tf_op jit(solution)/shard_map/while/body/eval_jaxpr/ppermute | solution.py:12
  347.1 26.1 %collective-permute-start.1 = (f32[2,128,512]{2,1,0:T(8,128)S(1)}, f32[2,128,512]{2,1,0:T(8,128)S(1)}, u32[]{:S(2)}, u32[]{:S(2)}) collective-permute-start(f32[2,128,512]{2,1,0:T(8,128)S(1)} %copy.53), channel_id=1, source_target_pairs={{16,0},{32,16},{48,32},{64,48},{80,64},{96,80},{112,96},{0,112},{1... | collective-permute-start | bytes 1572872 | tf_op jit(solution)/shard_map/while/body/eval_jaxpr/ppermute | solution.py:12
  373.3 26.2 %collective-permute-start = (f32[2048,128]{1,0:T(8,128)S(1)}, f32[2048,128]{1,0:T(8,128)S(1)}, u32[]{:S(2)}, u32[]{:S(2)}) collective-permute-start(f32[2048,128]{1,0:T(8,128)S(1)} %copy.52), channel_id=1, source_target_pairs={{1,0},{2,1},{3,2},{4,3},{5,4},{6,5},{7,6},{8,7},{9,8},{10,9},{11,1... | collective-permute-start | bytes 3145736 | tf_op jit(solution)/shard_map/while/body/eval_jaxpr/ppermute | solution.py:12
  373.8 25.7 %collective-permute-start.1 = (f32[2,128,512]{2,1,0:T(8,128)S(1)}, f32[2,128,512]{2,1,0:T(8,128)S(1)}, u32[]{:S(2)}, u32[]{:S(2)}) collective-permute-start(f32[2,128,512]{2,1,0:T(8,128)S(1)} %copy.53), channel_id=1, source_target_pairs={{16,0},{32,16},{48,32},{64,48},{80,64},{96,80},{112,96},{0,112},{1... | collective-permute-start | bytes 1572872 | tf_op jit(solution)/shard_map/while/body/eval_jaxpr/ppermute | solution.py:12
  399.6 26.6 %collective-permute-start = (f32[2048,128]{1,0:T(8,128)S(1)}, f32[2048,128]{1,0:T(8,128)S(1)}, u32[]{:S(2)}, u32[]{:S(2)}) collective-permute-start(f32[2048,128]{1,0:T(8,128)S(1)} %copy.52), channel_id=1, source_target_pairs={{1,0},{2,1},{3,2},{4,3},{5,4},{6,5},{7,6},{8,7},{9,8},{10,9},{11,1... | collective-permute-start | bytes 3145736 | tf_op jit(solution)/shard_map/while/body/eval_jaxpr/ppermute | solution.py:12
  400.1 26.1 %collective-permute-start.1 = (f32[2,128,512]{2,1,0:T(8,128)S(1)}, f32[2,128,512]{2,1,0:T(8,128)S(1)}, u32[]{:S(2)}, u32[]{:S(2)}) collective-permute-start(f32[2,128,512]{2,1,0:T(8,128)S(1)} %copy.53), channel_id=1, source_target_pairs={{16,0},{32,16},{48,32},{64,48},{80,64},{96,80},{112,96},{0,112},{1... | collective-permute-start | bytes 1572872 | tf_op jit(solution)/shard_map/while/body/eval_jaxpr/ppermute | solution.py:12
  426.3 26.2 %collective-permute-start = (f32[2048,128]{1,0:T(8,128)S(1)}, f32[2048,128]{1,0:T(8,128)S(1)}, u32[]{:S(2)}, u32[]{:S(2)}) collective-permute-start(f32[2048,128]{1,0:T(8,128)S(1)} %copy.52), channel_id=1, source_target_pairs={{1,0},{2,1},{3,2},{4,3},{5,4},{6,5},{7,6},{8,7},{9,8},{10,9},{11,1... | collective-permute-start | bytes 3145736 | tf_op jit(solution)/shard_map/while/body/eval_jaxpr/ppermute | solution.py:12
  426.8 25.7 %collective-permute-start.1 = (f32[2,128,512]{2,1,0:T(8,128)S(1)}, f32[2,128,512]{2,1,0:T(8,128)S(1)}, u32[]{:S(2)}, u32[]{:S(2)}) collective-permute-start(f32[2,128,512]{2,1,0:T(8,128)S(1)} %copy.53), channel_id=1, source_target_pairs={{16,0},{32,16},{48,32},{64,48},{80,64},{96,80},{112,96},{0,112},{1... | collective-permute-start | bytes 1572872 | tf_op jit(solution)/shard_map/while/body/eval_jaxpr/ppermute | solution.py:12
  452.6 26.6 %collective-permute-start = (f32[2048,128]{1,0:T(8,128)S(1)}, f32[2048,128]{1,0:T(8,128)S(1)}, u32[]{:S(2)}, u32[]{:S(2)}) collective-permute-start(f32[2048,128]{1,0:T(8,128)S(1)} %copy.52), channel_id=1, source_target_pairs={{1,0},{2,1},{3,2},{4,3},{5,4},{6,5},{7,6},{8,7},{9,8},{10,9},{11,1... | collective-permute-start | bytes 3145736 | tf_op jit(solution)/shard_map/while/body/eval_jaxpr/ppermute | solution.py:12
  453.1 26.1 %collective-permute-start.1 = (f32[2,128,512]{2,1,0:T(8,128)S(1)}, f32[2,128,512]{2,1,0:T(8,128)S(1)}, u32[]{:S(2)}, u32[]{:S(2)}) collective-permute-start(f32[2,128,512]{2,1,0:T(8,128)S(1)} %copy.53), channel_id=1, source_target_pairs={{16,0},{32,16},{48,32},{64,48},{80,64},{96,80},{112,96},{0,112},{1... | collective-permute-start | bytes 1572872 | tf_op jit(solution)/shard_map/while/body/eval_jaxpr/ppermute | solution.py:12
  479.3 26.2 %collective-permute-start = (f32[2048,128]{1,0:T(8,128)S(1)}, f32[2048,128]{1,0:T(8,128)S(1)}, u32[]{:S(2)}, u32[]{:S(2)}) collective-permute-start(f32[2048,128]{1,0:T(8,128)S(1)} %copy.52), channel_id=1, source_target_pairs={{1,0},{2,1},{3,2},{4,3},{5,4},{6,5},{7,6},{8,7},{9,8},{10,9},{11,1... | collective-permute-start | bytes 3145736 | tf_op jit(solution)/shard_map/while/body/eval_jaxpr/ppermute | solution.py:12
  479.8 25.7 %collective-permute-start.1 = (f32[2,128,512]{2,1,0:T(8,128)S(1)}, f32[2,128,512]{2,1,0:T(8,128)S(1)}, u32[]{:S(2)}, u32[]{:S(2)}) collective-permute-start(f32[2,128,512]{2,1,0:T(8,128)S(1)} %copy.53), channel_id=1, source_target_pairs={{16,0},{32,16},{48,32},{64,48},{80,64},{96,80},{112,96},{0,112},{1... | collective-permute-start | bytes 1572872 | tf_op jit(solution)/shard_map/while/body/eval_jaxpr/ppermute | solution.py:12
  (7 other events, 67.0 us)
where the time goes:
time: 519 us; the launch traced here: 518 us
  waiting for transfers between devices  326 us (63%)
  matrix products  104 us (20%)
  local copies, waits for them, and re-layouts  40 us (8%)
  starting transfers between devices  35.5 us (7%)
  other arithmetic  11.2 us (2%)
    ppermute x30, waiting for transfers between devices, shifted(): return lax.ppermute(block, axis, route)  289 us
    dot_general x16, matrix products, multiply(): jnp.dot(a_current, b_used, precision=lax.Precision.HIGHEST, preferred_ele...  104 us
    all_to_all x1, waiting for transfers between devices, per_device(): lax.all_to_all(a_send.reshape((n_col, slots, block_width, block_width)),...  18.5 us
    all_to_all x1, waiting for transfers between devices, per_device(): lax.all_to_all(b_send.reshape((n_row, per_row, block_width, block_width))...  18.2 us
  transfers between devices with their start and end apart: 34, of which 17 were waited for; matrix products, arithmetic and copies ran while one was open for 25% of the time, Pallas kernels for 0%

commit v1 on v0

v1 whole, which is shorter than its diff:
```python
import functools

import jax
import jax.numpy as jnp
from jax import lax
from jax.experimental import pallas as pl
from jax.experimental.pallas import tpu as pltpu
from jax.sharding import PartitionSpec as P

BS = 128
CAP = 2
NX, NY, NC, NZ = 4, 2, 2, 4
N_COL = NY * NX * NC
N_ROW = 2 * NZ
KB = 16
KZ = KB // NZ
RB = 16
CB = 4
MET = 8
F32 = jnp.float32
ANY = pl.BlockSpec(memory_space=pl.ANY)
SMEM = pl.BlockSpec(memory_space=pltpu.SMEM)
VMEM = pl.BlockSpec(memory_space=pltpu.VMEM)


def col_id(y, x, c):
    return (y % NY) * NX * NC + (x % NX) * NC + c % NC


def col_shift(value, dy=0, dx=0, dc=0):
    route = [
        (col_id(y, x, c), col_id(y + dy, x + dx, c + dc))
        for y in range(NY)
        for x in range(NX)
        for c in range(NC)
    ]
    return lax.ppermute(value, "col", route)


def row_shift(value, dy=0, dz=0):
    route = [
        (y * NZ + z, (y + dy) % 2 * NZ + (z + dz) % NZ) for y in range(2) for z in range(NZ)
    ]
    return lax.ppermute(value, "row", route)


def lane_marks(first, second):
    lane = lax.broadcasted_iota(jnp.int32, (MET, BS), 1)
    marks = jnp.where(lane == 0, first, jnp.where(lane == 1, second, -1))
    return marks.astype(F32)


def pack_a_kernel(counts, owners, blocks, send, marks, sems, mark_sem):
    start = jnp.int32(0)
    jobs = []
    for k in range(KB):
        count = counts[k]
        places = []
        for rank in range(CAP):
            slot = jnp.minimum(start + rank, blocks.shape[0] - 1)
            copy = pltpu.make_async_copy(
                blocks.at[slot], send.at[k, pl.ds(rank * BS, BS)], sems.at[k, rank]
            )
            have = count > rank
            pl.when(have)(copy.start)
            jobs.append((have, copy))
            places.append(jnp.where(have, lax.rem(owners[slot], RB), -1))
        marks[k] = lane_marks(*places)
        start = start + count
    tail = pltpu.make_async_copy(marks, send.at[:, pl.ds(CAP * BS, MET)], mark_sem)
    tail.start()
    for have, copy in jobs:
        pl.when(have)(copy.wait)
    tail.wait()


def pack_a(counts, owners, blocks):
    return pl.pallas_call(
        pack_a_kernel,
        out_shape=jax.ShapeDtypeStruct((N_COL, CAP * BS + MET, BS), F32),
        in_specs=[SMEM, SMEM, ANY],
        out_specs=ANY,
        scratch_shapes=[
            pltpu.VMEM((KB, MET, BS), F32),
            pltpu.SemaphoreType.DMA((KB, CAP)),
            pltpu.SemaphoreType.DMA,
        ],
        name="pack_a",
    )(counts, owners, blocks)


def pack_b_kernel(z_ref, counts, owners, blocks, *rest):
    sends, (marks, starts, sems, mark_sem) = rest[:NZ], rest[NZ:]
    start = jnp.int32(0)
    for k in range(KB):
        starts[k] = start
        start = start + counts[k]
    jobs = []
    tails = []
    for rel in range(NZ):
        base = lax.rem(z_ref[0] + rel, NZ) * KZ
        for kk in range(KZ):
            count = counts[base + kk]
            places = []
            for rank in range(CAP):
                slot = jnp.minimum(starts[base + kk] + rank, blocks.shape[0] - 1)
                piece = kk * CAP + rank
                copy = pltpu.make_async_copy(
                    blocks.at[slot], sends[rel].at[pl.ds(piece * BS, BS)], sems.at[rel, piece]
                )
                have = count > rank
                pl.when(have)(copy.start)
                jobs.append((have, copy))
                places.append(jnp.where(have, lax.rem(owners[slot], CB), -1))
            marks[rel, pl.ds(kk * MET, MET)] = lane_marks(*places)
        tail = pltpu.make_async_copy(
            marks.at[rel], sends[rel].at[pl.ds(KZ * CAP * BS, KZ * MET)], mark_sem.at[rel]
        )
        tail.start()
        tails.append(tail)
    for have, copy in jobs:
        pl.when(have)(copy.wait)
    for tail in tails:
        tail.wait()


def pack_b(z_now, counts, owners, blocks):
    rows = KZ * (CAP * BS + MET)
    return pl.pallas_call(
        pack_b_kernel,
        out_shape=[jax.ShapeDtypeStruct((rows, BS), F32)] * NZ,
        in_specs=[SMEM, SMEM, SMEM, ANY],
        out_specs=[ANY] * NZ,
        scratch_shapes=[
            pltpu.VMEM((NZ, KZ * MET, BS), F32),
            pltpu.SMEM((KB,), jnp.int32),
            pltpu.SemaphoreType.DMA((NZ, KZ * CAP)),
            pltpu.SemaphoreType.DMA((NZ,)),
        ],
        name="pack_b",
    )(z_now, counts, owners, blocks)


def unpack_a_kernel(got, panel, marks, sems, mark_sem):
    read = pltpu.make_async_copy(got.at[:, CAP * BS], marks, mark_sem)
    read.start()
    panel[...] = jnp.zeros_like(panel)
    read.wait()
    jobs = []
    for source in range(N_COL):
        for rank in range(CAP):
            place = marks[source, rank].astype(jnp.int32)
            have = place >= 0
            at = pl.multiple_of(jnp.maximum(place, 0) * BS, BS)
            copy = pltpu.make_async_copy(
                got.at[source, pl.ds(rank * BS, BS)], panel.at[pl.ds(at, BS)], sems.at[source, rank]
            )
            pl.when(have)(copy.start)
            jobs.append((have, copy))
    for have, copy in jobs:
        pl.when(have)(copy.wait)


def unpack_a(got):
    return pl.pallas_call(
        unpack_a_kernel,
        out_shape=jax.ShapeDtypeStruct((RB * BS, BS), F32),
        in_specs=[ANY],
        out_specs=VMEM,
        scratch_shapes=[
            pltpu.SMEM((N_COL, BS), F32),
            pltpu.SemaphoreType.DMA((N_COL, CAP)),
            pltpu.SemaphoreType.DMA,
        ],
        name="unpack_a",
    )(got)


def unpack_b_kernel(*refs):
    gots, (panel, marks, sems, mark_sem) = refs[:NZ], refs[NZ:]
    reads = []
    for rel in range(NZ):
        read = pltpu.make_async_copy(
            gots[rel].at[pl.ds(KZ * CAP * BS, KZ * MET)], marks.at[rel], mark_sem.at[rel]
        )
        read.start()
        reads.append(read)
    panel[...] = jnp.zeros_like(panel)
    for read in reads:
        read.wait()
    jobs = []
    for rel in range(NZ):
        for kk in range(KZ):
            for rank in range(CAP):
                place = marks[rel, kk * MET, rank].astype(jnp.int32)
                have = place >= 0
                at = pl.multiple_of(jnp.maximum(place, 0) * BS, BS)
                piece = kk * CAP + rank
                copy = pltpu.make_async_copy(
                    gots[rel].at[pl.ds(piece * BS, BS)],
                    panel.at[pl.ds(kk * BS, BS), pl.ds(at, BS)],
                    sems.at[rel, piece],
                )
                pl.when(have)(copy.start)
                jobs.append((have, copy))
    for have, copy in jobs:
        pl.when(have)(copy.wait)


def unpack_b(gots):
    return pl.pallas_call(
        unpack_b_kernel,
        out_shape=jax.ShapeDtypeStruct((KZ * BS, CB * BS), F32),
        in_specs=[ANY] * NZ,
        out_specs=VMEM,
        scratch_shapes=[
            pltpu.SMEM((NZ, KZ * MET, BS), F32),
            pltpu.SemaphoreType.DMA((NZ, KZ * CAP)),
            pltpu.SemaphoreType.DMA((NZ,)),
        ],
        name="unpack_b",
    )(*gots)


PHASES = (8, 6, 2)


def split(value):
    high = value.astype(jnp.bfloat16)
    return high, (value - high.astype(F32)).astype(jnp.bfloat16)


def order_b_kernel(order, here, ahead, behind, far_lo, far_hi, *rest):
    outs, (panel, sems) = rest[:6], rest[6:]
    half = KZ // 2
    z_now = order[KB]
    jobs = []
    for p in range(KB):
        k = order[p]
        rel = lax.rem(k // KZ - z_now + NZ, NZ)
        kk = lax.rem(k, KZ)
        row = pl.multiple_of(kk * BS, BS)
        row_hi = pl.multiple_of(jnp.maximum(kk - half, 0) * BS, BS)
        row_lo = pl.multiple_of(jnp.minimum(kk, half - 1) * BS, BS)
        for want, source in (
            (rel == 0, here.at[pl.ds(row, BS)]),
            (rel == 1, ahead.at[pl.ds(row, BS)]),
            (rel == 3, behind.at[pl.ds(row, BS)]),
            ((rel == 2) & (kk < half), far_lo.at[pl.ds(row_lo, BS)]),
            ((rel == 2) & (kk >= half), far_hi.at[pl.ds(row_hi, BS)]),
        ):
            copy = pltpu.make_async_copy(source, panel.at[pl.ds(p * BS, BS)], sems.at[p])
            pl.when(want)(copy.start)
        jobs.append(pltpu.make_async_copy(here.at[pl.ds(0, BS)], panel.at[pl.ds(p * BS, BS)], sems.at[p]))
    p = 0
    for i, n in enumerate(PHASES):
        for q in range(n):
            jobs[p].wait()
            high, low = split(panel[pl.ds(p * BS, BS), :])
            outs[2 * i][pl.ds(q * BS, BS), :] = high
            outs[2 * i + 1][pl.ds(q * BS, BS), :] = low
            p += 1


def order_b(order, pieces):
    outs = [
        jax.ShapeDtypeStruct((n * BS, CB * BS), jnp.bfloat16) for n in PHASES for _ in range(2)
    ]
    return pl.pallas_call(
        order_b_kernel,
        out_shape=outs,
        in_specs=[SMEM] + [ANY] * 5,
        out_specs=[VMEM] * 6,
        scratch_shapes=[
            pltpu.VMEM((KB * BS, CB * BS), F32),
            pltpu.SemaphoreType.DMA((KB,)),
        ],
        name="order_b",
    )(order, *pieces)


TM = 256


def product_kernel(n_whole, n_half, first, last, *refs):
    refs = list(refs)
    mask = refs.pop(0) if last else None
    whole = [refs.pop(0) for _ in range(n_whole)]
    halves = [(refs.pop(0), refs.pop(0)) for _ in range(n_half)]
    b_high, b_low = refs.pop(0), refs.pop(0)
    before = None if first else refs.pop(0)
    out = refs.pop(0)
    tile = pl.program_id(0)
    upper = tile < pl.num_programs(0) // 2
    columns = [ref[...] for ref in whole]
    columns += [jnp.where(upper, lo[...], hi[...]) for lo, hi in halves]
    high, low = split(jnp.concatenate(columns, axis=1))
    total = jnp.dot(high, b_high[...], preferred_element_type=F32)
    total += jnp.dot(high, b_low[...], preferred_element_type=F32)
    total += jnp.dot(low, b_high[...], preferred_element_type=F32)
    if not first:
        total += before[...]
    if last:
        for r in range(TM // BS):
            for c in range(CB):
                keep = mask[tile * (TM // BS) + r, c].astype(F32)
                piece = total[r * BS : (r + 1) * BS, c * BS : (c + 1) * BS]
                out[pl.ds(r * BS, BS), pl.ds(c * BS, BS)] = piece * keep
    else:
        out[...] = total


def product(whole, halves, b_pair, before=None, mask=None):
    rows, cols = RB * BS, CB * BS
    tiles = rows // TM
    depth = b_pair[0].shape[0]
    a_spec = pl.BlockSpec((TM, BS), lambda t: (t, 0))
    lo_spec = pl.BlockSpec((TM, BS), lambda t: (jnp.minimum(t, tiles // 2 - 1), 0))
    hi_spec = pl.BlockSpec((TM, BS), lambda t: (jnp.maximum(t - tiles // 2, 0), 0))
    b_spec = pl.BlockSpec((depth, cols), lambda t: (0, 0))
    c_spec = pl.BlockSpec((TM, cols), lambda t: (t, 0))
    args, specs = [], []
    if mask is not None:
        args.append(mask)
        specs.append(SMEM)
    args += whole
    specs += [a_spec] * len(whole)
    for pair in halves:
        args += pair
        specs += [lo_spec, hi_spec]
    args += b_pair
    specs += [b_spec] * 2
    if before is not None:
        args.append(before)
        specs.append(c_spec)
    return pl.pallas_call(
        functools.partial(
            product_kernel, len(whole), len(halves), before is None, mask is not None
        ),
        grid=(tiles,),
        out_shape=jax.ShapeDtypeStruct((rows, cols), F32),
        in_specs=specs,
        out_specs=c_spec,
        cost_estimate=pl.CostEstimate(
            flops=6 * rows * cols * depth,
            bytes_accessed=4 * (rows * depth + depth * cols + 2 * rows * cols),
            transcendentals=0,
        ),
        name="product",
    )(*args)


def per_device(a_blocks, a_rows, a_cols, a_counts, b_blocks, b_rows, b_cols, b_counts, out_mask):
    row_now = lax.axis_index("row")
    col_now = lax.axis_index("col")
    z_now = row_now % NZ
    y_now, x_now, c_now = col_now // (NX * NC), col_now // NC % NX, col_now % NC

    b_send = pack_b(
        z_now.reshape(1), b_counts.reshape(-1), b_cols.reshape(-1), b_blocks.reshape(-1, BS, BS)
    )
    a_send = pack_a(a_counts.reshape(-1), a_rows.reshape(-1), a_blocks.reshape(-1, BS, BS))
    b_got = [b_send[0]] + [row_shift(b_send[rel], dz=rel) for rel in range(1, NZ)]
    a_got = lax.all_to_all(a_send, "col", split_axis=0, concat_axis=0, tiled=True)

    b_part = unpack_b(b_got)
    b_here = b_part + row_shift(b_part, dy=1)
    half = KZ * BS // 2
    b_behind = row_shift(b_here, dz=1)
    b_ahead = row_shift(b_here, dz=-1)
    b_far_lo = row_shift(b_behind[:half], dz=1)
    b_far_hi = row_shift(b_ahead[half:], dz=-1)

    def swap(value):
        return col_shift(value, dc=1)

    half = RB * BS // 2
    plane = []
    own = unpack_a(a_got)
    other = col_shift(own, dy=1)
    for first in (own, other):
        behind = col_shift(first, dx=1)
        ahead = col_shift(first, dx=-1)
        far_lo = col_shift(behind[:half], dx=1)
        far_hi = col_shift(ahead[half:], dx=-1)
        plane.append((first, behind, ahead, far_lo, far_hi))

    def pairs(values):
        return [v for value in values for v in (value, swap(value))]

    def far_pairs(lo, hi):
        return [(lo, hi), (swap(lo), swap(hi))]

    def k_of(dy, dx):
        return [col_id(y_now + dy, x_now + dx, c_now + dc) for dc in (0, 1)]

    near = (0, -1, 1)
    order = [k for dx in near for k in k_of(0, dx)] + k_of(0, 2)
    order += [k for dx in near for k in k_of(1, dx)] + k_of(1, 2)
    order = jnp.stack(order + [z_now]).astype(jnp.int32)
    b_all = order_b(order, (b_here, b_ahead, b_behind, b_far_lo, b_far_hi))

    total = product(pairs(plane[0][:3]), far_pairs(*plane[0][3:]), b_all[0:2])
    total = product(pairs(plane[1][:3]), [], b_all[2:4], before=total)
    return product([], far_pairs(*plane[1][3:]), b_all[4:6], before=total, mask=out_mask)


def solution(mesh):
    lists = P("row", "col", None)
    blocks = P("row", "col", None, None, None)
    in_specs = (blocks, lists, lists, lists, blocks, lists, lists, lists, P("row", "col"))
    return jax.shard_map(
        per_device, mesh=mesh, in_specs=in_specs, out_specs=P("row", "col"), check_vma=False
    )
```

time: 519 us -> 268 us (0.52)
  the two profiles are of different devices: /device:TPU:103 before, /device:TPU:1 now
where the time goes in v1:
time: 268 us
  Pallas kernels  103 us (38%)
  waiting for transfers between devices  95.9 us (36%)
  starting transfers between devices  57 us (21%)
  local copies, waits for them, and re-layouts  11.2 us (4%)
    ppermute x8, waiting for transfers between devices, row_shift(): return lax.ppermute(value, 'row', route)  73.9 us
    pallas_call x1, Pallas kernels, pack_a(): pl.pallas_call(pack_a_kernel, out_shape=jax.ShapeDtypeStruct((N_COL, CAP...  37.8 us
    pallas_call x3, Pallas kernels, product(): pl.pallas_call(functools.partial(product_kernel, len(whole), len(halves),...  32.4 us
    ppermute x19, starting transfers between devices, col_shift(): return lax.ppermute(value, 'col', route)  23.8 us
    ppermute x19, waiting for transfers between devices, col_shift(): return lax.ppermute(value, 'col', route)  21.9 us
    pallas_call x1, Pallas kernels, pack_b(): pl.pallas_call(pack_b_kernel, out_shape=[jax.ShapeDtypeStruct((rows, BS),...  20.1 us
    all_to_all x1, starting transfers between devices, per_device(): lax.all_to_all(a_send, 'col', split_axis=0, concat_axis=0, tiled=True)  16.8 us
    ppermute x8, starting transfers between devices, row_shift(): return lax.ppermute(value, 'row', route)  16.4 us
  transfers between devices with their start and end apart: 28, of which 7 were waited for; matrix products, arithmetic and copies ran while one was open for 3% of the time, Pallas kernels for 28%

profile of v1, /device:TPU:1, one launch (start us, length us, event | category | flops | bytes accessed | tf_op | source)
XLA Modules:
  0.0 268.5 jit_solution(883389010507228772)
XLA Ops:
  0.0 20.1 %pack_b.1 = (f32[1056,128]{1,0:T(8,128)}, f32[1056,128]{1,0:T(8,128)}, f32[1056,128]{1,0:T(8,128)}, f32[1056,128]{1,0:T(8,128)}) custom-call(s32[1]{0:T(128)} %bitcast.19.z_ref, s32[16]{0:T(128)} %bitcast.25, s32[32]{0:T(128)} %bitcast.26, f32[32,128,128]{2,1,0:T(8,128)} %bitcast.24), custom_call_target="tpu_custom_call" | custom-call | tf_op jit(solution)/shard_map/pack_b/pallas_call | solution.py:129
  20.1 8.4 %collective-permute-start.7 = (f32[1056,128]{1,0:T(8,128)}, f32[1056,128]{1,0:T(8,128)S(1)}, u32[]{:S(2)}, u32[]{:S(2)}) collective-permute-start(f32[1056,128]{1,0:T(8,128)} %get-tuple-element.16), channel_id=1, source_target_pairs={{0,16},{16,32},{32,48},{48,0},{64,80},{80,96},{96,112},{112,64},{1... | collective-permute-start | bytes 1622024 | tf_op jit(solution)/shard_map/ppermute | solution.py:44
  28.5 2.5 collective-permute-start.9
  31.0 37.8 %pack_a.1 = f32[16,264,128]{2,1,0:T(8,128)} custom-call(s32[16]{0:T(128)} %bitcast.27, s32[32]{0:T(128)} %bitcast.28, f32[32,128,128]{2,1,0:T(8,128)} %bitcast.23), custom_call_target="tpu_custom_call" | custom-call | tf_op jit(solution)/shard_map/pack_a/pallas_call | solution.py:78
  68.8 16.8 %all-to-all-start = ((f32[16,264,128]{2,1,0:T(8,128)}), f32[16,264,128]{2,1,0:T(8,128)S(1)}, u32[]{:S(2)}, u32[]{:S(2)}) async-start(f32[16,264,128]{2,1,0:T(8,128)} %pack_a.1), calls=%async_computation | async-start | bytes 4325376 | tf_op jit(solution)/shard_map/all_to_all | solution.py:364
  86.4 4.1 %unpack_b.1 = f32[512,512]{1,0:T(8,128)} custom-call(f32[1056,128]{1,0:T(8,128)} %get-tuple-element.15.refs_0_, f32[1056,128]{1,0:T(8,128)} %copy-done.3, f32[1056,128]{1,0:T(8,128)} %collective-permute-done.8.refs_2_, f32[1056,128]{1,0:T(8,128)} %collective-permute-done.9.refs_3_), custom_call_target="tpu_custom_call" | custom-call | tf_op jit(solution)/shard_map/unpack_b/pallas_call | solution.py:211
  90.6 41.6 %collective-permute-done.10 = f32[512,512]{1,0:T(8,128)S(1)} collective-permute-done((f32[512,512]{1,0:T(8,128)}, f32[512,512]{1,0:T(8,128)S(1)}, u32[]{:S(2)}, u32[]{:S(2)}) %collective-permute-start.10) | collective-permute-done | bytes 1048608 | tf_op jit(solution)/shard_map/ppermute | solution.py:44
  132.2 1.4 add.237.here
  133.6 5.2 %collective-permute-start.12 = (f32[512,512]{1,0:T(8,128)S(1)}, f32[512,512]{1,0:T(8,128)}, u32[]{:S(2)}, u32[]{:S(2)}) collective-permute-start(f32[512,512]{1,0:T(8,128)S(1)} %add.237.here), channel_id=1, source_target_pairs={{0,16},{16,32},{32,48},{48,0},{64,80},{80,96},{96,112},{112,64},{1... | collective-permute-start | bytes 3145736 | tf_op jit(solution)/shard_map/ppermute | solution.py:44
  138.9 1.3 copy-done
  140.2 3.4 %unpack_a.1.refs_0_ = f32[2048,128]{1,0:T(8,128)} custom-call(f32[16,264,128]{2,1,0:T(8,128)} %copy-done), custom_call_target="tpu_custom_call" | custom-call | tf_op jit(solution)/shard_map/unpack_a/pallas_call | solution.py:165
  143.9 1.5 collective-permute-start.19
  145.3 1.2 collective-permute-start.21
  146.6 14.2 %collective-permute-done.12.behind = f32[512,512]{1,0:T(8,128)} collective-permute-done((f32[512,512]{1,0:T(8,128)S(1)}, f32[512,512]{1,0:T(8,128)}, u32[]{:S(2)}, u32[]{:S(2)}) %collective-permute-start.12) | collective-permute-done | bytes 1048608 | tf_op jit(solution)/shard_map/ppermute | solution.py:44
  160.8 1.4 collective-permute-start.18
  162.3 5.5 %collective-permute-done.refs_0_ = f32[2048,128]{1,0:T(8,128)} collective-permute-done((f32[2048,128]{1,0:T(8,128)}, f32[2048,128]{1,0:T(8,128)}, u32[]{:S(2)}, u32[]{:S(2)}) %collective-permute-start) | collective-permute-done | bytes 1048608 | tf_op jit(solution)/shard_map/ppermute | solution.py:37
  169.6 2.0 collective-permute-start.3
  172.0 2.7 %collective-permute-start.24 = (f32[1024,128]{1,0:T(8,128)S(1)}, f32[1024,128]{1,0:T(8,128)S(1)}, u32[]{:S(2)}, u32[]{:S(2)}) collective-permute-start(f32[1024,128]{1,0:T(8,128)S(1)} %slice.29), channel_id=1, source_target_pairs={{0,6},{1,7},{2,0},{3,1},{4,2},{5,3},{6,4},{7,5},{8,14},{9,15},{10,... | collective-permute-start | bytes 1572872 | tf_op jit(solution)/shard_map/ppermute | solution.py:37
  174.7 9.5 %collective-permute-done.13.far_lo = f32[256,512]{1,0:T(8,128)S(1)} collective-permute-done((f32[256,512]{1,0:T(8,128)S(1)}, f32[256,512]{1,0:T(8,128)S(1)}, u32[]{:S(2)}, u32[]{:S(2)}) %collective-permute-start.13) | collective-permute-done | bytes 524320 | tf_op jit(solution)/shard_map/ppermute | solution.py:44
  184.2 3.1 %collective-permute-start.20 = (f32[2048,128]{1,0:T(8,128)S(1)}, f32[2048,128]{1,0:T(8,128)S(1)}, u32[]{:S(2)}, u32[]{:S(2)}) collective-permute-start(f32[2048,128]{1,0:T(8,128)S(1)} %collective-permute-done.19.refs_2_), channel_id=1, source_target_pairs={{0,1},{1,0},{2,3},{3,2},{4,5},{5,4},{6,7},{7,6},{8,9},{9,8},{10,11... | collective-permute-start | bytes 3145736 | tf_op jit(solution)/shard_map/ppermute | solution.py:37
  187.3 16.0 %collective-permute-done.23.refs_6_ = f32[1024,128]{1,0:T(8,128)S(1)} collective-permute-done((f32[1024,128]{1,0:T(8,128)S(1)}, f32[1024,128]{1,0:T(8,128)S(1)}, u32[]{:S(2)}, u32[]{:S(2)}) %collective-permute-start.23) | collective-permute-done | bytes 524320 | tf_op jit(solution)/shard_map/ppermute | solution.py:37
  203.4 2.7 collective-permute-start.22
  206.9 1.9 slice.24
  208.8 1.9 slice.25
  210.7 8.5 %collective-permute-done.14.far_hi = f32[256,512]{1,0:T(8,128)} collective-permute-done((f32[256,512]{1,0:T(8,128)S(1)}, f32[256,512]{1,0:T(8,128)}, u32[]{:S(2)}, u32[]{:S(2)}) %collective-permute-start.14) | collective-permute-done | bytes 524320 | tf_op jit(solution)/shard_map/ppermute | solution.py:44
  219.2 2.7 collective-permute-start.4
  221.9 2.0 collective-permute-start.15
  227.3 5.0 %order_b.1 = (bf16[1024,512]{1,0:T(8,128)(2,1)}, bf16[1024,512]{1,0:T(8,128)(2,1)}, bf16[768,512]{1,0:T(8,128)(2,1)}, bf16[768,512]{1,0:T(8,128)(2,1)}, bf16[256...) custom-call(s32[17]{0:T(128)} %stack.71.order, f32[512,512]{1,0:T(8,128)} %copy-done.1, f32[512,512]{1,0:T(8,128)} %copy-done.2, ...), custom_call_target="tpu_custom_call" | custom-call | tf_op jit(solution)/shard_map/order_b/pallas_call | solution.py:269
  232.7 2.3 collective-permute-start.5
  235.1 12.3 %product.3.refs_8_ = f32[2048,512]{1,0:T(8,128)} custom-call(f32[2048,128]{1,0:T(8,128)} %unpack_a.1.refs_0_, f32[2048,128]{1,0:T(8,128)} %copy-done.11, f32[2048,128]{1,0:T(8,128)} %copy-done.8, f32[2048,128]{1,0:T(8,128)} %copy-done.12, f32[2048,128]{1,0:T(8,128)} %copy-done.9, f32[2048,128]{1,0:T(8,128)} %copy-done.13, f32[1024,128]{1,0:T(8,128)} %copy-done.14, ...), custom_call_target="tpu_custom_call" | custom-call | flops 6442450944 | bytes 18874368 | tf_op jit(solution)/shard_map/product/pallas_call | solution.py:336
  247.4 11.5 %product.4.refs_7_ = f32[2048,512]{1,0:T(8,128)} custom-call(f32[2048,128]{1,0:T(8,128)} %collective-permute-done.refs_0_, f32[2048,128]{1,0:T(8,128)} %collective-permute-done.15.refs_1_, f32[2048,128]{1,0:T(8,128)} %collective-permute-done.1.refs_2_, f32[2048,128]{1,0:T(8,128)} %collective-permute-done.16.refs_3_, ...), custom_call_target="tpu_custom_call" | custom-call | flops 4831838208 | bytes 16252928 | tf_op jit(solution)/shard_map/product/pallas_call | solution.py:336
  259.9 8.6 %product.5 = f32[2048,512]{1,0:T(8,128)} custom-call(s32[16,4]{1,0:T(8,128)} %copy.8.refs_0_, f32[1024,128]{1,0:T(8,128)} %copy-done.5, f32[1024,128]{1,0:T(8,128)} %collective-permute-done.4.refs_2_, f32[1024,128]{1,0:T(8,128)} %copy-done.6, f32[1024,128]{1,0:T(8,128)} %copy-done.7, bf16[256,512]{1,0:T(8,128)(2,1)} %get-tuple-element.19.refs_5_, ...), custom_call_target="tpu_custom_call" | custom-call | flops 1610612736 | bytes 11010048 | tf_op jit(solution)/shard_map/product/pallas_call | solution.py:336
  (77 shorter events, 8.9 us)
Async XLA Ops:
  20.1 65.5 %collective-permute-start.7 = (f32[1056,128]{1,0:T(8,128)}, f32[1056,128]{1,0:T(8,128)S(1)}, u32[]{:S(2)}, u32[]{:S(2)}) collective-permute-start(f32[1056,128]{1,0:T(8,128)} %get-tuple-element.16), channel_id=1, source_target_pairs={{0,16},{16,32},{32,48},{48,0},{64,80},{80,96},{96,112},{112,64},{1... | collective-permute-start | bytes 1622024 | tf_op jit(solution)/shard_map/ppermute | solution.py:44
  28.5 57.1 %collective-permute-start.8 = (f32[1056,128]{1,0:T(8,128)}, f32[1056,128]{1,0:T(8,128)}, u32[]{:S(2)}, u32[]{:S(2)}) collective-permute-start(f32[1056,128]{1,0:T(8,128)} %get-tuple-element.17), channel_id=1, source_target_pairs={{0,32},{16,48},{32,0},{48,16},{64,96},{80,112},{96,64},{112,80},{1... | collective-permute-start | bytes 1622024 | tf_op jit(solution)/shard_map/ppermute | solution.py:44
  28.5 57.1 %collective-permute-start.9 = (f32[1056,128]{1,0:T(8,128)}, f32[1056,128]{1,0:T(8,128)}, u32[]{:S(2)}, u32[]{:S(2)}) collective-permute-start(f32[1056,128]{1,0:T(8,128)} %get-tuple-element.18), channel_id=1, source_target_pairs={{0,48},{16,0},{32,16},{48,32},{64,112},{80,64},{96,80},{112,96},{1... | collective-permute-start | bytes 1622024 | tf_op jit(solution)/shard_map/ppermute | solution.py:44
  68.8 70.1 %all-to-all-start = ((f32[16,264,128]{2,1,0:T(8,128)}), f32[16,264,128]{2,1,0:T(8,128)S(1)}, u32[]{:S(2)}, u32[]{:S(2)}) async-start(f32[16,264,128]{2,1,0:T(8,128)} %pack_a.1), calls=%async_computation | async-start | bytes 4325376 | tf_op jit(solution)/shard_map/all_to_all | solution.py:364
  90.5 41.7 %collective-permute-start.10 = (f32[512,512]{1,0:T(8,128)}, f32[512,512]{1,0:T(8,128)S(1)}, u32[]{:S(2)}, u32[]{:S(2)}) collective-permute-start(f32[512,512]{1,0:T(8,128)} %unpack_b.1), channel_id=1, source_target_pairs={{0,64},{16,80},{32,96},{48,112},{64,0},{80,16},{96,32},{112,48},{1... | collective-permute-start | bytes 3145736 | tf_op jit(solution)/shard_map/ppermute | solution.py:44
  133.6 93.7 %copy-start.1 = (f32[512,512]{1,0:T(8,128)}, f32[512,512]{1,0:T(8,128)S(1)}, u32[]{:S(2)}) copy-start(f32[512,512]{1,0:T(8,128)S(1)} %add.237.here) | copy-start | bytes 3145732
  133.6 27.2 %collective-permute-start.12 = (f32[512,512]{1,0:T(8,128)S(1)}, f32[512,512]{1,0:T(8,128)}, u32[]{:S(2)}, u32[]{:S(2)}) collective-permute-start(f32[512,512]{1,0:T(8,128)S(1)} %add.237.here), channel_id=1, source_target_pairs={{0,16},{16,32},{32,48},{48,0},{64,80},{80,96},{96,112},{112,64},{1... | collective-permute-start | bytes 3145736 | tf_op jit(solution)/shard_map/ppermute | solution.py:44
  143.6 24.2 %collective-permute-start = (f32[2048,128]{1,0:T(8,128)}, f32[2048,128]{1,0:T(8,128)}, u32[]{:S(2)}, u32[]{:S(2)}) collective-permute-start(f32[2048,128]{1,0:T(8,128)} %unpack_a.1.refs_0_), channel_id=1, source_target_pairs={{0,8},{1,9},{2,10},{3,11},{4,12},{5,13},{6,14},{7,15},{8,0},{9,1},... | collective-permute-start | bytes 3145736 | tf_op jit(solution)/shard_map/ppermute | solution.py:37
  143.9 25.7 %collective-permute-start.19 = (f32[2048,128]{1,0:T(8,128)}, f32[2048,128]{1,0:T(8,128)S(1)}, u32[]{:S(2)}, u32[]{:S(2)}) collective-permute-start(f32[2048,128]{1,0:T(8,128)} %unpack_a.1.refs_0_), channel_id=1, source_target_pairs={{0,2},{1,3},{2,4},{3,5},{4,6},{5,7},{6,0},{7,1},{8,10},{9,11},{10,... | collective-permute-start | bytes 3145736 | tf_op jit(solution)/shard_map/ppermute | solution.py:37
  145.3 26.4 %collective-permute-start.11 = (f32[512,512]{1,0:T(8,128)S(1)}, f32[512,512]{1,0:T(8,128)S(1)}, u32[]{:S(2)}, u32[]{:S(2)}) collective-permute-start(f32[512,512]{1,0:T(8,128)S(1)} %add.237.here), channel_id=1, source_target_pairs={{0,48},{16,0},{32,16},{48,32},{64,112},{80,64},{96,80},{112,96},{1... | collective-permute-start | bytes 3145736 | tf_op jit(solution)/shard_map/ppermute | solution.py:44
  145.3 26.5 %collective-permute-start.21 = (f32[2048,128]{1,0:T(8,128)}, f32[2048,128]{1,0:T(8,128)S(1)}, u32[]{:S(2)}, u32[]{:S(2)}) collective-permute-start(f32[2048,128]{1,0:T(8,128)} %unpack_a.1.refs_0_), channel_id=1, source_target_pairs={{0,6},{1,7},{2,0},{3,1},{4,2},{5,3},{6,4},{7,5},{8,14},{9,15},{10,... | collective-permute-start | bytes 3145736 | tf_op jit(solution)/shard_map/ppermute | solution.py:37
  160.8 11.1 %collective-permute-start.18 = (f32[2048,128]{1,0:T(8,128)}, f32[2048,128]{1,0:T(8,128)S(1)}, u32[]{:S(2)}, u32[]{:S(2)}) collective-permute-start(f32[2048,128]{1,0:T(8,128)} %unpack_a.1.refs_0_), channel_id=1, source_target_pairs={{0,1},{1,0},{2,3},{3,2},{4,5},{5,4},{6,7},{7,6},{8,9},{9,8},{10,11... | collective-permute-start | bytes 3145736 | tf_op jit(solution)/shard_map/ppermute | solution.py:37
  167.8 38.4 %collective-permute-start.1 = (f32[2048,128]{1,0:T(8,128)}, f32[2048,128]{1,0:T(8,128)}, u32[]{:S(2)}, u32[]{:S(2)}) collective-permute-start(f32[2048,128]{1,0:T(8,128)} %collective-permute-done.refs_0_), channel_id=1, source_target_pairs={{0,2},{1,3},{2,4},{3,5},{4,6},{5,7},{6,0},{7,1},{8,10},{9,11},{10,... | collective-permute-start | bytes 3145736 | tf_op jit(solution)/shard_map/ppermute | solution.py:37
  169.6 37.2 %collective-permute-start.3 = (f32[2048,128]{1,0:T(8,128)}, f32[2048,128]{1,0:T(8,128)}, u32[]{:S(2)}, u32[]{:S(2)}) collective-permute-start(f32[2048,128]{1,0:T(8,128)} %collective-permute-done.refs_0_), channel_id=1, source_target_pairs={{0,6},{1,7},{2,0},{3,1},{4,2},{5,3},{6,4},{7,5},{8,14},{9,15},{10,... | collective-permute-start | bytes 3145736 | tf_op jit(solution)/shard_map/ppermute | solution.py:37
  171.7 54.3 %copy-start.10 = (s32[16,4]{0,1:T(4,128)S(1)}, s32[16,4]{0,1:T(4,128)}, u32[]{:S(2)}) copy-start(s32[16,4]{0,1:T(4,128)} %param.15) | copy-start | bytes 772
  171.7 54.3 %copy-start.2 = (f32[512,512]{1,0:T(8,128)}, f32[512,512]{1,0:T(8,128)S(1)}, u32[]{:S(2)}) copy-start(f32[512,512]{1,0:T(8,128)S(1)} %collective-permute-done.11.ahead) | copy-start | bytes 3145732
  171.7 12.5 %collective-permute-start.13 = (f32[256,512]{1,0:T(8,128)S(1)}, f32[256,512]{1,0:T(8,128)S(1)}, u32[]{:S(2)}, u32[]{:S(2)}) collective-permute-start(f32[256,512]{1,0:T(8,128)S(1)} %slice.26), channel_id=1, source_target_pairs={{0,16},{16,32},{32,48},{48,0},{64,80},{80,96},{96,112},{112,64},{1... | collective-permute-start | bytes 1572872 | tf_op jit(solution)/shard_map/ppermute | solution.py:44
  171.8 52.0 %copy-start.9 = (f32[2048,128]{1,0:T(8,128)}, f32[2048,128]{1,0:T(8,128)S(1)}, u32[]{:S(2)}) copy-start(f32[2048,128]{1,0:T(8,128)S(1)} %collective-permute-done.21.refs_4_) | copy-start | bytes 3145732
  171.8 31.5 %collective-permute-start.23 = (f32[1024,128]{1,0:T(8,128)S(1)}, f32[1024,128]{1,0:T(8,128)S(1)}, u32[]{:S(2)}, u32[]{:S(2)}) collective-permute-start(f32[1024,128]{1,0:T(8,128)S(1)} %slice.28), channel_id=1, source_target_pairs={{0,2},{1,3},{2,4},{3,5},{4,6},{5,7},{6,0},{7,1},{8,10},{9,11},{10,... | collective-permute-start | bytes 1572872 | tf_op jit(solution)/shard_map/ppermute | solution.py:37
  172.0 34.1 %collective-permute-start.24 = (f32[1024,128]{1,0:T(8,128)S(1)}, f32[1024,128]{1,0:T(8,128)S(1)}, u32[]{:S(2)}, u32[]{:S(2)}) collective-permute-start(f32[1024,128]{1,0:T(8,128)S(1)} %slice.29), channel_id=1, source_target_pairs={{0,6},{1,7},{2,0},{3,1},{4,2},{5,3},{6,4},{7,5},{8,14},{9,15},{10,... | collective-permute-start | bytes 1572872 | tf_op jit(solution)/shard_map/ppermute | solution.py:37
  184.2 39.7 %collective-permute-start.20 = (f32[2048,128]{1,0:T(8,128)S(1)}, f32[2048,128]{1,0:T(8,128)S(1)}, u32[]{:S(2)}, u32[]{:S(2)}) collective-permute-start(f32[2048,128]{1,0:T(8,128)S(1)} %collective-permute-done.19.refs_2_), channel_id=1, source_target_pairs={{0,1},{1,0},{2,3},{3,2},{4,5},{5,4},{6,7},{7,6},{8,9},{9,8},{10,11... | collective-permute-start | bytes 3145736 | tf_op jit(solution)/shard_map/ppermute | solution.py:37
  203.4 20.6 %collective-permute-start.22 = (f32[2048,128]{1,0:T(8,128)S(1)}, f32[2048,128]{1,0:T(8,128)S(1)}, u32[]{:S(2)}, u32[]{:S(2)}) collective-permute-start(f32[2048,128]{1,0:T(8,128)S(1)} %collective-permute-done.21.refs_4_), channel_id=1, source_target_pairs={{0,1},{1,0},{2,3},{3,2},{4,5},{5,4},{6,7},{7,6},{8,9},{9,8},{10,11... | collective-permute-start | bytes 3145736 | tf_op jit(solution)/shard_map/ppermute | solution.py:37
  206.1 13.1 %collective-permute-start.14 = (f32[256,512]{1,0:T(8,128)S(1)}, f32[256,512]{1,0:T(8,128)}, u32[]{:S(2)}, u32[]{:S(2)}) collective-permute-start(f32[256,512]{1,0:T(8,128)S(1)} %slice.27), channel_id=1, source_target_pairs={{0,48},{16,0},{32,16},{48,32},{64,112},{80,64},{96,80},{112,96},{1... | collective-permute-start | bytes 1572872 | tf_op jit(solution)/shard_map/ppermute | solution.py:44
  206.2 13.0 %collective-permute-start.25 = (f32[1024,128]{1,0:T(8,128)S(1)}, f32[1024,128]{1,0:T(8,128)S(1)}, u32[]{:S(2)}, u32[]{:S(2)}) collective-permute-start(f32[1024,128]{1,0:T(8,128)S(1)} %collective-permute-done.23.refs_6_), channel_id=1, source_target_pairs={{0,1},{1,0},{2,3},{3,2},{4,5},{5,4},{6,7},{7,6},{8,9},{9,8},{10,11... | collective-permute-start | bytes 1572872 | tf_op jit(solution)/shard_map/ppermute | solution.py:37
  206.8 15.1 %collective-permute-start.26 = (f32[1024,128]{1,0:T(8,128)S(1)}, f32[1024,128]{1,0:T(8,128)S(1)}, u32[]{:S(2)}, u32[]{:S(2)}) collective-permute-start(f32[1024,128]{1,0:T(8,128)S(1)} %collective-permute-done.24.refs_7_), channel_id=1, source_target_pairs={{0,1},{1,0},{2,3},{3,2},{4,5},{5,4},{6,7},{7,6},{8,9},{9,8},{10,11... | collective-permute-start | bytes 1572872 | tf_op jit(solution)/shard_map/ppermute | solution.py:37
  219.2 13.4 %collective-permute-start.2 = (f32[1024,128]{1,0:T(8,128)}, f32[1024,128]{1,0:T(8,128)S(1)}, u32[]{:S(2)}, u32[]{:S(2)}) collective-permute-start(f32[1024,128]{1,0:T(8,128)} %slice.24), channel_id=1, source_target_pairs={{0,2},{1,3},{2,4},{3,5},{4,6},{5,7},{6,0},{7,1},{8,10},{9,11},{10,... | collective-permute-start | bytes 1572872 | tf_op jit(solution)/shard_map/ppermute | solution.py:37
  219.2 15.8 %collective-permute-start.4 = (f32[1024,128]{1,0:T(8,128)}, f32[1024,128]{1,0:T(8,128)}, u32[]{:S(2)}, u32[]{:S(2)}) collective-permute-start(f32[1024,128]{1,0:T(8,128)} %slice.25), channel_id=1, source_target_pairs={{0,6},{1,7},{2,0},{3,1},{4,2},{5,3},{6,4},{7,5},{8,14},{9,15},{10,... | collective-permute-start | bytes 1572872 | tf_op jit(solution)/shard_map/ppermute | solution.py:37
  221.9 25.5 %collective-permute-start.15 = (f32[2048,128]{1,0:T(8,128)}, f32[2048,128]{1,0:T(8,128)}, u32[]{:S(2)}, u32[]{:S(2)}) collective-permute-start(f32[2048,128]{1,0:T(8,128)} %collective-permute-done.refs_0_), channel_id=1, source_target_pairs={{0,1},{1,0},{2,3},{3,2},{4,5},{5,4},{6,7},{7,6},{8,9},{9,8},{10,11... | collective-permute-start | bytes 3145736 | tf_op jit(solution)/shard_map/ppermute | solution.py:37
  223.9 23.5 %collective-permute-start.16 = (f32[2048,128]{1,0:T(8,128)}, f32[2048,128]{1,0:T(8,128)}, u32[]{:S(2)}, u32[]{:S(2)}) collective-permute-start(f32[2048,128]{1,0:T(8,128)} %collective-permute-done.1.refs_2_), channel_id=1, source_target_pairs={{0,1},{1,0},{2,3},{3,2},{4,5},{5,4},{6,7},{7,6},{8,9},{9,8},{10,11... | collective-permute-start | bytes 3145736 | tf_op jit(solution)/shard_map/ppermute | solution.py:37
  225.8 21.6 %collective-permute-start.17 = (f32[2048,128]{1,0:T(8,128)}, f32[2048,128]{1,0:T(8,128)}, u32[]{:S(2)}, u32[]{:S(2)}) collective-permute-start(f32[2048,128]{1,0:T(8,128)} %collective-permute-done.3.refs_4_), channel_id=1, source_target_pairs={{0,1},{1,0},{2,3},{3,2},{4,5},{5,4},{6,7},{7,6},{8,9},{9,8},{10,11... | collective-permute-start | bytes 3145736 | tf_op jit(solution)/shard_map/ppermute | solution.py:37
  232.7 26.3 %collective-permute-start.5 = (f32[1024,128]{1,0:T(8,128)S(1)}, f32[1024,128]{1,0:T(8,128)S(1)}, u32[]{:S(2)}, u32[]{:S(2)}) collective-permute-start(f32[1024,128]{1,0:T(8,128)S(1)} %collective-permute-done.2.refs_1_), channel_id=1, source_target_pairs={{0,1},{1,0},{2,3},{3,2},{4,5},{5,4},{6,7},{7,6},{8,9},{9,8},{10,11... | collective-permute-start | bytes 1572872 | tf_op jit(solution)/shard_map/ppermute | solution.py:37
  235.0 24.0 %collective-permute-start.6 = (f32[1024,128]{1,0:T(8,128)}, f32[1024,128]{1,0:T(8,128)S(1)}, u32[]{:S(2)}, u32[]{:S(2)}) collective-permute-start(f32[1024,128]{1,0:T(8,128)} %collective-permute-done.4.refs_2_), channel_id=1, source_target_pairs={{0,1},{1,0},{2,3},{3,2},{4,5},{5,4},{6,7},{7,6},{8,9},{9,8},{10,11... | collective-permute-start | bytes 1572872 | tf_op jit(solution)/shard_map/ppermute | solution.py:37
  (14 other events, 202.2 us)

commit v2 on v1

--- a/solution.py
+++ b/solution.py
@@ -50,7 +50,7 @@
     return marks.astype(F32)
 
 
-def pack_a_kernel(counts, owners, blocks, send, marks, sems, mark_sem):
+def pack_a_kernel(counts, owners, blocks, send, sems):
     start = jnp.int32(0)
     jobs = []
     for k in range(KB):
@@ -65,13 +65,10 @@
             pl.when(have)(copy.start)
             jobs.append((have, copy))
             places.append(jnp.where(have, lax.rem(owners[slot], RB), -1))
-        marks[k] = lane_marks(*places)
+        send[k, pl.ds(CAP * BS, MET)] = lane_marks(*places)
         start = start + count
-    tail = pltpu.make_async_copy(marks, send.at[:, pl.ds(CAP * BS, MET)], mark_sem)
-    tail.start()
     for have, copy in jobs:
         pl.when(have)(copy.wait)
-    tail.wait()
 
 
 def pack_a(counts, owners, blocks):
@@ -79,24 +76,19 @@
         pack_a_kernel,
         out_shape=jax.ShapeDtypeStruct((N_COL, CAP * BS + MET, BS), F32),
         in_specs=[SMEM, SMEM, ANY],
-        out_specs=ANY,
-        scratch_shapes=[
-            pltpu.VMEM((KB, MET, BS), F32),
-            pltpu.SemaphoreType.DMA((KB, CAP)),
-            pltpu.SemaphoreType.DMA,
-        ],
+        out_specs=VMEM,
+        scratch_shapes=[pltpu.SemaphoreType.DMA((KB, CAP))],
         name="pack_a",
     )(counts, owners, blocks)
 
 
 def pack_b_kernel(z_ref, counts, owners, blocks, *rest):
-    sends, (marks, starts, sems, mark_sem) = rest[:NZ], rest[NZ:]
+    sends, (starts, sems) = rest[:NZ], rest[NZ:]
     start = jnp.int32(0)
     for k in range(KB):
         starts[k] = start
         start = start + counts[k]
     jobs = []
-    tails = []
     for rel in range(NZ):
         base = lax.rem(z_ref[0] + rel, NZ) * KZ
         for kk in range(KZ):
@@ -112,16 +104,9 @@
                 pl.when(have)(copy.start)
                 jobs.append((have, copy))
                 places.append(jnp.where(have, lax.rem(owners[slot], CB), -1))
-            marks[rel, pl.ds(kk * MET, MET)] = lane_marks(*places)
-        tail = pltpu.make_async_copy(
-            marks.at[rel], sends[rel].at[pl.ds(KZ * CAP * BS, KZ * MET)], mark_sem.at[rel]
-        )
-        tail.start()
-        tails.append(tail)
+            sends[rel][pl.ds(KZ * CAP * BS + kk * MET, MET)] = lane_marks(*places)
     for have, copy in jobs:
         pl.when(have)(copy.wait)
-    for tail in tails:
-        tail.wait()
 
 
 def pack_b(z_now, counts, owners, blocks):
@@ -130,12 +115,10 @@
         pack_b_kernel,
         out_shape=[jax.ShapeDtypeStruct((rows, BS), F32)] * NZ,
         in_specs=[SMEM, SMEM, SMEM, ANY],
-        out_specs=[ANY] * NZ,
+        out_specs=[VMEM] * NZ,
         scratch_shapes=[
-            pltpu.VMEM((NZ, KZ * MET, BS), F32),
             pltpu.SMEM((KB,), jnp.int32),
             pltpu.SemaphoreType.DMA((NZ, KZ * CAP)),
-            pltpu.SemaphoreType.DMA((NZ,)),
         ],
         name="pack_b",
     )(z_now, counts, owners, blocks)
@@ -165,7 +148,7 @@
     return pl.pallas_call(
         unpack_a_kernel,
         out_shape=jax.ShapeDtypeStruct((RB * BS, BS), F32),
-        in_specs=[ANY],
+        in_specs=[VMEM],
         out_specs=VMEM,
         scratch_shapes=[
             pltpu.SMEM((N_COL, BS), F32),
@@ -211,7 +194,7 @@
     return pl.pallas_call(
         unpack_b_kernel,
         out_shape=jax.ShapeDtypeStruct((KZ * BS, CB * BS), F32),
-        in_specs=[ANY] * NZ,
+        in_specs=[VMEM] * NZ,
         out_specs=VMEM,
         scratch_shapes=[
             pltpu.SMEM((NZ, KZ * MET, BS), F32),
@@ -231,7 +214,7 @@
 
 
 def order_b_kernel(order, here, ahead, behind, far_lo, far_hi, *rest):
-    outs, (panel, sems) = rest[:6], rest[6:]
+    outs, (panel, sems) = rest[:3], rest[3:]
     half = KZ // 2
     z_now = order[KB]
     jobs = []
@@ -257,20 +240,19 @@
         for q in range(n):
             jobs[p].wait()
             high, low = split(panel[pl.ds(p * BS, BS), :])
-            outs[2 * i][pl.ds(q * BS, BS), :] = high
-            outs[2 * i + 1][pl.ds(q * BS, BS), :] = low
+            outs[i][pl.ds(q * BS, BS), :] = high
+            outs[i][pl.ds((n + q) * BS, BS), :] = low
+            outs[i][pl.ds((2 * n + q) * BS, BS), :] = high
             p += 1
 
 
 def order_b(order, pieces):
-    outs = [
-        jax.ShapeDtypeStruct((n * BS, CB * BS), jnp.bfloat16) for n in PHASES for _ in range(2)
-    ]
+    outs = [jax.ShapeDtypeStruct((3 * n * BS, CB * BS), jnp.bfloat16) for n in PHASES]
     return pl.pallas_call(
         order_b_kernel,
         out_shape=outs,
         in_specs=[SMEM] + [ANY] * 5,
-        out_specs=[VMEM] * 6,
+        out_specs=[VMEM] * 3,
         scratch_shapes=[
             pltpu.VMEM((KB * BS, CB * BS), F32),
             pltpu.SemaphoreType.DMA((KB,)),
@@ -279,7 +261,7 @@
     )(order, *pieces)
 
 
-TM = 256
+TM = 512
 
 
 def product_kernel(n_whole, n_half, first, last, *refs):
@@ -287,7 +269,7 @@
     mask = refs.pop(0) if last else None
     whole = [refs.pop(0) for _ in range(n_whole)]
     halves = [(refs.pop(0), refs.pop(0)) for _ in range(n_half)]
-    b_high, b_low = refs.pop(0), refs.pop(0)
+    b_stack = refs.pop(0)
     before = None if first else refs.pop(0)
     out = refs.pop(0)
     tile = pl.program_id(0)
@@ -295,9 +277,9 @@
     columns = [ref[...] for ref in whole]
     columns += [jnp.where(upper, lo[...], hi[...]) for lo, hi in halves]
     high, low = split(jnp.concatenate(columns, axis=1))
-    total = jnp.dot(high, b_high[...], preferred_element_type=F32)
-    total += jnp.dot(high, b_low[...], preferred_element_type=F32)
-    total += jnp.dot(low, b_high[...], preferred_element_type=F32)
+    total = jnp.dot(
+        jnp.concatenate([high, high, low], axis=1), b_stack[...], preferred_element_type=F32
+    )
     if not first:
         total += before[...]
     if last:
@@ -310,14 +292,14 @@
         out[...] = total
 
 
-def product(whole, halves, b_pair, before=None, mask=None):
+def product(whole, halves, b_stack, before=None, mask=None):
     rows, cols = RB * BS, CB * BS
     tiles = rows // TM
-    depth = b_pair[0].shape[0]
+    depth = b_stack.shape[0] // 3
     a_spec = pl.BlockSpec((TM, BS), lambda t: (t, 0))
     lo_spec = pl.BlockSpec((TM, BS), lambda t: (jnp.minimum(t, tiles // 2 - 1), 0))
     hi_spec = pl.BlockSpec((TM, BS), lambda t: (jnp.maximum(t - tiles // 2, 0), 0))
-    b_spec = pl.BlockSpec((depth, cols), lambda t: (0, 0))
+    b_spec = pl.BlockSpec((3 * depth, cols), lambda t: (0, 0))
     c_spec = pl.BlockSpec((TM, cols), lambda t: (t, 0))
     args, specs = [], []
     if mask is not None:
@@ -328,8 +310,8 @@
     for pair in halves:
         args += pair
         specs += [lo_spec, hi_spec]
-    args += b_pair
-    specs += [b_spec] * 2
+    args.append(b_stack)
+    specs.append(b_spec)
     if before is not None:
         args.append(before)
         specs.append(c_spec)
@@ -400,9 +382,9 @@
     order = jnp.stack(order + [z_now]).astype(jnp.int32)
     b_all = order_b(order, (b_here, b_ahead, b_behind, b_far_lo, b_far_hi))
 
-    total = product(pairs(plane[0][:3]), far_pairs(*plane[0][3:]), b_all[0:2])
-    total = product(pairs(plane[1][:3]), [], b_all[2:4], before=total)
-    return product([], far_pairs(*plane[1][3:]), b_all[4:6], before=total, mask=out_mask)
+    total = product(pairs(plane[0][:3]), far_pairs(*plane[0][3:]), b_all[0])
+    total = product(pairs(plane[1][:3]), [], b_all[1], before=total)
+    return product([], far_pairs(*plane[1][3:]), b_all[2], before=total, mask=out_mask)
 
 
 def solution(mesh):

time: 268 us -> 201 us (0.75)
  Pallas kernels: 103 us -> 50.9 us
  starting transfers between devices: 57 us -> 45.5 us
  waiting for transfers between devices: 95.9 us -> 91.1 us
    pallas_call x1, Pallas kernels: 37.8 us -> 3.63 us  [pack_a(): pl.pallas_call(pack_a_kernel, out_shape=jax.ShapeDtypeStruct((N_COL, CAP...]
    pallas_call x1, Pallas kernels: 20.1 us -> 3.28 us  [pack_b(): pl.pallas_call(pack_b_kernel, out_shape=[jax.ShapeDtypeStruct((rows, BS),...]
    all_to_all x1, starting transfers between devices: 16.8 us -> 6.55 us  [per_device(): lax.all_to_all(a_send, 'col', split_axis=0, concat_axis=0, tiled=True)]
    pallas_call x3, Pallas kernels: 32.4 us -> 28.1 us  [product(): pl.pallas_call(functools.partial(product_kernel, len(whole), len(halves),...]
    ppermute x8, waiting for transfers between devices: 73.9 us -> 69.8 us  [row_shift(): return lax.ppermute(value, 'row', route)]
  transfers between devices with their start and end apart: 28 -> 28, of which waited for: 7 -> 8; matrix products, arithmetic and copies ran while one was open for 3% -> 4% of each run, Pallas kernels for 28% -> 21%
where the time goes in v2:
time: 201 us; the launch traced here: 200 us
  waiting for transfers between devices  91.1 us (45%)
  Pallas kernels  50.9 us (25%)
  starting transfers between devices  45.5 us (23%)
  local copies, waits for them, and re-layouts  10.4 us (5%)
    ppermute x8, waiting for transfers between devices, row_shift(): return lax.ppermute(value, 'row', route)  69.8 us
    pallas_call x3, Pallas kernels, product(): pl.pallas_call(functools.partial(product_kernel, len(whole), len(halves),...  28.1 us
    ppermute x19, starting transfers between devices, col_shift(): return lax.ppermute(value, 'col', route)  24.7 us
    ppermute x19, waiting for transfers between devices, col_shift(): return lax.ppermute(value, 'col', route)  21.3 us
    ppermute x8, starting transfers between devices, row_shift(): return lax.ppermute(value, 'row', route)  14.2 us
    all_to_all x1, starting transfers between devices, per_device(): lax.all_to_all(a_send, 'col', split_axis=0, concat_axis=0, tiled=True)  6.55 us
    pallas_call x1, Pallas kernels, order_b(): pl.pallas_call(order_b_kernel, out_shape=outs, in_specs=[SMEM] + [ANY] *...  5.62 us
    pallas_call x1, Pallas kernels, unpack_a(): pl.pallas_call(unpack_a_kernel, out_shape=jax.ShapeDtypeStruct((RB * BS,...  5.3 us
  transfers between devices with their start and end apart: 28, of which 8 were waited for; matrix products, arithmetic and copies ran while one was open for 4% of the time, Pallas kernels for 21%

profile of v2, /device:TPU:1, one launch (start us, length us, event | category | flops | bytes accessed | tf_op | source)
XLA Modules:
  0.0 199.6 jit_solution(15403805247052382988)
XLA Ops:
  0.0 3.3 %pack_b.1 = (f32[1056,128]{1,0:T(8,128)}, f32[1056,128]{1,0:T(8,128)}, f32[1056,128]{1,0:T(8,128)}, f32[1056,128]{1,0:T(8,128)}) custom-call(s32[1]{0:T(128)} %bitcast.19.z_ref, s32[16]{0:T(128)} %bitcast.25, s32[32]{0:T(128)} %bitcast.26, f32[32,128,128]{2,1,0:T(8,128)} %bitcast.24), custom_call_target="tpu_custom_call" | custom-call | tf_op jit(solution)/shard_map/pack_b/pallas_call | solution.py:114
  3.3 2.5 %collective-permute-start.7 = (f32[1056,128]{1,0:T(8,128)}, f32[1056,128]{1,0:T(8,128)S(1)}, u32[]{:S(2)}, u32[]{:S(2)}) collective-permute-start(f32[1056,128]{1,0:T(8,128)} %get-tuple-element.13), channel_id=1, source_target_pairs={{0,16},{16,32},{32,48},{48,0},{64,80},{80,96},{96,112},{112,64},{1... | collective-permute-start | bytes 1622024 | tf_op jit(solution)/shard_map/ppermute | solution.py:44
  5.8 3.5 %collective-permute-start.8 = (f32[1056,128]{1,0:T(8,128)}, f32[1056,128]{1,0:T(8,128)}, u32[]{:S(2)}, u32[]{:S(2)}) collective-permute-start(f32[1056,128]{1,0:T(8,128)} %get-tuple-element.14), channel_id=1, source_target_pairs={{0,32},{16,48},{32,0},{48,16},{64,96},{80,112},{96,64},{112,80},{1... | collective-permute-start | bytes 1622024 | tf_op jit(solution)/shard_map/ppermute | solution.py:44
  10.1 3.6 %pack_a.1 = f32[16,264,128]{2,1,0:T(8,128)} custom-call(s32[16]{0:T(128)} %bitcast.27, s32[32]{0:T(128)} %bitcast.28, f32[32,128,128]{2,1,0:T(8,128)} %bitcast.23), custom_call_target="tpu_custom_call" | custom-call | tf_op jit(solution)/shard_map/pack_a/pallas_call | solution.py:75
  13.7 6.5 %all-to-all-start = ((f32[16,264,128]{2,1,0:T(8,128)}), f32[16,264,128]{2,1,0:T(8,128)S(1)}, u32[]{:S(2)}, u32[]{:S(2)}) async-start(f32[16,264,128]{2,1,0:T(8,128)} %pack_a.1), calls=%async_computation | async-start | bytes 4325376 | tf_op jit(solution)/shard_map/all_to_all | solution.py:346
  20.5 12.5 %collective-permute-done.8.refs_2_ = f32[1056,128]{1,0:T(8,128)} collective-permute-done((f32[1056,128]{1,0:T(8,128)}, f32[1056,128]{1,0:T(8,128)}, u32[]{:S(2)}, u32[]{:S(2)}) %collective-permute-start.8) | collective-permute-done | bytes 540704 | tf_op jit(solution)/shard_map/ppermute | solution.py:44
  33.0 5.0 %unpack_b.1 = f32[512,512]{1,0:T(8,128)} custom-call(f32[1056,128]{1,0:T(8,128)} %get-tuple-element.12.refs_0_, f32[1056,128]{1,0:T(8,128)} %copy-done.3, f32[1056,128]{1,0:T(8,128)} %collective-permute-done.8.refs_2_, f32[1056,128]{1,0:T(8,128)} %collective-permute-done.9.refs_3_), custom_call_target="tpu_custom_call" | custom-call | tf_op jit(solution)/shard_map/unpack_b/pallas_call | solution.py:194
  38.0 2.9 %collective-permute-start.10 = (f32[512,512]{1,0:T(8,128)}, f32[512,512]{1,0:T(8,128)S(1)}, u32[]{:S(2)}, u32[]{:S(2)}) collective-permute-start(f32[512,512]{1,0:T(8,128)} %unpack_b.1), channel_id=1, source_target_pairs={{0,64},{16,80},{32,96},{48,112},{64,0},{80,16},{96,32},{112,48},{1... | collective-permute-start | bytes 3145736 | tf_op jit(solution)/shard_map/ppermute | solution.py:44
  40.9 29.1 %collective-permute-done.10 = f32[512,512]{1,0:T(8,128)S(1)} collective-permute-done((f32[512,512]{1,0:T(8,128)}, f32[512,512]{1,0:T(8,128)S(1)}, u32[]{:S(2)}, u32[]{:S(2)}) %collective-permute-start.10) | collective-permute-done | bytes 1048608 | tf_op jit(solution)/shard_map/ppermute | solution.py:44
  70.0 1.4 add.237.here
  73.5 5.3 %unpack_a.1.refs_0_ = f32[2048,128]{1,0:T(8,128)} custom-call(f32[16,264,128]{2,1,0:T(8,128)} %copy-done), custom_call_target="tpu_custom_call" | custom-call | tf_op jit(solution)/shard_map/unpack_a/pallas_call | solution.py:148
  80.5 1.9 collective-permute-start.11
  82.4 1.8 collective-permute-start.21
  84.3 12.9 %collective-permute-done.12.behind = f32[512,512]{1,0:T(8,128)} collective-permute-done((f32[512,512]{1,0:T(8,128)S(1)}, f32[512,512]{1,0:T(8,128)}, u32[]{:S(2)}, u32[]{:S(2)}) %collective-permute-start.12) | collective-permute-done | bytes 1048608 | tf_op jit(solution)/shard_map/ppermute | solution.py:44
  98.4 4.9 %collective-permute-done.refs_0_ = f32[2048,128]{1,0:T(8,128)} collective-permute-done((f32[2048,128]{1,0:T(8,128)}, f32[2048,128]{1,0:T(8,128)}, u32[]{:S(2)}, u32[]{:S(2)}) %collective-permute-start) | collective-permute-done | bytes 1048608 | tf_op jit(solution)/shard_map/ppermute | solution.py:37
  105.2 2.2 %collective-permute-start.3 = (f32[2048,128]{1,0:T(8,128)}, f32[2048,128]{1,0:T(8,128)}, u32[]{:S(2)}, u32[]{:S(2)}) collective-permute-start(f32[2048,128]{1,0:T(8,128)} %collective-permute-done.refs_0_), channel_id=1, source_target_pairs={{0,6},{1,7},{2,0},{3,1},{4,2},{5,3},{6,4},{7,5},{8,14},{9,15},{10,... | collective-permute-start | bytes 3145736 | tf_op jit(solution)/shard_map/ppermute | solution.py:37
  108.1 2.7 %collective-permute-start.24 = (f32[1024,128]{1,0:T(8,128)S(1)}, f32[1024,128]{1,0:T(8,128)S(1)}, u32[]{:S(2)}, u32[]{:S(2)}) collective-permute-start(f32[1024,128]{1,0:T(8,128)S(1)} %slice.29), channel_id=1, source_target_pairs={{0,6},{1,7},{2,0},{3,1},{4,2},{5,3},{6,4},{7,5},{8,14},{9,15},{10,... | collective-permute-start | bytes 1572872 | tf_op jit(solution)/shard_map/ppermute | solution.py:37
  110.9 9.4 %collective-permute-done.13.far_lo = f32[256,512]{1,0:T(8,128)S(1)} collective-permute-done((f32[256,512]{1,0:T(8,128)S(1)}, f32[256,512]{1,0:T(8,128)S(1)}, u32[]{:S(2)}, u32[]{:S(2)}) %collective-permute-start.13) | collective-permute-done | bytes 524320 | tf_op jit(solution)/shard_map/ppermute | solution.py:44
  120.3 2.8 %collective-permute-start.20 = (f32[2048,128]{1,0:T(8,128)S(1)}, f32[2048,128]{1,0:T(8,128)S(1)}, u32[]{:S(2)}, u32[]{:S(2)}) collective-permute-start(f32[2048,128]{1,0:T(8,128)S(1)} %collective-permute-done.19.refs_2_), channel_id=1, source_target_pairs={{0,1},{1,0},{2,3},{3,2},{4,5},{5,4},{6,7},{7,6},{8,9},{9,8},{10,11... | collective-permute-start | bytes 3145736 | tf_op jit(solution)/shard_map/ppermute | solution.py:37
  123.1 16.4 %collective-permute-done.23.refs_6_ = f32[1024,128]{1,0:T(8,128)S(1)} collective-permute-done((f32[1024,128]{1,0:T(8,128)S(1)}, f32[1024,128]{1,0:T(8,128)S(1)}, u32[]{:S(2)}, u32[]{:S(2)}) %collective-permute-start.23) | collective-permute-done | bytes 524320 | tf_op jit(solution)/shard_map/ppermute | solution.py:37
  139.5 2.3 %collective-permute-start.22 = (f32[2048,128]{1,0:T(8,128)S(1)}, f32[2048,128]{1,0:T(8,128)S(1)}, u32[]{:S(2)}, u32[]{:S(2)}) collective-permute-start(f32[2048,128]{1,0:T(8,128)S(1)} %collective-permute-done.21.refs_4_), channel_id=1, source_target_pairs={{0,1},{1,0},{2,3},{3,2},{4,5},{5,4},{6,7},{7,6},{8,9},{9,8},{10,11... | collective-permute-start | bytes 3145736 | tf_op jit(solution)/shard_map/ppermute | solution.py:37
  143.0 2.1 %collective-permute-start.25 = (f32[1024,128]{1,0:T(8,128)S(1)}, f32[1024,128]{1,0:T(8,128)S(1)}, u32[]{:S(2)}, u32[]{:S(2)}) collective-permute-start(f32[1024,128]{1,0:T(8,128)S(1)} %collective-permute-done.23.refs_6_), channel_id=1, source_target_pairs={{0,1},{1,0},{2,3},{3,2},{4,5},{5,4},{6,7},{7,6},{8,9},{9,8},{10,11... | collective-permute-start | bytes 1572872 | tf_op jit(solution)/shard_map/ppermute | solution.py:37
  145.2 1.9 slice.24
  147.1 1.9 slice.25
  149.0 5.7 %collective-permute-done.14.far_hi = f32[256,512]{1,0:T(8,128)} collective-permute-done((f32[256,512]{1,0:T(8,128)S(1)}, f32[256,512]{1,0:T(8,128)}, u32[]{:S(2)}, u32[]{:S(2)}) %collective-permute-start.14) | collective-permute-done | bytes 524320 | tf_op jit(solution)/shard_map/ppermute | solution.py:44
  154.7 2.7 %collective-permute-start.4 = (f32[1024,128]{1,0:T(8,128)}, f32[1024,128]{1,0:T(8,128)}, u32[]{:S(2)}, u32[]{:S(2)}) collective-permute-start(f32[1024,128]{1,0:T(8,128)} %slice.25), channel_id=1, source_target_pairs={{0,6},{1,7},{2,0},{3,1},{4,2},{5,3},{6,4},{7,5},{8,14},{9,15},{10,... | collective-permute-start | bytes 1572872 | tf_op jit(solution)/shard_map/ppermute | solution.py:37
  157.3 2.2 %collective-permute-start.15 = (f32[2048,128]{1,0:T(8,128)}, f32[2048,128]{1,0:T(8,128)}, u32[]{:S(2)}, u32[]{:S(2)}) collective-permute-start(f32[2048,128]{1,0:T(8,128)} %collective-permute-done.refs_0_), channel_id=1, source_target_pairs={{0,1},{1,0},{2,3},{3,2},{4,5},{5,4},{6,7},{7,6},{8,9},{9,8},{10,11... | collective-permute-start | bytes 3145736 | tf_op jit(solution)/shard_map/ppermute | solution.py:37
  163.1 5.6 %order_b.1 = (bf16[3072,512]{1,0:T(8,128)(2,1)}, bf16[2304,512]{1,0:T(8,128)(2,1)}, bf16[768,512]{1,0:T(8,128)(2,1)}) custom-call(s32[17]{0:T(128)} %stack.71.order, f32[512,512]{1,0:T(8,128)} %copy-done.1, f32[512,512]{1,0:T(8,128)} %copy-done.2, f32[512,512]{1,0:T(8,128)} %collective-permute-done.12.behind, f32[256,512]{1,0:T(8,128)} %copy-done.4, ...), custom_call_target="tpu_custom_call" | custom-call | tf_op jit(solution)/shard_map/order_b/pallas_call | solution.py:251
  168.7 1.7 collective-permute-start.5
  170.5 11.4 %product.3.refs_7_ = f32[2048,512]{1,0:T(8,128)} custom-call(f32[2048,128]{1,0:T(8,128)} %unpack_a.1.refs_0_, f32[2048,128]{1,0:T(8,128)} %copy-done.11, f32[2048,128]{1,0:T(8,128)} %copy-done.8, f32[2048,128]{1,0:T(8,128)} %copy-done.12, f32[2048,128]{1,0:T(8,128)} %copy-done.9, f32[2048,128]{1,0:T(8,128)} %copy-done.13, f32[1024,128]{1,0:T(8,128)} %copy-done.14, ...), custom_call_target="tpu_custom_call" | custom-call | flops 6442450944 | bytes 18874368 | tf_op jit(solution)/shard_map/product/pallas_call | solution.py:318
  181.9 10.2 %product.4.refs_6_ = f32[2048,512]{1,0:T(8,128)} custom-call(f32[2048,128]{1,0:T(8,128)} %collective-permute-done.refs_0_, f32[2048,128]{1,0:T(8,128)} %collective-permute-done.15.refs_1_, f32[2048,128]{1,0:T(8,128)} %collective-permute-done.1.refs_2_, f32[2048,128]{1,0:T(8,128)} %collective-permute-done.16.refs_3_, ...), custom_call_target="tpu_custom_call" | custom-call | flops 4831838208 | bytes 16252928 | tf_op jit(solution)/shard_map/product/pallas_call | solution.py:318
  193.1 6.5 %product.5 = f32[2048,512]{1,0:T(8,128)} custom-call(s32[16,4]{1,0:T(8,128)} %copy.8.refs_0_, f32[1024,128]{1,0:T(8,128)} %copy-done.5, f32[1024,128]{1,0:T(8,128)} %collective-permute-done.4.refs_2_, f32[1024,128]{1,0:T(8,128)} %copy-done.6, f32[1024,128]{1,0:T(8,128)} %copy-done.7, bf16[768,512]{1,0:T(8,128)(2,1)} %get-tuple-element.16.refs_5_, ...), custom_call_target="tpu_custom_call" | custom-call | flops 1610612736 | bytes 11010048 | tf_op jit(solution)/shard_map/product/pallas_call | solution.py:318
  (77 shorter events, 14.5 us)
Async XLA Ops:
  3.3 17.2 %collective-permute-start.7 = (f32[1056,128]{1,0:T(8,128)}, f32[1056,128]{1,0:T(8,128)S(1)}, u32[]{:S(2)}, u32[]{:S(2)}) collective-permute-start(f32[1056,128]{1,0:T(8,128)} %get-tuple-element.13), channel_id=1, source_target_pairs={{0,16},{16,32},{32,48},{48,0},{64,80},{80,96},{96,112},{112,64},{1... | collective-permute-start | bytes 1622024 | tf_op jit(solution)/shard_map/ppermute | solution.py:44
  5.8 27.2 %collective-permute-start.8 = (f32[1056,128]{1,0:T(8,128)}, f32[1056,128]{1,0:T(8,128)}, u32[]{:S(2)}, u32[]{:S(2)}) collective-permute-start(f32[1056,128]{1,0:T(8,128)} %get-tuple-element.14), channel_id=1, source_target_pairs={{0,32},{16,48},{32,0},{48,16},{64,96},{80,112},{96,64},{112,80},{1... | collective-permute-start | bytes 1622024 | tf_op jit(solution)/shard_map/ppermute | solution.py:44
  9.3 23.7 %collective-permute-start.9 = (f32[1056,128]{1,0:T(8,128)}, f32[1056,128]{1,0:T(8,128)}, u32[]{:S(2)}, u32[]{:S(2)}) collective-permute-start(f32[1056,128]{1,0:T(8,128)} %get-tuple-element.15), channel_id=1, source_target_pairs={{0,48},{16,0},{32,16},{48,32},{64,112},{80,64},{96,80},{112,96},{1... | collective-permute-start | bytes 1622024 | tf_op jit(solution)/shard_map/ppermute | solution.py:44
  13.7 58.4 %all-to-all-start = ((f32[16,264,128]{2,1,0:T(8,128)}), f32[16,264,128]{2,1,0:T(8,128)S(1)}, u32[]{:S(2)}, u32[]{:S(2)}) async-start(f32[16,264,128]{2,1,0:T(8,128)} %pack_a.1), calls=%async_computation | async-start | bytes 4325376 | tf_op jit(solution)/shard_map/all_to_all | solution.py:346
  38.0 32.0 %collective-permute-start.10 = (f32[512,512]{1,0:T(8,128)}, f32[512,512]{1,0:T(8,128)S(1)}, u32[]{:S(2)}, u32[]{:S(2)}) collective-permute-start(f32[512,512]{1,0:T(8,128)} %unpack_b.1), channel_id=1, source_target_pairs={{0,64},{16,80},{32,96},{48,112},{64,0},{80,16},{96,32},{112,48},{1... | collective-permute-start | bytes 3145736 | tf_op jit(solution)/shard_map/ppermute | solution.py:44
  71.4 91.7 %copy-start.1 = (f32[512,512]{1,0:T(8,128)}, f32[512,512]{1,0:T(8,128)S(1)}, u32[]{:S(2)}) copy-start(f32[512,512]{1,0:T(8,128)S(1)} %add.237.here) | copy-start | bytes 3145732
  71.4 25.7 %collective-permute-start.12 = (f32[512,512]{1,0:T(8,128)S(1)}, f32[512,512]{1,0:T(8,128)}, u32[]{:S(2)}, u32[]{:S(2)}) collective-permute-start(f32[512,512]{1,0:T(8,128)S(1)} %add.237.here), channel_id=1, source_target_pairs={{0,16},{16,32},{32,48},{48,0},{64,80},{80,96},{96,112},{112,64},{1... | collective-permute-start | bytes 3145736 | tf_op jit(solution)/shard_map/ppermute | solution.py:44
  78.8 24.4 %collective-permute-start = (f32[2048,128]{1,0:T(8,128)}, f32[2048,128]{1,0:T(8,128)}, u32[]{:S(2)}, u32[]{:S(2)}) collective-permute-start(f32[2048,128]{1,0:T(8,128)} %unpack_a.1.refs_0_), channel_id=1, source_target_pairs={{0,8},{1,9},{2,10},{3,11},{4,12},{5,13},{6,14},{7,15},{8,0},{9,1},... | collective-permute-start | bytes 3145736 | tf_op jit(solution)/shard_map/ppermute | solution.py:37
  79.6 25.6 %collective-permute-start.19 = (f32[2048,128]{1,0:T(8,128)}, f32[2048,128]{1,0:T(8,128)S(1)}, u32[]{:S(2)}, u32[]{:S(2)}) collective-permute-start(f32[2048,128]{1,0:T(8,128)} %unpack_a.1.refs_0_), channel_id=1, source_target_pairs={{0,2},{1,3},{2,4},{3,5},{4,6},{5,7},{6,0},{7,1},{8,10},{9,11},{10,... | collective-permute-start | bytes 3145736 | tf_op jit(solution)/shard_map/ppermute | solution.py:37
  80.5 26.9 %collective-permute-start.11 = (f32[512,512]{1,0:T(8,128)S(1)}, f32[512,512]{1,0:T(8,128)S(1)}, u32[]{:S(2)}, u32[]{:S(2)}) collective-permute-start(f32[512,512]{1,0:T(8,128)S(1)} %add.237.here), channel_id=1, source_target_pairs={{0,48},{16,0},{32,16},{48,32},{64,112},{80,64},{96,80},{112,96},{1... | collective-permute-start | bytes 3145736 | tf_op jit(solution)/shard_map/ppermute | solution.py:44
  82.4 25.6 %collective-permute-start.21 = (f32[2048,128]{1,0:T(8,128)}, f32[2048,128]{1,0:T(8,128)S(1)}, u32[]{:S(2)}, u32[]{:S(2)}) collective-permute-start(f32[2048,128]{1,0:T(8,128)} %unpack_a.1.refs_0_), channel_id=1, source_target_pairs={{0,6},{1,7},{2,0},{3,1},{4,2},{5,3},{6,4},{7,5},{8,14},{9,15},{10,... | collective-permute-start | bytes 3145736 | tf_op jit(solution)/shard_map/ppermute | solution.py:37
  97.1 11.0 %collective-permute-start.18 = (f32[2048,128]{1,0:T(8,128)}, f32[2048,128]{1,0:T(8,128)S(1)}, u32[]{:S(2)}, u32[]{:S(2)}) collective-permute-start(f32[2048,128]{1,0:T(8,128)} %unpack_a.1.refs_0_), channel_id=1, source_target_pairs={{0,1},{1,0},{2,3},{3,2},{4,5},{5,4},{6,7},{7,6},{8,9},{9,8},{10,11... | collective-permute-start | bytes 3145736 | tf_op jit(solution)/shard_map/ppermute | solution.py:37
  103.3 39.7 %collective-permute-start.1 = (f32[2048,128]{1,0:T(8,128)}, f32[2048,128]{1,0:T(8,128)}, u32[]{:S(2)}, u32[]{:S(2)}) collective-permute-start(f32[2048,128]{1,0:T(8,128)} %collective-permute-done.refs_0_), channel_id=1, source_target_pairs={{0,2},{1,3},{2,4},{3,5},{4,6},{5,7},{6,0},{7,1},{8,10},{9,11},{10,... | collective-permute-start | bytes 3145736 | tf_op jit(solution)/shard_map/ppermute | solution.py:37
  105.2 39.9 %collective-permute-start.3 = (f32[2048,128]{1,0:T(8,128)}, f32[2048,128]{1,0:T(8,128)}, u32[]{:S(2)}, u32[]{:S(2)}) collective-permute-start(f32[2048,128]{1,0:T(8,128)} %collective-permute-done.refs_0_), channel_id=1, source_target_pairs={{0,6},{1,7},{2,0},{3,1},{4,2},{5,3},{6,4},{7,5},{8,14},{9,15},{10,... | collective-permute-start | bytes 3145736 | tf_op jit(solution)/shard_map/ppermute | solution.py:37
  107.4 54.3 %copy-start.10 = (s32[16,4]{0,1:T(4,128)S(1)}, s32[16,4]{0,1:T(4,128)}, u32[]{:S(2)}) copy-start(s32[16,4]{0,1:T(4,128)} %param.15) | copy-start | bytes 772
  107.4 55.6 %copy-start.2 = (f32[512,512]{1,0:T(8,128)}, f32[512,512]{1,0:T(8,128)S(1)}, u32[]{:S(2)}) copy-start(f32[512,512]{1,0:T(8,128)S(1)} %collective-permute-done.11.ahead) | copy-start | bytes 3145732
  107.4 12.9 %collective-permute-start.13 = (f32[256,512]{1,0:T(8,128)S(1)}, f32[256,512]{1,0:T(8,128)S(1)}, u32[]{:S(2)}, u32[]{:S(2)}) collective-permute-start(f32[256,512]{1,0:T(8,128)S(1)} %slice.26), channel_id=1, source_target_pairs={{0,16},{16,32},{32,48},{48,0},{64,80},{80,96},{96,112},{112,64},{1... | collective-permute-start | bytes 1572872 | tf_op jit(solution)/shard_map/ppermute | solution.py:44
  108.1 31.4 %collective-permute-start.23 = (f32[1024,128]{1,0:T(8,128)S(1)}, f32[1024,128]{1,0:T(8,128)S(1)}, u32[]{:S(2)}, u32[]{:S(2)}) collective-permute-start(f32[1024,128]{1,0:T(8,128)S(1)} %slice.28), channel_id=1, source_target_pairs={{0,2},{1,3},{2,4},{3,5},{4,6},{5,7},{6,0},{7,1},{8,10},{9,11},{10,... | collective-permute-start | bytes 1572872 | tf_op jit(solution)/shard_map/ppermute | solution.py:37
  108.1 51.6 %copy-start.11 = (f32[2048,128]{1,0:T(8,128)}, f32[2048,128]{1,0:T(8,128)S(1)}, u32[]{:S(2)}) copy-start(f32[2048,128]{1,0:T(8,128)S(1)} %collective-permute-done.18.refs_1_) | copy-start | bytes 3145732
  108.1 33.7 %collective-permute-start.24 = (f32[1024,128]{1,0:T(8,128)S(1)}, f32[1024,128]{1,0:T(8,128)S(1)}, u32[]{:S(2)}, u32[]{:S(2)}) collective-permute-start(f32[1024,128]{1,0:T(8,128)S(1)} %slice.29), channel_id=1, source_target_pairs={{0,6},{1,7},{2,0},{3,1},{4,2},{5,3},{6,4},{7,5},{8,14},{9,15},{10,... | collective-permute-start | bytes 1572872 | tf_op jit(solution)/shard_map/ppermute | solution.py:37
  120.3 39.3 %collective-permute-start.20 = (f32[2048,128]{1,0:T(8,128)S(1)}, f32[2048,128]{1,0:T(8,128)S(1)}, u32[]{:S(2)}, u32[]{:S(2)}) collective-permute-start(f32[2048,128]{1,0:T(8,128)S(1)} %collective-permute-done.19.refs_2_), channel_id=1, source_target_pairs={{0,1},{1,0},{2,3},{3,2},{4,5},{5,4},{6,7},{7,6},{8,9},{9,8},{10,11... | collective-permute-start | bytes 3145736 | tf_op jit(solution)/shard_map/ppermute | solution.py:37
  139.5 20.2 %collective-permute-start.22 = (f32[2048,128]{1,0:T(8,128)S(1)}, f32[2048,128]{1,0:T(8,128)S(1)}, u32[]{:S(2)}, u32[]{:S(2)}) collective-permute-start(f32[2048,128]{1,0:T(8,128)S(1)} %collective-permute-done.21.refs_4_), channel_id=1, source_target_pairs={{0,1},{1,0},{2,3},{3,2},{4,5},{5,4},{6,7},{7,6},{8,9},{9,8},{10,11... | collective-permute-start | bytes 3145736 | tf_op jit(solution)/shard_map/ppermute | solution.py:37
  141.8 12.8 %collective-permute-start.14 = (f32[256,512]{1,0:T(8,128)S(1)}, f32[256,512]{1,0:T(8,128)}, u32[]{:S(2)}, u32[]{:S(2)}) collective-permute-start(f32[256,512]{1,0:T(8,128)S(1)} %slice.27), channel_id=1, source_target_pairs={{0,48},{16,0},{32,16},{48,32},{64,112},{80,64},{96,80},{112,96},{1... | collective-permute-start | bytes 1572872 | tf_op jit(solution)/shard_map/ppermute | solution.py:44
  143.0 11.7 %collective-permute-start.25 = (f32[1024,128]{1,0:T(8,128)S(1)}, f32[1024,128]{1,0:T(8,128)S(1)}, u32[]{:S(2)}, u32[]{:S(2)}) collective-permute-start(f32[1024,128]{1,0:T(8,128)S(1)} %collective-permute-done.23.refs_6_), channel_id=1, source_target_pairs={{0,1},{1,0},{2,3},{3,2},{4,5},{5,4},{6,7},{7,6},{8,9},{9,8},{10,11... | collective-permute-start | bytes 1572872 | tf_op jit(solution)/shard_map/ppermute | solution.py:37
  145.1 12.2 %collective-permute-start.26 = (f32[1024,128]{1,0:T(8,128)S(1)}, f32[1024,128]{1,0:T(8,128)S(1)}, u32[]{:S(2)}, u32[]{:S(2)}) collective-permute-start(f32[1024,128]{1,0:T(8,128)S(1)} %collective-permute-done.24.refs_7_), channel_id=1, source_target_pairs={{0,1},{1,0},{2,3},{3,2},{4,5},{5,4},{6,7},{7,6},{8,9},{9,8},{10,11... | collective-permute-start | bytes 1572872 | tf_op jit(solution)/shard_map/ppermute | solution.py:37
  154.6 14.1 %collective-permute-start.2 = (f32[1024,128]{1,0:T(8,128)}, f32[1024,128]{1,0:T(8,128)S(1)}, u32[]{:S(2)}, u32[]{:S(2)}) collective-permute-start(f32[1024,128]{1,0:T(8,128)} %slice.24), channel_id=1, source_target_pairs={{0,2},{1,3},{2,4},{3,5},{4,6},{5,7},{6,0},{7,1},{8,10},{9,11},{10,... | collective-permute-start | bytes 1572872 | tf_op jit(solution)/shard_map/ppermute | solution.py:37
  154.7 15.8 %collective-permute-start.4 = (f32[1024,128]{1,0:T(8,128)}, f32[1024,128]{1,0:T(8,128)}, u32[]{:S(2)}, u32[]{:S(2)}) collective-permute-start(f32[1024,128]{1,0:T(8,128)} %slice.25), channel_id=1, source_target_pairs={{0,6},{1,7},{2,0},{3,1},{4,2},{5,3},{6,4},{7,5},{8,14},{9,15},{10,... | collective-permute-start | bytes 1572872 | tf_op jit(solution)/shard_map/ppermute | solution.py:37
  157.3 24.6 %collective-permute-start.15 = (f32[2048,128]{1,0:T(8,128)}, f32[2048,128]{1,0:T(8,128)}, u32[]{:S(2)}, u32[]{:S(2)}) collective-permute-start(f32[2048,128]{1,0:T(8,128)} %collective-permute-done.refs_0_), channel_id=1, source_target_pairs={{0,1},{1,0},{2,3},{3,2},{4,5},{5,4},{6,7},{7,6},{8,9},{9,8},{10,11... | collective-permute-start | bytes 3145736 | tf_op jit(solution)/shard_map/ppermute | solution.py:37
  159.6 22.3 %collective-permute-start.16 = (f32[2048,128]{1,0:T(8,128)}, f32[2048,128]{1,0:T(8,128)}, u32[]{:S(2)}, u32[]{:S(2)}) collective-permute-start(f32[2048,128]{1,0:T(8,128)} %collective-permute-done.1.refs_2_), channel_id=1, source_target_pairs={{0,1},{1,0},{2,3},{3,2},{4,5},{5,4},{6,7},{7,6},{8,9},{9,8},{10,11... | collective-permute-start | bytes 3145736 | tf_op jit(solution)/shard_map/ppermute | solution.py:37
  161.6 20.3 %collective-permute-start.17 = (f32[2048,128]{1,0:T(8,128)}, f32[2048,128]{1,0:T(8,128)}, u32[]{:S(2)}, u32[]{:S(2)}) collective-permute-start(f32[2048,128]{1,0:T(8,128)} %collective-permute-done.3.refs_4_), channel_id=1, source_target_pairs={{0,1},{1,0},{2,3},{3,2},{4,5},{5,4},{6,7},{7,6},{8,9},{9,8},{10,11... | collective-permute-start | bytes 3145736 | tf_op jit(solution)/shard_map/ppermute | solution.py:37
  168.7 23.4 %collective-permute-start.5 = (f32[1024,128]{1,0:T(8,128)S(1)}, f32[1024,128]{1,0:T(8,128)S(1)}, u32[]{:S(2)}, u32[]{:S(2)}) collective-permute-start(f32[1024,128]{1,0:T(8,128)S(1)} %collective-permute-done.2.refs_1_), channel_id=1, source_target_pairs={{0,1},{1,0},{2,3},{3,2},{4,5},{5,4},{6,7},{7,6},{8,9},{9,8},{10,11... | collective-permute-start | bytes 1572872 | tf_op jit(solution)/shard_map/ppermute | solution.py:37
  170.4 21.8 %collective-permute-start.6 = (f32[1024,128]{1,0:T(8,128)}, f32[1024,128]{1,0:T(8,128)S(1)}, u32[]{:S(2)}, u32[]{:S(2)}) collective-permute-start(f32[1024,128]{1,0:T(8,128)} %collective-permute-done.4.refs_2_), channel_id=1, source_target_pairs={{0,1},{1,0},{2,3},{3,2},{4,5},{5,4},{6,7},{7,6},{8,9},{9,8},{10,11... | collective-permute-start | bytes 1572872 | tf_op jit(solution)/shard_map/ppermute | solution.py:37
  (14 other events, 214.5 us)

commit v3 on v2

v3 whole, which is shorter than its diff:
```python
import functools

import jax
import jax.numpy as jnp
from jax import lax
from jax.experimental import pallas as pl
from jax.experimental.pallas import tpu as pltpu
from jax.sharding import PartitionSpec as P

BS = 128
CAP = 2
NX, NY, NC, NZ = 4, 2, 2, 4
N_COL = NY * NX * NC
N_ROW = 2 * NZ
KB = 16
KZ = KB // NZ
RB = 16
CB = 4
MET = 8
F32 = jnp.float32
ANY = pl.BlockSpec(memory_space=pl.ANY)
HBM = pl.BlockSpec(memory_space=pltpu.HBM)
SMEM = pl.BlockSpec(memory_space=pltpu.SMEM)
VMEM = pl.BlockSpec(memory_space=pltpu.VMEM)


def col_id(y, x, c):
    return (y % NY) * NX * NC + (x % NX) * NC + c % NC


def col_shift(value, dy=0, dx=0, dc=0, by_core=False):
    route = [
        (col_id(y, x, c), col_id(y + dy, x + (dx if c == 0 or not by_core else -dx), c + dc))
        for y in range(NY)
        for x in range(NX)
        for c in range(NC)
    ]
    return lax.ppermute(value, "col", route)


def row_shift(value, dy=0, dz=0):
    route = [
        (y * NZ + z, (y + dy) % 2 * NZ + (z + dz) % NZ) for y in range(2) for z in range(NZ)
    ]
    return lax.ppermute(value, "row", route)


def row_shift_by_core(value, dz):
    route = []
    for i in range(N_ROW):
        for j in range(N_COL):
            step = dz if j % NC == 0 else -dz
            route.append((i * N_COL + j, (i // NZ * NZ + (i + step) % NZ) * N_COL + j))
    return lax.ppermute(value, ("row", "col"), route)


def after(value, *others):
    return lax.optimization_barrier((value, *others))[0]


def place():
    row, col = lax.axis_index("row"), lax.axis_index("col")
    core = lax.rem(col, NC)
    return (
        lax.rem(row, NZ),
        lax.div(col, NX * NC),
        lax.rem(lax.div(col, NC), NX),
        core,
        1 - 2 * core,
    )


def lane_marks(first, second):
    lane = lax.broadcasted_iota(jnp.int32, (MET, BS), 1)
    marks = jnp.where(lane == 0, first, jnp.where(lane == 1, second, -1))
    return marks.astype(F32)


def pack_a_kernel(counts, owners, blocks, send, sems):
    start = jnp.int32(0)
    jobs = []
    for k in range(KB):
        count = counts[k]
        places = []
        for rank in range(CAP):
            slot = jnp.minimum(start + rank, blocks.shape[0] - 1)
            copy = pltpu.make_async_copy(
                blocks.at[slot], send.at[k, pl.ds(rank * BS, BS)], sems.at[k, rank]
            )
            have = count > rank
            pl.when(have)(copy.start)
            jobs.append((have, copy))
            places.append(jnp.where(have, lax.rem(owners[slot], RB), -1))
        send[k, pl.ds(CAP * BS, MET)] = lane_marks(*places)
        start = start + count
    for have, copy in jobs:
        pl.when(have)(copy.wait)


def pack_a(counts, owners, blocks):
    return pl.pallas_call(
        pack_a_kernel,
        out_shape=jax.ShapeDtypeStruct((N_COL, CAP * BS + MET, BS), F32),
        in_specs=[SMEM, SMEM, ANY],
        out_specs=VMEM,
        scratch_shapes=[pltpu.SemaphoreType.DMA((KB, CAP))],
        name="pack_a",
    )(counts, owners, blocks)


def pack_b_kernel(counts, owners, blocks, *rest):
    sends, (starts, sems) = rest[:NZ], rest[NZ:]
    start = jnp.int32(0)
    for k in range(KB):
        starts[k] = start
        start = start + counts[k]
    jobs = []
    for rel in range(NZ):
        base = lax.rem(place()[0] + rel, NZ) * KZ
        for kk in range(KZ):
            count = counts[base + kk]
            places = []
            for rank in range(CAP):
                slot = jnp.minimum(starts[base + kk] + rank, blocks.shape[0] - 1)
                piece = kk * CAP + rank
                copy = pltpu.make_async_copy(
                    blocks.at[slot], sends[rel].at[pl.ds(piece * BS, BS)], sems.at[rel, piece]
                )
                have = count > rank
                pl.when(have)(copy.start)
                jobs.append((have, copy))
                places.append(jnp.where(have, lax.rem(owners[slot], CB), -1))
            sends[rel][pl.ds(KZ * CAP * BS + kk * MET, MET)] = lane_marks(*places)
    for have, copy in jobs:
        pl.when(have)(copy.wait)


def pack_b(counts, owners, blocks):
    rows = KZ * (CAP * BS + MET)
    return pl.pallas_call(
        pack_b_kernel,
        out_shape=[jax.ShapeDtypeStruct((rows, BS), F32)] * NZ,
        in_specs=[SMEM, SMEM, ANY],
        out_specs=[VMEM] * NZ,
        scratch_shapes=[
            pltpu.SMEM((KB,), jnp.int32),
            pltpu.SemaphoreType.DMA((NZ, KZ * CAP)),
        ],
        name="pack_b",
    )(counts, owners, blocks)


def unpack_a_kernel(got, panel, marks, sems, mark_sem):
    read = pltpu.make_async_copy(got.at[:, CAP * BS], marks, mark_sem)
    read.start()
    panel[...] = jnp.zeros_like(panel)
    read.wait()
    jobs = []
    for source in range(N_COL):
        for rank in range(CAP):
            place = marks[source, rank].astype(jnp.int32)
            have = place >= 0
            at = pl.multiple_of(jnp.maximum(place, 0) * BS, BS)
            copy = pltpu.make_async_copy(
                got.at[source, pl.ds(rank * BS, BS)], panel.at[pl.ds(at, BS)], sems.at[source, rank]
            )
            pl.when(have)(copy.start)
            jobs.append((have, copy))
    for have, copy in jobs:
        pl.when(have)(copy.wait)


def unpack_a(got):
    return pl.pallas_call(
        unpack_a_kernel,
        out_shape=jax.ShapeDtypeStruct((RB * BS, BS), F32),
        in_specs=[HBM],
        out_specs=VMEM,
        scratch_shapes=[
            pltpu.SMEM((N_COL, BS), F32),
            pltpu.SemaphoreType.DMA((N_COL, CAP)),
            pltpu.SemaphoreType.DMA,
        ],
        name="unpack_a",
    )(got)


def unpack_b_kernel(*refs):
    gots, (panel, marks, sems, mark_sem) = refs[:NZ], refs[NZ:]
    reads = []
    for rel in range(NZ):
        read = pltpu.make_async_copy(
            gots[rel].at[pl.ds(KZ * CAP * BS, KZ * MET)], marks.at[rel], mark_sem.at[rel]
        )
        read.start()
        reads.append(read)
    panel[...] = jnp.zeros_like(panel)
    for read in reads:
        read.wait()
    jobs = []
    for rel in range(NZ):
        for kk in range(KZ):
            for rank in range(CAP):
                place = marks[rel, kk * MET, rank].astype(jnp.int32)
                have = place >= 0
                at = pl.multiple_of(jnp.maximum(place, 0) * BS, BS)
                piece = kk * CAP + rank
                copy = pltpu.make_async_copy(
                    gots[rel].at[pl.ds(piece * BS, BS)],
                    panel.at[pl.ds(kk * BS, BS), pl.ds(at, BS)],
                    sems.at[rel, piece],
                )
                pl.when(have)(copy.start)
                jobs.append((have, copy))
    for have, copy in jobs:
        pl.when(have)(copy.wait)


def unpack_b(gots):
    return pl.pallas_call(
        unpack_b_kernel,
        out_shape=jax.ShapeDtypeStruct((KZ * BS, CB * BS), F32),
        in_specs=[HBM] * NZ,
        out_specs=VMEM,
        scratch_shapes=[
            pltpu.SMEM((NZ, KZ * MET, BS), F32),
            pltpu.SemaphoreType.DMA((NZ, KZ * CAP)),
            pltpu.SemaphoreType.DMA((NZ,)),
        ],
        name="unpack_b",
    )(*gots)


def split(value):
    high = value.astype(jnp.bfloat16)
    return high, (value - high.astype(F32)).astype(jnp.bfloat16)


def k_order():
    _, y, x, c, step = place()
    ks = []
    for dy in range(NY):
        y_at = lax.rem(y + dy, NY)
        for dx in (0, -step, step, 2):
            for dc in range(NC):
                x_at = lax.rem(x + NX + (dx if dc == 0 or isinstance(dx, int) else -dx), NX)
                ks.append(y_at * (NX * NC) + x_at * NC + lax.rem(c + dc, NC))
    return ks


TM = 512


def product_kernel(mask, here, first, second, far, *rest):
    pieces, (out, panel, stack, sems) = rest[:KB], rest[KB:]
    tile = pl.program_id(0)

    @pl.when(tile == 0)
    def _():
        z_now, step = place()[0], place()[4]
        jobs = []
        for p, k in enumerate(k_order()):
            hop = lax.rem((z_now - lax.div(k, KZ)) * step + 2 * NZ, NZ)
            row = pl.multiple_of(lax.rem(k, KZ) * BS, BS)
            for want, source in ((0, here), (1, first), (2, far), (3, second)):
                copy = pltpu.make_async_copy(
                    source.at[pl.ds(row, BS)], panel.at[pl.ds(p * BS, BS)], sems.at[p]
                )
                pl.when(hop == want)(copy.start)
            jobs.append(copy)
        for p, job in enumerate(jobs):
            job.wait()
            high, low = split(panel[pl.ds(p * BS, BS), :])
            stack[pl.ds(p * BS, BS), :] = high
            stack[pl.ds((KB + p) * BS, BS), :] = low

    high, low = split(jnp.concatenate([ref[...] for ref in pieces], axis=1))
    total = jnp.dot(
        jnp.concatenate([high, high], axis=1), stack[...], preferred_element_type=F32
    )
    total += jnp.dot(low, stack[pl.ds(0, KB * BS), :], preferred_element_type=F32)
    for r in range(TM // BS):
        for c in range(CB):
            keep = mask[tile * (TM // BS) + r, c].astype(F32)
            piece = total[r * BS : (r + 1) * BS, c * BS : (c + 1) * BS]
            out[pl.ds(r * BS, BS), pl.ds(c * BS, BS)] = piece * keep


def product(mask, b_pieces, a_pieces):
    rows, cols = RB * BS, CB * BS
    return pl.pallas_call(
        product_kernel,
        grid=(rows // TM,),
        out_shape=jax.ShapeDtypeStruct((rows, cols), F32),
        in_specs=[SMEM]
        + [ANY] * len(b_pieces)
        + [pl.BlockSpec((TM, BS), lambda t: (t, 0))] * len(a_pieces),
        out_specs=pl.BlockSpec((TM, cols), lambda t: (t, 0)),
        scratch_shapes=[
            pltpu.VMEM((KB * BS, cols), F32),
            pltpu.VMEM((2 * KB * BS, cols), jnp.bfloat16),
            pltpu.SemaphoreType.DMA((KB,)),
        ],
        compiler_params=pltpu.CompilerParams(vmem_limit_bytes=48 << 20),
        name="product",
    )(mask, *b_pieces, *a_pieces)


def per_device(a_blocks, a_rows, a_cols, a_counts, b_blocks, b_rows, b_cols, b_counts, out_mask):
    a_send = pack_a(a_counts.reshape(-1), a_rows.reshape(-1), a_blocks.reshape(-1, BS, BS))
    a_got = lax.all_to_all(a_send, "col", split_axis=0, concat_axis=0, tiled=True)
    b_send = pack_b(
        after(b_counts.reshape(-1), a_send), b_cols.reshape(-1), b_blocks.reshape(-1, BS, BS)
    )
    b_got = [b_send[0]] + [row_shift(b_send[rel], dz=rel) for rel in range(1, NZ)]
    b_part = unpack_b(b_got)
    own = unpack_a(a_got)
    joined = lax.optimization_barrier

    def swap(value, *earlier):
        return col_shift(after(value, *earlier) if earlier else value, dc=1)

    def hop(value, step):
        return col_shift(value, dx=step, by_core=True)

    own_first, own_second, other = hop(own, 1), hop(own, -1), col_shift(own, dy=1)
    own_first, own_second = joined((own_first, own_second))
    own_far = hop(own_first, 1)
    b_here = b_part + after(row_shift(b_part, dy=1), own_first)
    b_first, b_second = row_shift_by_core(b_here, 1), row_shift_by_core(b_here, -1)
    b_far = row_shift_by_core(b_first, 1)
    other_first, other_second = hop(other, 1), hop(other, -1)
    other_far = hop(other_first, 1)

    a_all = []
    for value in (own, own_first, own_second, own_far):
        a_all += [value, swap(value)]
    for value in (other, other_first, other_second, other_far):
        a_all += [value, swap(value)]
    return product(out_mask, (b_here, b_first, b_second, b_far), a_all)


def solution(mesh):
    lists = P("row", "col", None)
    blocks = P("row", "col", None, None, None)
    in_specs = (blocks, lists, lists, lists, blocks, lists, lists, lists, P("row", "col"))
    return jax.shard_map(
        per_device, mesh=mesh, in_specs=in_specs, out_specs=P("row", "col"), check_vma=False
    )
```

time: 201 us -> 161 us (0.80)
  Pallas kernels: 50.9 us -> 33.4 us
  local copies, waits for them, and re-layouts: 10.4 us -> 1.45 us
  waiting for transfers between devices: 91.1 us -> 82.3 us
  starting transfers between devices: 45.5 us -> 41 us
    ppermute x8 -> x4, waiting for transfers between devices: 69.8 us -> 19.1 us  [row_shift(): return lax.ppermute(value, 'row', route)]
    ppermute x0 -> x3, waiting for transfers between devices: none -> 21.7 us  [row_shift_by_core(): return lax.ppermute(value, ('row', 'col'), route)]
    all_to_all x1, waiting for transfers between devices: 0.01 us -> 19.5 us  [per_device(): lax.all_to_all(a_send, 'col', split_axis=0, concat_axis=0, tiled=True)]
    pallas_call x4 -> x1, Pallas kernels: 33.7 us -> 19.2 us  [product(): pl.pallas_call(product_kernel, grid=(rows // TM,), out_shape=jax.ShapeDty...]
    ppermute x0 -> x3, starting transfers between devices: none -> 7.24 us  [row_shift_by_core(): return lax.ppermute(value, ('row', 'col'), route)]
    ppermute x19 -> x15, starting transfers between devices: 24.7 us -> 18.4 us  [col_shift(): return lax.ppermute(value, 'col', route)]
    ppermute x8 -> x4, starting transfers between devices: 14.2 us -> 8.48 us  [row_shift(): return lax.ppermute(value, 'row', route)]
    slice x6 -> x0, local copies, waits for them, and re-layouts: 4.96 us -> none  [the longest x2 1.94 us: per_device(): far_lo = col_shift(behind[:half], dx=1)]
  transfers between devices with their start and end apart: 28 -> 23, of which waited for: 8 -> 7; matrix products, arithmetic and copies ran while one was open for 4% -> 1% of each run, Pallas kernels for 21% -> 7%
where the time goes in v3:
time: 161 us; the launch traced here: 160 us
  waiting for transfers between devices  82.3 us (51%)
  starting transfers between devices  41 us (25%)
  Pallas kernels  33.4 us (21%)
    ppermute x15, waiting for transfers between devices, col_shift(): return lax.ppermute(value, 'col', route)  22.1 us
    ppermute x3, waiting for transfers between devices, row_shift_by_core(): return lax.ppermute(value, ('row', 'col'), route)  21.7 us
    all_to_all x1, waiting for transfers between devices, per_device(): lax.all_to_all(a_send, 'col', split_axis=0, concat_axis=0, tiled=True)  19.5 us
    pallas_call x1, Pallas kernels, product(): pl.pallas_call(product_kernel, grid=(rows // TM,), out_shape=jax.ShapeDty...  19.2 us
    ppermute x4, waiting for transfers between devices, row_shift(): return lax.ppermute(value, 'row', route)  19.1 us
    ppermute x15, starting transfers between devices, col_shift(): return lax.ppermute(value, 'col', route)  18.4 us
    ppermute x4, starting transfers between devices, row_shift(): return lax.ppermute(value, 'row', route)  8.48 us
    ppermute x3, starting transfers between devices, row_shift_by_core(): return lax.ppermute(value, ('row', 'col'), route)  7.24 us
  transfers between devices with their start and end apart: 23, of which 7 were waited for; matrix products, arithmetic and copies ran while one was open for 1% of the time, Pallas kernels for 7%

profile of v3, /device:TPU:1, one launch (start us, length us, event | category | flops | bytes accessed | tf_op | source)
XLA Modules:
  0.0 159.9 jit_solution(4930778870502810503)
XLA Ops:
  0.0 3.5 %pack_a.1 = f32[16,264,128]{2,1,0:T(8,128)} custom-call(s32[16]{0:T(128)} %bitcast.8, s32[32]{0:T(128)} %bitcast.9, f32[32,128,128]{2,1,0:T(8,128)} %bitcast.6), custom_call_target="tpu_custom_call" | custom-call | tf_op jit(solution)/shard_map/pack_a/pallas_call | solution.py:101
  3.5 6.8 %all-to-all-start = ((f32[16,264,128]{2,1,0:T(8,128)}), f32[16,264,128]{2,1,0:T(8,128)S(1)}, u32[]{:S(2)}, u32[]{:S(2)}) async-start(f32[16,264,128]{2,1,0:T(8,128)} %pack_a.1), calls=%async_computation | async-start | bytes 4325376 | tf_op jit(solution)/shard_map/all_to_all | solution.py:311
  10.3 3.5 %pack_b.1 = (f32[1056,128]{1,0:T(8,128)}, f32[1056,128]{1,0:T(8,128)}, f32[1056,128]{1,0:T(8,128)}, f32[1056,128]{1,0:T(8,128)}) custom-call(s32[16]{0:T(128)} %bitcast.10, s32[32]{0:T(128)} %bitcast.11, f32[32,128,128]{2,1,0:T(8,128)} %bitcast.7), custom_call_target="tpu_custom_call" | custom-call | tf_op jit(solution)/shard_map/pack_b/pallas_call | solution.py:140
  13.8 1.7 %collective-permute-start = (f32[1056,128]{1,0:T(8,128)}, f32[1056,128]{1,0:T(8,128)}, u32[]{:S(2)}, u32[]{:S(2)}) collective-permute-start(f32[1056,128]{1,0:T(8,128)} %get-tuple-element.15), channel_id=1, source_target_pairs={{0,16},{16,32},{32,48},{48,0},{64,80},{80,96},{96,112},{112,64},{1... | collective-permute-start | bytes 1622024 | tf_op jit(solution)/shard_map/ppermute | solution.py:45
  15.5 3.5 %collective-permute-start.1 = (f32[1056,128]{1,0:T(8,128)}, f32[1056,128]{1,0:T(8,128)}, u32[]{:S(2)}, u32[]{:S(2)}) collective-permute-start(f32[1056,128]{1,0:T(8,128)} %get-tuple-element.16), channel_id=1, source_target_pairs={{0,32},{16,48},{32,0},{48,16},{64,96},{80,112},{96,64},{112,80},{1... | collective-permute-start | bytes 1622024 | tf_op jit(solution)/shard_map/ppermute | solution.py:45
  19.4 19.5 %all-to-all-done.got = f32[16,264,128]{2,1,0:T(8,128)S(1)} async-done(((f32[16,264,128]{2,1,0:T(8,128)}), f32[16,264,128]{2,1,0:T(8,128)S(1)}, u32[]{:S(2)}, u32[]{:S(2)}) %all-to-all-start) | async-done | bytes 2162720 | tf_op jit(solution)/shard_map/all_to_all | solution.py:311
  38.9 1.3 copy-done.1
  40.2 3.2 %unpack_a.1.rest_0_ = f32[2048,128]{1,0:T(8,128)} custom-call(f32[16,264,128]{2,1,0:T(8,128)} %copy-done.1), custom_call_target="tpu_custom_call" | custom-call | tf_op jit(solution)/shard_map/unpack_a/pallas_call | solution.py:174
  43.5 0.9 collective-permute-start.14
  44.4 2.2 %collective-permute-start.5 = (f32[2048,128]{1,0:T(8,128)}, f32[2048,128]{1,0:T(8,128)}, u32[]{:S(2)}, u32[]{:S(2)}) collective-permute-start(f32[2048,128]{1,0:T(8,128)} %unpack_a.1.rest_0_), channel_id=1, source_target_pairs={{0,6},{1,3},{2,0},{3,5},{4,2},{5,7},{6,4},{7,1},{8,14},{9,11},{10,... | collective-permute-start | bytes 3145736 | tf_op jit(solution)/shard_map/ppermute | solution.py:38
  47.1 4.1 %unpack_b.1 = f32[512,512]{1,0:T(8,128)} custom-call(f32[1056,128]{1,0:T(8,128)} %get-tuple-element.14.refs_0_, f32[1056,128]{1,0:T(8,128)} %collective-permute-done.refs_1_, f32[1056,128]{1,0:T(8,128)} %collective-permute-done.1.refs_2_, f32[1056,128]{1,0:T(8,128)} %collective-permute-done.2.refs_3_), custom_call_target="tpu_custom_call" | custom-call | tf_op jit(solution)/shard_map/unpack_b/pallas_call | solution.py:220
  51.2 2.9 %collective-permute-start.3 = (f32[512,512]{1,0:T(8,128)}, f32[512,512]{1,0:T(8,128)S(1)}, u32[]{:S(2)}, u32[]{:S(2)}) collective-permute-start(f32[512,512]{1,0:T(8,128)} %unpack_b.1), channel_id=1, source_target_pairs={{0,64},{16,80},{32,96},{48,112},{64,0},{80,16},{96,32},{112,48},{1... | collective-permute-start | bytes 3145736 | tf_op jit(solution)/shard_map/ppermute | solution.py:45
  54.1 1.0 collective-permute-start.9
  55.1 12.7 %collective-permute-done.14.rest_8_ = f32[2048,128]{1,0:T(8,128)} collective-permute-done((f32[2048,128]{1,0:T(8,128)}, f32[2048,128]{1,0:T(8,128)}, u32[]{:S(2)}, u32[]{:S(2)}) %collective-permute-start.14) | collective-permute-done | bytes 1048608 | tf_op jit(solution)/shard_map/ppermute | solution.py:38
  67.8 2.6 %collective-permute-start.18 = (f32[2048,128]{1,0:T(8,128)}, f32[2048,128]{1,0:T(8,128)}, u32[]{:S(2)}, u32[]{:S(2)}) collective-permute-start(f32[2048,128]{1,0:T(8,128)} %collective-permute-done.14.rest_8_), channel_id=1, source_target_pairs={{0,6},{1,3},{2,0},{3,5},{4,2},{5,7},{6,4},{7,1},{8,14},{9,11},{10,... | collective-permute-start | bytes 3145736 | tf_op jit(solution)/shard_map/ppermute | solution.py:38
  70.4 1.3 collective-permute-done.4.rest_2_
  71.7 1.3 collective-permute-start.16
  73.1 19.0 %collective-permute-done.3 = f32[512,512]{1,0:T(8,128)S(1)} collective-permute-done((f32[512,512]{1,0:T(8,128)}, f32[512,512]{1,0:T(8,128)S(1)}, u32[]{:S(2)}, u32[]{:S(2)}) %collective-permute-start.3) | collective-permute-done | bytes 1048608 | tf_op jit(solution)/shard_map/ppermute | solution.py:45
  92.1 1.8 %collective-permute-start.11 = (f32[2048,128]{1,0:T(8,128)}, f32[2048,128]{1,0:T(8,128)S(1)}, u32[]{:S(2)}, u32[]{:S(2)}) collective-permute-start(f32[2048,128]{1,0:T(8,128)} %collective-permute-done.5.rest_4_), channel_id=1, source_target_pairs={{0,1},{1,0},{2,3},{3,2},{4,5},{5,4},{6,7},{7,6},{8,9},{9,8},{10,11... | collective-permute-start | bytes 3145736 | tf_op jit(solution)/shard_map/ppermute | solution.py:38
  93.9 1.4 add.3.here
  95.3 0.5 collective-permute-start.12
  95.8 2.1 %collective-permute-start.10 = (f32[2048,128]{1,0:T(8,128)}, f32[2048,128]{1,0:T(8,128)S(1)}, u32[]{:S(2)}, u32[]{:S(2)}) collective-permute-start(f32[2048,128]{1,0:T(8,128)} %collective-permute-done.4.rest_2_), channel_id=1, source_target_pairs={{0,1},{1,0},{2,3},{3,2},{4,5},{5,4},{6,7},{7,6},{8,9},{9,8},{10,11... | collective-permute-start | bytes 3145736 | tf_op jit(solution)/shard_map/ppermute | solution.py:38
  97.9 1.7 %collective-permute-start.7 = (f32[512,512]{1,0:T(8,128)S(1)}, f32[512,512]{1,0:T(8,128)S(1)}, u32[]{:S(2)}, u32[]{:S(2)}) collective-permute-start(f32[512,512]{1,0:T(8,128)S(1)} %add.3.here), channel_id=1, source_target_pairs={{0,48},{1,17},{2,50},{3,19},{4,52},{5,21},{6,54},{7,23},{8,56},{9,... | collective-permute-start | bytes 3145736 | tf_op jit(solution)/shard_map/ppermute | solution.py:54
  99.6 2.1 %collective-permute-start.6 = (f32[512,512]{1,0:T(8,128)S(1)}, f32[512,512]{1,0:T(8,128)}, u32[]{:S(2)}, u32[]{:S(2)}) collective-permute-start(f32[512,512]{1,0:T(8,128)S(1)} %add.3.here), channel_id=1, source_target_pairs={{0,16},{1,49},{2,18},{3,51},{4,20},{5,53},{6,22},{7,55},{8,24},{9,... | collective-permute-start | bytes 3145736 | tf_op jit(solution)/shard_map/ppermute | solution.py:54
  101.7 0.6 collective-permute-start.20
  102.4 8.0 %collective-permute-done.12.rest_6_ = f32[2048,128]{1,0:T(8,128)} collective-permute-done((f32[2048,128]{1,0:T(8,128)}, f32[2048,128]{1,0:T(8,128)}, u32[]{:S(2)}, u32[]{:S(2)}) %collective-permute-start.12) | collective-permute-done | bytes 1048608 | tf_op jit(solution)/shard_map/ppermute | solution.py:38
  110.4 1.3 collective-permute-start.17
  111.8 10.1 %collective-permute-done.7.second = f32[512,512]{1,0:T(8,128)S(1)} collective-permute-done((f32[512,512]{1,0:T(8,128)S(1)}, f32[512,512]{1,0:T(8,128)S(1)}, u32[]{:S(2)}, u32[]{:S(2)}) %collective-permute-start.7) | collective-permute-done | bytes 1048608 | tf_op jit(solution)/shard_map/ppermute | solution.py:54
  121.9 3.2 %collective-permute-start.13 = (f32[2048,128]{1,0:T(8,128)}, f32[2048,128]{1,0:T(8,128)}, u32[]{:S(2)}, u32[]{:S(2)}) collective-permute-start(f32[2048,128]{1,0:T(8,128)} %collective-permute-done.12.rest_6_), channel_id=1, source_target_pairs={{0,1},{1,0},{2,3},{3,2},{4,5},{5,4},{6,7},{7,6},{8,9},{9,8},{10,11... | collective-permute-start | bytes 3145736 | tf_op jit(solution)/shard_map/ppermute | solution.py:38
  125.1 3.4 %collective-permute-start.8 = (f32[512,512]{1,0:T(8,128)}, f32[512,512]{1,0:T(8,128)}, u32[]{:S(2)}, u32[]{:S(2)}) collective-permute-start(f32[512,512]{1,0:T(8,128)} %collective-permute-done.6.first), channel_id=1, source_target_pairs={{0,16},{1,49},{2,18},{3,51},{4,20},{5,53},{6,22},{7,55},{8,24},{9,... | collective-permute-start | bytes 3145736 | tf_op jit(solution)/shard_map/ppermute | solution.py:54
  128.9 11.6 %collective-permute-done.8.far = f32[512,512]{1,0:T(8,128)} collective-permute-done((f32[512,512]{1,0:T(8,128)}, f32[512,512]{1,0:T(8,128)}, u32[]{:S(2)}, u32[]{:S(2)}) %collective-permute-start.8) | collective-permute-done | bytes 1048608 | tf_op jit(solution)/shard_map/ppermute | solution.py:54
  140.6 19.2 %product.1 = f32[2048,512]{1,0:T(8,128)} custom-call(s32[16,4]{1,0:T(8,128)S(1)} %copy.8.mask, f32[512,512]{1,0:T(8,128)S(1)} %add.3.here, f32[512,512]{1,0:T(8,128)} %collective-permute-done.6.first, f32[512,512]{1,0:T(8,128)S(1)} %collective-permute-done.7.second, f32[512,512]{1,0:T(8,128)} %collective-permute-done.8.far, f32[2048,128]{1,0:T(8,128)S(1)} %copy-done, ...), custom_call_target="tpu_custom_call" | custom-call | tf_op jit(solution)/shard_map/product/pallas_call | solution.py:291
  (35 shorter events, 1.4 us)
Async XLA Ops:
  3.5 35.4 %all-to-all-start = ((f32[16,264,128]{2,1,0:T(8,128)}), f32[16,264,128]{2,1,0:T(8,128)S(1)}, u32[]{:S(2)}, u32[]{:S(2)}) async-start(f32[16,264,128]{2,1,0:T(8,128)} %pack_a.1), calls=%async_computation | async-start | bytes 4325376 | tf_op jit(solution)/shard_map/all_to_all | solution.py:311
  13.8 32.8 %collective-permute-start = (f32[1056,128]{1,0:T(8,128)}, f32[1056,128]{1,0:T(8,128)}, u32[]{:S(2)}, u32[]{:S(2)}) collective-permute-start(f32[1056,128]{1,0:T(8,128)} %get-tuple-element.15), channel_id=1, source_target_pairs={{0,16},{16,32},{32,48},{48,0},{64,80},{80,96},{96,112},{112,64},{1... | collective-permute-start | bytes 1622024 | tf_op jit(solution)/shard_map/ppermute | solution.py:45
  15.5 31.6 %collective-permute-start.1 = (f32[1056,128]{1,0:T(8,128)}, f32[1056,128]{1,0:T(8,128)}, u32[]{:S(2)}, u32[]{:S(2)}) collective-permute-start(f32[1056,128]{1,0:T(8,128)} %get-tuple-element.16), channel_id=1, source_target_pairs={{0,32},{16,48},{32,0},{48,16},{64,96},{80,112},{96,64},{112,80},{1... | collective-permute-start | bytes 1622024 | tf_op jit(solution)/shard_map/ppermute | solution.py:45
  19.0 28.1 %collective-permute-start.2 = (f32[1056,128]{1,0:T(8,128)}, f32[1056,128]{1,0:T(8,128)}, u32[]{:S(2)}, u32[]{:S(2)}) collective-permute-start(f32[1056,128]{1,0:T(8,128)} %get-tuple-element.17), channel_id=1, source_target_pairs={{0,48},{16,0},{32,16},{48,32},{64,112},{80,64},{96,80},{112,96},{1... | collective-permute-start | bytes 1622024 | tf_op jit(solution)/shard_map/ppermute | solution.py:45
  38.9 1.3 copy-start.1
  43.5 10.6 %copy-start = (f32[2048,128]{1,0:T(8,128)S(1)}, f32[2048,128]{1,0:T(8,128)}, u32[]{:S(2)}) copy-start(f32[2048,128]{1,0:T(8,128)} %unpack_a.1.rest_0_) | copy-start | bytes 3145732
  43.5 24.4 %collective-permute-start.14 = (f32[2048,128]{1,0:T(8,128)}, f32[2048,128]{1,0:T(8,128)}, u32[]{:S(2)}, u32[]{:S(2)}) collective-permute-start(f32[2048,128]{1,0:T(8,128)} %unpack_a.1.rest_0_), channel_id=1, source_target_pairs={{0,8},{1,9},{2,10},{3,11},{4,12},{5,13},{6,14},{7,15},{8,0},{9,1},... | collective-permute-start | bytes 3145736 | tf_op jit(solution)/shard_map/ppermute | solution.py:38
  44.4 26.0 %collective-permute-start.5 = (f32[2048,128]{1,0:T(8,128)}, f32[2048,128]{1,0:T(8,128)}, u32[]{:S(2)}, u32[]{:S(2)}) collective-permute-start(f32[2048,128]{1,0:T(8,128)} %unpack_a.1.rest_0_), channel_id=1, source_target_pairs={{0,6},{1,3},{2,0},{3,5},{4,2},{5,7},{6,4},{7,1},{8,14},{9,11},{10,... | collective-permute-start | bytes 3145736 | tf_op jit(solution)/shard_map/ppermute | solution.py:38
  46.6 25.1 %collective-permute-start.4 = (f32[2048,128]{1,0:T(8,128)}, f32[2048,128]{1,0:T(8,128)}, u32[]{:S(2)}, u32[]{:S(2)}) collective-permute-start(f32[2048,128]{1,0:T(8,128)} %unpack_a.1.rest_0_), channel_id=1, source_target_pairs={{0,2},{1,7},{2,4},{3,1},{4,6},{5,3},{6,0},{7,5},{8,10},{9,15},{10,... | collective-permute-start | bytes 3145736 | tf_op jit(solution)/shard_map/ppermute | solution.py:38
  51.2 77.7 %copy-start.6 = (s32[16,4]{0,1:T(4,128)S(1)}, s32[16,4]{0,1:T(4,128)}, u32[]{:S(2)}) copy-start(s32[16,4]{0,1:T(4,128)} %param.15) | copy-start | bytes 772
  51.2 40.9 %collective-permute-start.3 = (f32[512,512]{1,0:T(8,128)}, f32[512,512]{1,0:T(8,128)S(1)}, u32[]{:S(2)}, u32[]{:S(2)}) collective-permute-start(f32[512,512]{1,0:T(8,128)} %unpack_b.1), channel_id=1, source_target_pairs={{0,64},{16,80},{32,96},{48,112},{64,0},{80,16},{96,32},{112,48},{1... | collective-permute-start | bytes 3145736 | tf_op jit(solution)/shard_map/ppermute | solution.py:45
  54.1 41.3 %collective-permute-start.9 = (f32[2048,128]{1,0:T(8,128)S(1)}, f32[2048,128]{1,0:T(8,128)S(1)}, u32[]{:S(2)}, u32[]{:S(2)}) collective-permute-start(f32[2048,128]{1,0:T(8,128)S(1)} %copy-done), channel_id=1, source_target_pairs={{0,1},{1,0},{2,3},{3,2},{4,5},{5,4},{6,7},{7,6},{8,9},{9,8},{10,11... | collective-permute-start | bytes 3145736 | tf_op jit(solution)/shard_map/ppermute | solution.py:38
  67.8 27.9 %collective-permute-start.18 = (f32[2048,128]{1,0:T(8,128)}, f32[2048,128]{1,0:T(8,128)}, u32[]{:S(2)}, u32[]{:S(2)}) collective-permute-start(f32[2048,128]{1,0:T(8,128)} %collective-permute-done.14.rest_8_), channel_id=1, source_target_pairs={{0,6},{1,3},{2,0},{3,5},{4,2},{5,7},{6,4},{7,1},{8,14},{9,11},{10,... | collective-permute-start | bytes 3145736 | tf_op jit(solution)/shard_map/ppermute | solution.py:38
  71.7 26.2 %collective-permute-start.16 = (f32[2048,128]{1,0:T(8,128)}, f32[2048,128]{1,0:T(8,128)}, u32[]{:S(2)}, u32[]{:S(2)}) collective-permute-start(f32[2048,128]{1,0:T(8,128)} %collective-permute-done.14.rest_8_), channel_id=1, source_target_pairs={{0,2},{1,7},{2,4},{3,1},{4,6},{5,3},{6,0},{7,5},{8,10},{9,15},{10,... | collective-permute-start | bytes 3145736 | tf_op jit(solution)/shard_map/ppermute | solution.py:38
  73.0 26.6 %collective-permute-start.15 = (f32[2048,128]{1,0:T(8,128)}, f32[2048,128]{1,0:T(8,128)S(1)}, u32[]{:S(2)}, u32[]{:S(2)}) collective-permute-start(f32[2048,128]{1,0:T(8,128)} %collective-permute-done.14.rest_8_), channel_id=1, source_target_pairs={{0,1},{1,0},{2,3},{3,2},{4,5},{5,4},{6,7},{7,6},{8,9},{9,8},{10,11... | collective-permute-start | bytes 3145736 | tf_op jit(solution)/shard_map/ppermute | solution.py:38
  92.1 9.6 %collective-permute-start.11 = (f32[2048,128]{1,0:T(8,128)}, f32[2048,128]{1,0:T(8,128)S(1)}, u32[]{:S(2)}, u32[]{:S(2)}) collective-permute-start(f32[2048,128]{1,0:T(8,128)} %collective-permute-done.5.rest_4_), channel_id=1, source_target_pairs={{0,1},{1,0},{2,3},{3,2},{4,5},{5,4},{6,7},{7,6},{8,9},{9,8},{10,11... | collective-permute-start | bytes 3145736 | tf_op jit(solution)/shard_map/ppermute | solution.py:38
  95.3 33.2 %copy-start.2 = (f32[2048,128]{1,0:T(8,128)}, f32[2048,128]{1,0:T(8,128)S(1)}, u32[]{:S(2)}) copy-start(f32[2048,128]{1,0:T(8,128)S(1)} %collective-permute-done.9.rest_1_) | copy-start | bytes 3145732
  95.3 15.1 %collective-permute-start.12 = (f32[2048,128]{1,0:T(8,128)}, f32[2048,128]{1,0:T(8,128)}, u32[]{:S(2)}, u32[]{:S(2)}) collective-permute-start(f32[2048,128]{1,0:T(8,128)} %collective-permute-done.4.rest_2_), channel_id=1, source_target_pairs={{0,2},{1,7},{2,4},{3,1},{4,6},{5,3},{6,0},{7,5},{8,10},{9,15},{10,... | collective-permute-start | bytes 3145736 | tf_op jit(solution)/shard_map/ppermute | solution.py:38
  95.8 15.9 %collective-permute-start.10 = (f32[2048,128]{1,0:T(8,128)}, f32[2048,128]{1,0:T(8,128)S(1)}, u32[]{:S(2)}, u32[]{:S(2)}) collective-permute-start(f32[2048,128]{1,0:T(8,128)} %collective-permute-done.4.rest_2_), channel_id=1, source_target_pairs={{0,1},{1,0},{2,3},{3,2},{4,5},{5,4},{6,7},{7,6},{8,9},{9,8},{10,11... | collective-permute-start | bytes 3145736 | tf_op jit(solution)/shard_map/ppermute | solution.py:38
  97.9 24.0 %collective-permute-start.7 = (f32[512,512]{1,0:T(8,128)S(1)}, f32[512,512]{1,0:T(8,128)S(1)}, u32[]{:S(2)}, u32[]{:S(2)}) collective-permute-start(f32[512,512]{1,0:T(8,128)S(1)} %add.3.here), channel_id=1, source_target_pairs={{0,48},{1,17},{2,50},{3,19},{4,52},{5,21},{6,54},{7,23},{8,56},{9,... | collective-permute-start | bytes 3145736 | tf_op jit(solution)/shard_map/ppermute | solution.py:54
  99.6 28.9 %copy-start.3 = (f32[2048,128]{1,0:T(8,128)}, f32[2048,128]{1,0:T(8,128)S(1)}, u32[]{:S(2)}) copy-start(f32[2048,128]{1,0:T(8,128)S(1)} %collective-permute-done.15.rest_9_) | copy-start | bytes 3145732
  99.6 25.5 %collective-permute-start.6 = (f32[512,512]{1,0:T(8,128)S(1)}, f32[512,512]{1,0:T(8,128)}, u32[]{:S(2)}, u32[]{:S(2)}) collective-permute-start(f32[512,512]{1,0:T(8,128)S(1)} %add.3.here), channel_id=1, source_target_pairs={{0,16},{1,49},{2,18},{3,51},{4,20},{5,53},{6,22},{7,55},{8,24},{9,... | collective-permute-start | bytes 3145736 | tf_op jit(solution)/shard_map/ppermute | solution.py:54
  101.7 26.8 %copy-start.4 = (f32[2048,128]{1,0:T(8,128)}, f32[2048,128]{1,0:T(8,128)S(1)}, u32[]{:S(2)}) copy-start(f32[2048,128]{1,0:T(8,128)S(1)} %collective-permute-done.11.rest_5_) | copy-start | bytes 3145732
  101.7 26.8 %collective-permute-start.20 = (f32[2048,128]{1,0:T(8,128)}, f32[2048,128]{1,0:T(8,128)}, u32[]{:S(2)}, u32[]{:S(2)}) collective-permute-start(f32[2048,128]{1,0:T(8,128)} %collective-permute-done.16.rest_10_), channel_id=1, source_target_pairs={{0,2},{1,7},{2,4},{3,1},{4,6},{5,3},{6,0},{7,5},{8,10},{9,15},{10,... | collective-permute-start | bytes 3145736 | tf_op jit(solution)/shard_map/ppermute | solution.py:38
  110.4 18.5 %collective-permute-start.17 = (f32[2048,128]{1,0:T(8,128)}, f32[2048,128]{1,0:T(8,128)}, u32[]{:S(2)}, u32[]{:S(2)}) collective-permute-start(f32[2048,128]{1,0:T(8,128)} %collective-permute-done.16.rest_10_), channel_id=1, source_target_pairs={{0,1},{1,0},{2,3},{3,2},{4,5},{5,4},{6,7},{7,6},{8,9},{9,8},{10,11... | collective-permute-start | bytes 3145736 | tf_op jit(solution)/shard_map/ppermute | solution.py:38
  111.7 16.8 %copy-start.5 = (f32[2048,128]{1,0:T(8,128)}, f32[2048,128]{1,0:T(8,128)S(1)}, u32[]{:S(2)}) copy-start(f32[2048,128]{1,0:T(8,128)S(1)} %collective-permute-done.10.rest_3_) | copy-start | bytes 3145732
  111.7 17.2 %collective-permute-start.19 = (f32[2048,128]{1,0:T(8,128)}, f32[2048,128]{1,0:T(8,128)}, u32[]{:S(2)}, u32[]{:S(2)}) collective-permute-start(f32[2048,128]{1,0:T(8,128)} %collective-permute-done.18.rest_12_), channel_id=1, source_target_pairs={{0,1},{1,0},{2,3},{3,2},{4,5},{5,4},{6,7},{7,6},{8,9},{9,8},{10,11... | collective-permute-start | bytes 3145736 | tf_op jit(solution)/shard_map/ppermute | solution.py:38
  121.9 7.0 %collective-permute-start.13 = (f32[2048,128]{1,0:T(8,128)}, f32[2048,128]{1,0:T(8,128)}, u32[]{:S(2)}, u32[]{:S(2)}) collective-permute-start(f32[2048,128]{1,0:T(8,128)} %collective-permute-done.12.rest_6_), channel_id=1, source_target_pairs={{0,1},{1,0},{2,3},{3,2},{4,5},{5,4},{6,7},{7,6},{8,9},{9,8},{10,11... | collective-permute-start | bytes 3145736 | tf_op jit(solution)/shard_map/ppermute | solution.py:38
  125.1 15.5 %collective-permute-start.8 = (f32[512,512]{1,0:T(8,128)}, f32[512,512]{1,0:T(8,128)}, u32[]{:S(2)}, u32[]{:S(2)}) collective-permute-start(f32[512,512]{1,0:T(8,128)} %collective-permute-done.6.first), channel_id=1, source_target_pairs={{0,16},{1,49},{2,18},{3,51},{4,20},{5,53},{6,22},{7,55},{8,24},{9,... | collective-permute-start | bytes 3145736 | tf_op jit(solution)/shard_map/ppermute | solution.py:54
  128.6 12.0 %collective-permute-start.21 = (f32[2048,128]{1,0:T(8,128)}, f32[2048,128]{1,0:T(8,128)}, u32[]{:S(2)}, u32[]{:S(2)}) collective-permute-start(f32[2048,128]{1,0:T(8,128)} %collective-permute-done.20.rest_14_), channel_id=1, source_target_pairs={{0,1},{1,0},{2,3},{3,2},{4,5},{5,4},{6,7},{7,6},{8,9},{9,8},{10,11... | collective-permute-start | bytes 3145736 | tf_op jit(solution)/shard_map/ppermute | solution.py:38

commit v4 on v3

--- a/solution.py
+++ b/solution.py
@@ -251,59 +251,88 @@
 TM = 512
 
 
-def product_kernel(mask, here, first, second, far, *rest):
-    pieces, (out, panel, stack, sems) = rest[:KB], rest[KB:]
-    tile = pl.program_id(0)
+def product_kernel(last, mask, *refs):
+    refs = list(refs)
+    b_pieces = [refs.pop(0) for _ in range(1 if last else NZ - 1)]
+    pieces = [refs.pop(0) for _ in range(KB)]
+    before = refs.pop(0) if last else None
+    out, rows, panel, stack, a_sems, b_sems = refs
+    tile, tiles = pl.program_id(0), pl.num_programs(0)
+    depth = len(b_pieces) * KZ * BS
+    z_now, step = place()[0], place()[4]
+
+    def fetch(at, wait):
+        buffer = lax.rem(at, 2)
+        for piece, k in zip(pieces, k_order()):
+            hop = lax.rem((z_now - lax.div(k, KZ)) * step + 2 * NZ, NZ)
+            slot = lax.rem(k, KZ) + (0 if last else KZ * jnp.minimum(hop, 2))
+            copy = pltpu.make_async_copy(
+                piece.at[pl.ds(pl.multiple_of(at * TM, TM), TM)],
+                rows.at[buffer, :, pl.ds(pl.multiple_of(slot * BS, BS), BS)],
+                a_sems.at[buffer, slot],
+            )
+            pl.when(hop == 2 if last else hop != 2)(copy.wait if wait else copy.start)
 
     @pl.when(tile == 0)
     def _():
-        z_now, step = place()[0], place()[4]
-        jobs = []
-        for p, k in enumerate(k_order()):
-            hop = lax.rem((z_now - lax.div(k, KZ)) * step + 2 * NZ, NZ)
-            row = pl.multiple_of(lax.rem(k, KZ) * BS, BS)
-            for want, source in ((0, here), (1, first), (2, far), (3, second)):
-                copy = pltpu.make_async_copy(
-                    source.at[pl.ds(row, BS)], panel.at[pl.ds(p * BS, BS)], sems.at[p]
-                )
-                pl.when(hop == want)(copy.start)
-            jobs.append(copy)
-        for p, job in enumerate(jobs):
+        jobs = [
+            pltpu.make_async_copy(piece, panel.at[pl.ds(i * KZ * BS, KZ * BS)], b_sems.at[i])
+            for i, piece in enumerate(b_pieces)
+        ]
+        for job in jobs:
+            job.start()
+        fetch(tile, False)
+        fetch(tile + 1, False)
+        for job in jobs:
             job.wait()
-            high, low = split(panel[pl.ds(p * BS, BS), :])
-            stack[pl.ds(p * BS, BS), :] = high
-            stack[pl.ds((KB + p) * BS, BS), :] = low
-
-    high, low = split(jnp.concatenate([ref[...] for ref in pieces], axis=1))
+        high, low = split(panel[...])
+        stack[pl.ds(0, depth), :] = high
+        stack[pl.ds(depth, depth), :] = low
+
+    fetch(tile, True)
+    high, low = split(rows[lax.rem(tile, 2)])
     total = jnp.dot(
         jnp.concatenate([high, high], axis=1), stack[...], preferred_element_type=F32
     )
-    total += jnp.dot(low, stack[pl.ds(0, KB * BS), :], preferred_element_type=F32)
-    for r in range(TM // BS):
-        for c in range(CB):
-            keep = mask[tile * (TM // BS) + r, c].astype(F32)
-            piece = total[r * BS : (r + 1) * BS, c * BS : (c + 1) * BS]
-            out[pl.ds(r * BS, BS), pl.ds(c * BS, BS)] = piece * keep
-
-
-def product(mask, b_pieces, a_pieces):
-    rows, cols = RB * BS, CB * BS
+    total += jnp.dot(low, stack[pl.ds(0, depth), :], preferred_element_type=F32)
+    if last:
+        total += before[...]
+        for r in range(TM // BS):
+            for c in range(CB):
+                keep = mask[tile * (TM // BS) + r, c].astype(F32)
+                piece = total[r * BS : (r + 1) * BS, c * BS : (c + 1) * BS]
+                out[pl.ds(r * BS, BS), pl.ds(c * BS, BS)] = piece * keep
+    else:
+        out[...] = total
+    pl.when(tile + 2 < tiles)(lambda: fetch(tile + 2, False))
+
+
+def product(mask, b_pieces, a_pieces, before=None):
+    height, cols = RB * BS, CB * BS
+    depth = len(b_pieces) * KZ * BS
+    c_spec = pl.BlockSpec((TM, cols), lambda t: (t, 0))
+    last = before is not None
     return pl.pallas_call(
-        product_kernel,
-        grid=(rows // TM,),
-        out_shape=jax.ShapeDtypeStruct((rows, cols), F32),
-        in_specs=[SMEM]
-        + [ANY] * len(b_pieces)
-        + [pl.BlockSpec((TM, BS), lambda t: (t, 0))] * len(a_pieces),
-        out_specs=pl.BlockSpec((TM, cols), lambda t: (t, 0)),
+        functools.partial(product_kernel, last),
+        grid=(height // TM,),
+        out_shape=jax.ShapeDtypeStruct((height, cols), F32),
+        in_specs=[SMEM] + [HBM] * (len(b_pieces) + KB) + [c_spec] * last,
+        out_specs=c_spec,
         scratch_shapes=[
-            pltpu.VMEM((KB * BS, cols), F32),
-            pltpu.VMEM((2 * KB * BS, cols), jnp.bfloat16),
-            pltpu.SemaphoreType.DMA((KB,)),
+            pltpu.VMEM((2, TM, depth), F32),
+            pltpu.VMEM((depth, cols), F32),
+            pltpu.VMEM((2 * depth, cols), jnp.bfloat16),
+            pltpu.SemaphoreType.DMA((2, depth // BS)),
+            pltpu.SemaphoreType.DMA((len(b_pieces),)),
         ],
-        compiler_params=pltpu.CompilerParams(vmem_limit_bytes=48 << 20),
+        compiler_params=pltpu.CompilerParams(vmem_limit_bytes=58 << 20),
+        cost_estimate=pl.CostEstimate(
+            flops=6 * height * cols * depth,
+            bytes_accessed=4 * (height * depth + depth * cols + 2 * height * cols),
+            transcendentals=0,
+        ),
         name="product",
-    )(mask, *b_pieces, *a_pieces)
+    )(mask, *b_pieces, *a_pieces, *([before] if last else []))
 
 
 def per_device(a_blocks, a_rows, a_cols, a_counts, b_blocks, b_rows, b_cols, b_counts, out_mask):
@@ -323,21 +352,50 @@
     def hop(value, step):
         return col_shift(value, dx=step, by_core=True)
 
-    own_first, own_second, other = hop(own, 1), hop(own, -1), col_shift(own, dy=1)
-    own_first, own_second = joined((own_first, own_second))
-    own_far = hop(own_first, 1)
-    b_here = b_part + after(row_shift(b_part, dy=1), own_first)
-    b_first, b_second = row_shift_by_core(b_here, 1), row_shift_by_core(b_here, -1)
-    b_far = row_shift_by_core(b_first, 1)
-    other_first, other_second = hop(other, 1), hop(other, -1)
-    other_far = hop(other_first, 1)
-
-    a_all = []
-    for value in (own, own_first, own_second, own_far):
-        a_all += [value, swap(value)]
-    for value in (other, other_first, other_second, other_far):
-        a_all += [value, swap(value)]
-    return product(out_mask, (b_here, b_first, b_second, b_far), a_all)
+    with jax.named_scope("t_F"):
+        v_F = hop(own, 1)
+    with jax.named_scope("t_S"):
+        v_S = row_shift(b_part, dy=1)
+    with jax.named_scope("t_G"):
+        v_G = hop(own, -1)
+    with jax.named_scope("t_H"):
+        v_H = hop(after(v_F, v_G), 1)
+    with jax.named_scope("t_cown"):
+        v_cown = swap(after(own, v_G))
+    with jax.named_scope("t_Y"):
+        v_Y = col_shift(own, dy=1)
+    with jax.named_scope("t_cF"):
+        v_cF = swap(v_F)
+    with jax.named_scope("t_cY"):
+        v_cY = swap(after(v_Y, v_G))
+    with jax.named_scope("t_cH"):
+        v_cH = swap(v_H)
+    with jax.named_scope("t_cG"):
+        v_cG = swap(v_G)
+    with jax.named_scope("t_YF"):
+        v_YF = hop(after(v_Y, v_G), 1)
+    with jax.named_scope("t_YG"):
+        v_YG = hop(v_Y, -1)
+    with jax.named_scope("t_cYF"):
+        v_cYF = swap(after(v_YF, v_cown))
+    with jax.named_scope("t_cYG"):
+        v_cYG = swap(v_YG)
+    v_b_here = b_part + after(v_S, v_F)
+    with jax.named_scope("t_YH"):
+        v_YH = hop(after(v_YF, v_YF), 1)
+    with jax.named_scope("t_bG"):
+        v_bG = row_shift_by_core(v_b_here, -1)
+    with jax.named_scope("t_bF"):
+        v_bF = row_shift_by_core(v_b_here, 1)
+    with jax.named_scope("t_bH"):
+        v_bH = row_shift_by_core(after(v_bF, v_G), 1)
+    with jax.named_scope("t_cYH"):
+        v_cYH = swap(v_YH)
+    b_all = (v_b_here, v_bF, v_bG, v_bH)
+    a_all = [own, v_cown, v_F, v_cF, v_G, v_cG, v_H, v_cH]
+    a_all += [v_Y, v_cY, v_YF, v_cYF, v_YG, v_cYG, v_YH, v_cYH]
+    total = product(out_mask, b_all[:3], a_all)
+    return product(out_mask, b_all[3:], a_all, before=total)
 
 
 def solution(mesh):

time: 161 us -> 159 us (0.988)
  waiting for transfers between devices: 82.3 us -> 72.4 us
  Pallas kernels: 33.4 us -> 43 us
  starting transfers between devices: 41 us -> 37.6 us
    pallas_call x1 -> x2, Pallas kernels: 19.2 us -> 28.1 us  [product(): pl.pallas_call(functools.partial(product_kernel, last), grid=(height // T...]
    ppermute x3, waiting for transfers between devices: 21.7 us -> 13 us  [row_shift_by_core(): return lax.ppermute(value, ('row', 'col'), route)]
    ppermute x15, starting transfers between devices: 18.4 us -> 16.7 us  [col_shift(): return lax.ppermute(value, 'col', route)]
  transfers between devices with their start and end apart: 23 -> 23, of which waited for: 7 -> 6; matrix products, arithmetic and copies ran while one was open for 1% -> 2% of each run, Pallas kernels for 7% -> 18%
where the time goes in v4:
time: 159 us; the launch traced here: 158 us
  waiting for transfers between devices  72.4 us (46%)
  Pallas kernels  43 us (27%)
  starting transfers between devices  37.6 us (24%)
  local copies, waits for them, and re-layouts  3.02 us (2%)
  other arithmetic  1.74 us (1%)
    pallas_call x2, Pallas kernels, product(): pl.pallas_call(functools.partial(product_kernel, last), grid=(height // T...  28.1 us
    ppermute x15, waiting for transfers between devices, col_shift(): return lax.ppermute(value, 'col', route)  21.8 us
    all_to_all x1, waiting for transfers between devices, per_device(): lax.all_to_all(a_send, 'col', split_axis=0, concat_axis=0, tiled=True)  19.4 us
    ppermute x4, waiting for transfers between devices, row_shift(): return lax.ppermute(value, 'row', route)  18.2 us
    ppermute x15, starting transfers between devices, col_shift(): return lax.ppermute(value, 'col', route)  16.7 us
    ppermute x3, waiting for transfers between devices, row_shift_by_core(): return lax.ppermute(value, ('row', 'col'), route)  13 us
    ppermute x4, starting transfers between devices, row_shift(): return lax.ppermute(value, 'row', route)  8.01 us
    all_to_all x1, starting transfers between devices, per_device(): lax.all_to_all(a_send, 'col', split_axis=0, concat_axis=0, tiled=True)  6.64 us
  transfers between devices with their start and end apart: 23, of which 6 were waited for; matrix products, arithmetic and copies ran while one was open for 2% of the time, Pallas kernels for 18%

profile of v4, /device:TPU:1, one launch (start us, length us, event | category | flops | bytes accessed | tf_op | source)
XLA Modules:
  0.0 158.1 jit_solution(2112795760358659005)
XLA Ops:
  0.0 3.7 %pack_a.1 = f32[16,264,128]{2,1,0:T(8,128)} custom-call(s32[16]{0:T(128)} %bitcast.8, s32[32]{0:T(128)} %bitcast.9, f32[32,128,128]{2,1,0:T(8,128)} %bitcast.6), custom_call_target="tpu_custom_call" | custom-call | tf_op jit(solution)/shard_map/pack_a/pallas_call | solution.py:101
  3.7 6.6 %all-to-all-start = ((f32[16,264,128]{2,1,0:T(8,128)}), f32[16,264,128]{2,1,0:T(8,128)S(1)}, u32[]{:S(2)}, u32[]{:S(2)}) async-start(f32[16,264,128]{2,1,0:T(8,128)} %pack_a.1), calls=%async_computation | async-start | bytes 4325376 | tf_op jit(solution)/shard_map/all_to_all | solution.py:340
  10.4 3.6 %pack_b.1 = (f32[1056,128]{1,0:T(8,128)}, f32[1056,128]{1,0:T(8,128)}, f32[1056,128]{1,0:T(8,128)}, f32[1056,128]{1,0:T(8,128)}) custom-call(s32[16]{0:T(128)} %bitcast.10, s32[32]{0:T(128)} %bitcast.11, f32[32,128,128]{2,1,0:T(8,128)} %bitcast.7), custom_call_target="tpu_custom_call" | custom-call | tf_op jit(solution)/shard_map/pack_b/pallas_call | solution.py:140
  13.9 1.6 %collective-permute-start = (f32[1056,128]{1,0:T(8,128)}, f32[1056,128]{1,0:T(8,128)}, u32[]{:S(2)}, u32[]{:S(2)}) collective-permute-start(f32[1056,128]{1,0:T(8,128)} %get-tuple-element.19), channel_id=1, source_target_pairs={{0,16},{16,32},{32,48},{48,0},{64,80},{80,96},{96,112},{112,64},{1... | collective-permute-start | bytes 1622024 | tf_op jit(solution)/shard_map/ppermute | solution.py:45
  15.6 3.2 %collective-permute-start.1 = (f32[1056,128]{1,0:T(8,128)}, f32[1056,128]{1,0:T(8,128)}, u32[]{:S(2)}, u32[]{:S(2)}) collective-permute-start(f32[1056,128]{1,0:T(8,128)} %get-tuple-element.20), channel_id=1, source_target_pairs={{0,32},{16,48},{32,0},{48,16},{64,96},{80,112},{96,64},{112,80},{1... | collective-permute-start | bytes 1622024 | tf_op jit(solution)/shard_map/ppermute | solution.py:45
  18.8 0.8 collective-permute-start.2
  19.5 19.4 %all-to-all-done.got = f32[16,264,128]{2,1,0:T(8,128)S(1)} async-done(((f32[16,264,128]{2,1,0:T(8,128)}), f32[16,264,128]{2,1,0:T(8,128)S(1)}, u32[]{:S(2)}, u32[]{:S(2)}) %all-to-all-start) | async-done | bytes 2162720 | tf_op jit(solution)/shard_map/all_to_all | solution.py:340
  38.9 1.3 copy-done
  40.2 3.4 %unpack_a.1.refs_3_.refs_1_ = f32[2048,128]{1,0:T(8,128)} custom-call(f32[16,264,128]{2,1,0:T(8,128)} %copy-done), custom_call_target="tpu_custom_call" | custom-call | tf_op jit(solution)/shard_map/unpack_a/pallas_call | solution.py:174
  43.6 0.8 collective-permute-start.13
  44.4 2.2 %collective-permute-start.6 = (f32[2048,128]{1,0:T(8,128)}, f32[2048,128]{1,0:T(8,128)S(1)}, u32[]{:S(2)}, u32[]{:S(2)}) collective-permute-start(f32[2048,128]{1,0:T(8,128)} %unpack_a.1.refs_3_.refs_1_), channel_id=1, source_target_pairs={{0,6},{1,3},{2,0},{3,5},{4,2},{5,7},{6,4},{7,1},{8,14},{9,11},{10,... | collective-permute-start | bytes 3145736 | tf_op jit(solution)/shard_map/t_G/ppermute | solution.py:38
  46.7 4.3 %unpack_b.1 = f32[512,512]{1,0:T(8,128)} custom-call(f32[1056,128]{1,0:T(8,128)} %get-tuple-element.18.refs_0_, f32[1056,128]{1,0:T(8,128)} %collective-permute-done.refs_1_, f32[1056,128]{1,0:T(8,128)} %collective-permute-done.1.refs_2_, f32[1056,128]{1,0:T(8,128)} %collective-permute-done.2.refs_3_), custom_call_target="tpu_custom_call" | custom-call | tf_op jit(solution)/shard_map/unpack_b/pallas_call | solution.py:220
  50.9 2.4 %collective-permute-start.3 = (f32[512,512]{1,0:T(8,128)}, f32[512,512]{1,0:T(8,128)S(1)}, u32[]{:S(2)}, u32[]{:S(2)}) collective-permute-start(f32[512,512]{1,0:T(8,128)} %unpack_b.1), channel_id=1, source_target_pairs={{0,64},{16,80},{32,96},{48,112},{64,0},{80,16},{96,32},{112,48},{1... | collective-permute-start | bytes 3145736 | tf_op jit(solution)/shard_map/t_S/ppermute | solution.py:45
  53.4 0.6 collective-permute-start.4
  54.0 14.0 %collective-permute-done.13.refs_11_.refs_9_ = f32[2048,128]{1,0:T(8,128)S(1)} collective-permute-done((f32[2048,128]{1,0:T(8,128)}, f32[2048,128]{1,0:T(8,128)S(1)}, u32[]{:S(2)}, u32[]{:S(2)}) %collective-permute-start.13) | collective-permute-done | bytes 1048608 | tf_op jit(solution)/shard_map/t_Y/ppermute | solution.py:38
  68.6 1.9 %collective-permute-start.17 = (f32[2048,128]{1,0:T(8,128)S(1)}, f32[2048,128]{1,0:T(8,128)}, u32[]{:S(2)}, u32[]{:S(2)}) collective-permute-start(f32[2048,128]{1,0:T(8,128)S(1)} %collective-permute-done.13.refs_11_.refs_9_), channel_id=1, source_target_pairs={{0,6},{1,3},{2,0},{3,5},{4,2},{5,7},{6,4},{7,1},{8,14},{9,11},{10,... | collective-permute-start | bytes 3145736 | tf_op jit(solution)/shard_map/t_YG/ppermute | solution.py:38
  70.5 3.4 %collective-permute-start.8 = (f32[2048,128]{1,0:T(8,128)S(1)}, f32[2048,128]{1,0:T(8,128)S(1)}, u32[]{:S(2)}, u32[]{:S(2)}) collective-permute-start(f32[2048,128]{1,0:T(8,128)S(1)} %copy-done.1), channel_id=1, source_target_pairs={{0,1},{1,0},{2,3},{3,2},{4,5},{5,4},{6,7},{7,6},{8,9},{9,8},{10,11... | collective-permute-start | bytes 3145736 | tf_op jit(solution)/shard_map/t_cown/ppermute | solution.py:38
  73.9 18.2 %collective-permute-done.3 = f32[512,512]{1,0:T(8,128)S(1)} collective-permute-done((f32[512,512]{1,0:T(8,128)}, f32[512,512]{1,0:T(8,128)S(1)}, u32[]{:S(2)}, u32[]{:S(2)}) %collective-permute-start.3) | collective-permute-done | bytes 1048608 | tf_op jit(solution)/shard_map/t_S/ppermute | solution.py:45
  92.1 1.7 %collective-permute-start.14 = (f32[2048,128]{1,0:T(8,128)S(1)}, f32[2048,128]{1,0:T(8,128)S(1)}, u32[]{:S(2)}, u32[]{:S(2)}) collective-permute-start(f32[2048,128]{1,0:T(8,128)S(1)} %collective-permute-done.13.refs_11_.refs_9_), channel_id=1, source_target_pairs={{0,1},{1,0},{2,3},{3,2},{4,5},{5,4},{6,7},{7,6},{8,9},{9,8},{10,11... | collective-permute-start | bytes 3145736 | tf_op jit(solution)/shard_map/t_cY/ppermute | solution.py:38
  93.9 1.7 %add.3.refs_0_ = f32[512,512]{1,0:T(8,128)S(1)} add(f32[512,512]{1,0:T(8,128)} %unpack_b.1, f32[512,512]{1,0:T(8,128)S(1)} %collective-permute-done.3) | non-fusion elementwise | flops 262144 | bytes 3145728 | tf_op jit(solution)/shard_map/add | solution.py:383
  96.1 2.2 %collective-permute-start.9 = (f32[2048,128]{1,0:T(8,128)S(1)}, f32[2048,128]{1,0:T(8,128)S(1)}, u32[]{:S(2)}, u32[]{:S(2)}) collective-permute-start(f32[2048,128]{1,0:T(8,128)S(1)} %collective-permute-done.4.refs_5_.refs_3_), channel_id=1, source_target_pairs={{0,1},{1,0},{2,3},{3,2},{4,5},{5,4},{6,7},{7,6},{8,9},{9,8},{10,11... | collective-permute-start | bytes 3145736 | tf_op jit(solution)/shard_map/t_cF/ppermute | solution.py:38
  98.3 3.7 %collective-permute-start.5 = (f32[512,512]{1,0:T(8,128)S(1)}, f32[512,512]{1,0:T(8,128)}, u32[]{:S(2)}, u32[]{:S(2)}) collective-permute-start(f32[512,512]{1,0:T(8,128)S(1)} %add.3.refs_0_), channel_id=1, source_target_pairs={{0,16},{1,49},{2,18},{3,51},{4,20},{5,53},{6,22},{7,55},{8,24},{9,... | collective-permute-start | bytes 3145736 | tf_op jit(solution)/shard_map/t_bF/ppermute | solution.py:54
  102.1 0.6 collective-permute-start.19
  102.8 7.7 %collective-permute-done.11.refs_9_.refs_7_ = f32[2048,128]{1,0:T(8,128)} collective-permute-done((f32[2048,128]{1,0:T(8,128)S(1)}, f32[2048,128]{1,0:T(8,128)}, u32[]{:S(2)}, u32[]{:S(2)}) %collective-permute-start.11) | collective-permute-done | bytes 1048608 | tf_op jit(solution)/shard_map/t_H/ppermute | solution.py:38
  110.5 1.5 collective-permute-start.16
  112.2 11.5 %collective-permute-done.5.refs_1_ = f32[512,512]{1,0:T(8,128)} collective-permute-done((f32[512,512]{1,0:T(8,128)S(1)}, f32[512,512]{1,0:T(8,128)}, u32[]{:S(2)}, u32[]{:S(2)}) %collective-permute-start.5) | collective-permute-done | bytes 1048608 | tf_op jit(solution)/shard_map/t_bF/ppermute | solution.py:54
  124.3 1.5 collective-permute-done.21.refs_2_
  125.8 1.0 copy-done.12
  126.7 2.4 %collective-permute-start.7 = (f32[512,512]{1,0:T(8,128)}, f32[512,512]{1,0:T(8,128)}, u32[]{:S(2)}, u32[]{:S(2)}) collective-permute-start(f32[512,512]{1,0:T(8,128)} %collective-permute-done.5.refs_1_), channel_id=1, source_target_pairs={{0,16},{1,49},{2,18},{3,51},{4,20},{5,53},{6,22},{7,55},{8,24},{9,... | collective-permute-start | bytes 3145736 | tf_op jit(solution)/shard_map/t_bH/ppermute | solution.py:54
  129.1 0.7 copy.9.mask
  129.9 17.9 %product.2.refs_17_ = f32[2048,512]{1,0:T(8,128)} custom-call(s32[16,4]{1,0:T(8,128)} %copy.9.mask, f32[512,512]{1,0:T(8,128)} %copy-done.9, f32[512,512]{1,0:T(8,128)} %collective-permute-done.5.refs_1_, f32[512,512]{1,0:T(8,128)} %copy-done.12, f32[2048,128]{1,0:T(8,128)} %unpack_a.1.refs_3_.refs_1_, f32[2048,128]{1,0:T(8,128)} %copy-done.5, ...), custom_call_target="tpu_custom_call" | custom-call | flops 9663676416 | bytes 24117248 | tf_op jit(solution)/shard_map/product/pallas_call | solution.py:315
  147.8 10.1 %product.3 = f32[2048,512]{1,0:T(8,128)} custom-call(s32[16,4]{1,0:T(8,128)} %copy.9.mask, f32[512,512]{1,0:T(8,128)} %collective-permute-done.7.refs_0_, f32[2048,128]{1,0:T(8,128)} %unpack_a.1.refs_3_.refs_1_, f32[2048,128]{1,0:T(8,128)} %copy-done.5, f32[2048,128]{1,0:T(8,128)} %copy-done.4, f32[2048,128]{1,0:T(8,128)} %copy-done.8, ...), custom_call_target="tpu_custom_call" | custom-call | flops 3221225472 | bytes 13631488 | tf_op jit(solution)/shard_map/product/pallas_call | solution.py:315
  (48 shorter events, 1.9 us)
Async XLA Ops:
  3.7 35.2 %all-to-all-start = ((f32[16,264,128]{2,1,0:T(8,128)}), f32[16,264,128]{2,1,0:T(8,128)S(1)}, u32[]{:S(2)}, u32[]{:S(2)}) async-start(f32[16,264,128]{2,1,0:T(8,128)} %pack_a.1), calls=%async_computation | async-start | bytes 4325376 | tf_op jit(solution)/shard_map/all_to_all | solution.py:340
  13.9 32.7 %collective-permute-start = (f32[1056,128]{1,0:T(8,128)}, f32[1056,128]{1,0:T(8,128)}, u32[]{:S(2)}, u32[]{:S(2)}) collective-permute-start(f32[1056,128]{1,0:T(8,128)} %get-tuple-element.19), channel_id=1, source_target_pairs={{0,16},{16,32},{32,48},{48,0},{64,80},{80,96},{96,112},{112,64},{1... | collective-permute-start | bytes 1622024 | tf_op jit(solution)/shard_map/ppermute | solution.py:45
  15.6 31.1 %collective-permute-start.1 = (f32[1056,128]{1,0:T(8,128)}, f32[1056,128]{1,0:T(8,128)}, u32[]{:S(2)}, u32[]{:S(2)}) collective-permute-start(f32[1056,128]{1,0:T(8,128)} %get-tuple-element.20), channel_id=1, source_target_pairs={{0,32},{16,48},{32,0},{48,16},{64,96},{80,112},{96,64},{112,80},{1... | collective-permute-start | bytes 1622024 | tf_op jit(solution)/shard_map/ppermute | solution.py:45
  18.8 27.9 %collective-permute-start.2 = (f32[1056,128]{1,0:T(8,128)}, f32[1056,128]{1,0:T(8,128)}, u32[]{:S(2)}, u32[]{:S(2)}) collective-permute-start(f32[1056,128]{1,0:T(8,128)} %get-tuple-element.21), channel_id=1, source_target_pairs={{0,48},{16,0},{32,16},{48,32},{64,112},{80,64},{96,80},{112,96},{1... | collective-permute-start | bytes 1622024 | tf_op jit(solution)/shard_map/ppermute | solution.py:45
  43.6 9.8 %copy-start.1 = (f32[2048,128]{1,0:T(8,128)S(1)}, f32[2048,128]{1,0:T(8,128)}, u32[]{:S(2)}) copy-start(f32[2048,128]{1,0:T(8,128)} %unpack_a.1.refs_3_.refs_1_) | copy-start | bytes 3145732
  43.6 24.4 %collective-permute-start.13 = (f32[2048,128]{1,0:T(8,128)}, f32[2048,128]{1,0:T(8,128)S(1)}, u32[]{:S(2)}, u32[]{:S(2)}) collective-permute-start(f32[2048,128]{1,0:T(8,128)} %unpack_a.1.refs_3_.refs_1_), channel_id=1, source_target_pairs={{0,8},{1,9},{2,10},{3,11},{4,12},{5,13},{6,14},{7,15},{8,0},{9,1},... | collective-permute-start | bytes 3145736 | tf_op jit(solution)/shard_map/t_Y/ppermute | solution.py:38
  44.4 23.6 %collective-permute-start.6 = (f32[2048,128]{1,0:T(8,128)}, f32[2048,128]{1,0:T(8,128)S(1)}, u32[]{:S(2)}, u32[]{:S(2)}) collective-permute-start(f32[2048,128]{1,0:T(8,128)} %unpack_a.1.refs_3_.refs_1_), channel_id=1, source_target_pairs={{0,6},{1,3},{2,0},{3,5},{4,2},{5,7},{6,4},{7,1},{8,14},{9,11},{10,... | collective-permute-start | bytes 3145736 | tf_op jit(solution)/shard_map/t_G/ppermute | solution.py:38
  50.9 78.2 %copy-start.11 = (s32[16,4]{0,1:T(4,128)S(1)}, s32[16,4]{0,1:T(4,128)}, u32[]{:S(2)}) copy-start(s32[16,4]{0,1:T(4,128)} %param.15) | copy-start | bytes 772
  50.9 41.2 %collective-permute-start.3 = (f32[512,512]{1,0:T(8,128)}, f32[512,512]{1,0:T(8,128)S(1)}, u32[]{:S(2)}, u32[]{:S(2)}) collective-permute-start(f32[512,512]{1,0:T(8,128)} %unpack_b.1), channel_id=1, source_target_pairs={{0,64},{16,80},{32,96},{48,112},{64,0},{80,16},{96,32},{112,48},{1... | collective-permute-start | bytes 3145736 | tf_op jit(solution)/shard_map/t_S/ppermute | solution.py:45
  53.4 40.4 %collective-permute-start.4 = (f32[2048,128]{1,0:T(8,128)S(1)}, f32[2048,128]{1,0:T(8,128)S(1)}, u32[]{:S(2)}, u32[]{:S(2)}) collective-permute-start(f32[2048,128]{1,0:T(8,128)S(1)} %copy-done.1), channel_id=1, source_target_pairs={{0,2},{1,7},{2,4},{3,1},{4,6},{5,3},{6,0},{7,5},{8,10},{9,15},{10,... | collective-permute-start | bytes 3145736 | tf_op jit(solution)/shard_map/t_F/ppermute | solution.py:38
  68.0 61.8 %copy-start.2 = (f32[2048,128]{1,0:T(8,128)}, f32[2048,128]{1,0:T(8,128)S(1)}, u32[]{:S(2)}) copy-start(f32[2048,128]{1,0:T(8,128)S(1)} %collective-permute-done.13.refs_11_.refs_9_) | copy-start | bytes 3145732
  68.1 61.8 %copy-start.3 = (f32[2048,128]{1,0:T(8,128)}, f32[2048,128]{1,0:T(8,128)S(1)}, u32[]{:S(2)}) copy-start(f32[2048,128]{1,0:T(8,128)S(1)} %collective-permute-done.6.refs_7_.refs_5_) | copy-start | bytes 3145732
  68.1 27.6 %collective-permute-start.15 = (f32[2048,128]{1,0:T(8,128)S(1)}, f32[2048,128]{1,0:T(8,128)}, u32[]{:S(2)}, u32[]{:S(2)}) collective-permute-start(f32[2048,128]{1,0:T(8,128)S(1)} %collective-permute-done.13.refs_11_.refs_9_), channel_id=1, source_target_pairs={{0,2},{1,7},{2,4},{3,1},{4,6},{5,3},{6,0},{7,5},{8,10},{9,15},{10,... | collective-permute-start | bytes 3145736 | tf_op jit(solution)/shard_map/t_YF/ppermute | solution.py:38
  68.6 27.6 %collective-permute-start.17 = (f32[2048,128]{1,0:T(8,128)S(1)}, f32[2048,128]{1,0:T(8,128)}, u32[]{:S(2)}, u32[]{:S(2)}) collective-permute-start(f32[2048,128]{1,0:T(8,128)S(1)} %collective-permute-done.13.refs_11_.refs_9_), channel_id=1, source_target_pairs={{0,6},{1,3},{2,0},{3,5},{4,2},{5,7},{6,4},{7,1},{8,14},{9,11},{10,... | collective-permute-start | bytes 3145736 | tf_op jit(solution)/shard_map/t_YG/ppermute | solution.py:38
  70.5 27.9 %collective-permute-start.8 = (f32[2048,128]{1,0:T(8,128)S(1)}, f32[2048,128]{1,0:T(8,128)S(1)}, u32[]{:S(2)}, u32[]{:S(2)}) collective-permute-start(f32[2048,128]{1,0:T(8,128)S(1)} %copy-done.1), channel_id=1, source_target_pairs={{0,1},{1,0},{2,3},{3,2},{4,5},{5,4},{6,7},{7,6},{8,9},{9,8},{10,11... | collective-permute-start | bytes 3145736 | tf_op jit(solution)/shard_map/t_cown/ppermute | solution.py:38
  92.1 10.0 %collective-permute-start.14 = (f32[2048,128]{1,0:T(8,128)S(1)}, f32[2048,128]{1,0:T(8,128)S(1)}, u32[]{:S(2)}, u32[]{:S(2)}) collective-permute-start(f32[2048,128]{1,0:T(8,128)S(1)} %collective-permute-done.13.refs_11_.refs_9_), channel_id=1, source_target_pairs={{0,1},{1,0},{2,3},{3,2},{4,5},{5,4},{6,7},{7,6},{8,9},{9,8},{10,11... | collective-permute-start | bytes 3145736 | tf_op jit(solution)/shard_map/t_cY/ppermute | solution.py:38
  93.8 8.9 %collective-permute-start.10 = (f32[2048,128]{1,0:T(8,128)S(1)}, f32[2048,128]{1,0:T(8,128)S(1)}, u32[]{:S(2)}, u32[]{:S(2)}) collective-permute-start(f32[2048,128]{1,0:T(8,128)S(1)} %collective-permute-done.6.refs_7_.refs_5_), channel_id=1, source_target_pairs={{0,1},{1,0},{2,3},{3,2},{4,5},{5,4},{6,7},{7,6},{8,9},{9,8},{10,11... | collective-permute-start | bytes 3145736 | tf_op jit(solution)/shard_map/t_cG/ppermute | solution.py:38
  95.6 28.1 %copy-start.9 = (f32[512,512]{1,0:T(8,128)}, f32[512,512]{1,0:T(8,128)S(1)}, u32[]{:S(2)}) copy-start(f32[512,512]{1,0:T(8,128)S(1)} %add.3.refs_0_) | copy-start | bytes 3145732
  95.6 14.9 %collective-permute-start.11 = (f32[2048,128]{1,0:T(8,128)S(1)}, f32[2048,128]{1,0:T(8,128)}, u32[]{:S(2)}, u32[]{:S(2)}) collective-permute-start(f32[2048,128]{1,0:T(8,128)S(1)} %collective-permute-done.4.refs_5_.refs_3_), channel_id=1, source_target_pairs={{0,2},{1,7},{2,4},{3,1},{4,6},{5,3},{6,0},{7,5},{8,10},{9,15},{10,... | collective-permute-start | bytes 3145736 | tf_op jit(solution)/shard_map/t_H/ppermute | solution.py:38
  96.1 15.9 %collective-permute-start.9 = (f32[2048,128]{1,0:T(8,128)S(1)}, f32[2048,128]{1,0:T(8,128)S(1)}, u32[]{:S(2)}, u32[]{:S(2)}) collective-permute-start(f32[2048,128]{1,0:T(8,128)S(1)} %collective-permute-done.4.refs_5_.refs_3_), channel_id=1, source_target_pairs={{0,1},{1,0},{2,3},{3,2},{4,5},{5,4},{6,7},{7,6},{8,9},{9,8},{10,11... | collective-permute-start | bytes 3145736 | tf_op jit(solution)/shard_map/t_cF/ppermute | solution.py:38
  98.3 13.7 %copy-start.5 = (f32[2048,128]{1,0:T(8,128)}, f32[2048,128]{1,0:T(8,128)S(1)}, u32[]{:S(2)}) copy-start(f32[2048,128]{1,0:T(8,128)S(1)} %collective-permute-done.8.refs_4_.refs_2_) | copy-start | bytes 3145732
  98.3 25.3 %collective-permute-start.5 = (f32[512,512]{1,0:T(8,128)S(1)}, f32[512,512]{1,0:T(8,128)}, u32[]{:S(2)}, u32[]{:S(2)}) collective-permute-start(f32[512,512]{1,0:T(8,128)S(1)} %add.3.refs_0_), channel_id=1, source_target_pairs={{0,16},{1,49},{2,18},{3,51},{4,20},{5,53},{6,22},{7,55},{8,24},{9,... | collective-permute-start | bytes 3145736 | tf_op jit(solution)/shard_map/t_bF/ppermute | solution.py:54
  102.1 10.1 %copy-start.6 = (f32[2048,128]{1,0:T(8,128)}, f32[2048,128]{1,0:T(8,128)S(1)}, u32[]{:S(2)}) copy-start(f32[2048,128]{1,0:T(8,128)S(1)} %collective-permute-done.14.refs_12_.refs_10_) | copy-start | bytes 3145732
  102.1 21.6 %collective-permute-start.19 = (f32[2048,128]{1,0:T(8,128)}, f32[2048,128]{1,0:T(8,128)S(1)}, u32[]{:S(2)}, u32[]{:S(2)}) collective-permute-start(f32[2048,128]{1,0:T(8,128)} %collective-permute-done.15.refs_13_.refs_11_), channel_id=1, source_target_pairs={{0,2},{1,7},{2,4},{3,1},{4,6},{5,3},{6,0},{7,5},{8,10},{9,15},{10,... | collective-permute-start | bytes 3145736 | tf_op jit(solution)/shard_map/t_YH/ppermute | solution.py:38
  102.7 21.0 %copy-start.7 = (f32[2048,128]{1,0:T(8,128)}, f32[2048,128]{1,0:T(8,128)S(1)}, u32[]{:S(2)}) copy-start(f32[2048,128]{1,0:T(8,128)S(1)} %collective-permute-done.10.refs_8_.refs_6_) | copy-start | bytes 3145732
  102.7 23.1 %collective-permute-start.21 = (f32[512,512]{1,0:T(8,128)S(1)}, f32[512,512]{1,0:T(8,128)S(1)}, u32[]{:S(2)}, u32[]{:S(2)}) collective-permute-start(f32[512,512]{1,0:T(8,128)S(1)} %add.3.refs_0_), channel_id=1, source_target_pairs={{0,48},{1,17},{2,50},{3,19},{4,52},{5,21},{6,54},{7,23},{8,56},{9,... | collective-permute-start | bytes 3145736 | tf_op jit(solution)/shard_map/t_bG/ppermute | solution.py:54
  110.5 19.3 %collective-permute-start.16 = (f32[2048,128]{1,0:T(8,128)}, f32[2048,128]{1,0:T(8,128)}, u32[]{:S(2)}, u32[]{:S(2)}) collective-permute-start(f32[2048,128]{1,0:T(8,128)} %collective-permute-done.15.refs_13_.refs_11_), channel_id=1, source_target_pairs={{0,1},{1,0},{2,3},{3,2},{4,5},{5,4},{6,7},{7,6},{8,9},{9,8},{10,11... | collective-permute-start | bytes 3145736 | tf_op jit(solution)/shard_map/t_cYF/ppermute | solution.py:38
  112.1 11.6 %copy-start.8 = (f32[2048,128]{1,0:T(8,128)}, f32[2048,128]{1,0:T(8,128)S(1)}, u32[]{:S(2)}) copy-start(f32[2048,128]{1,0:T(8,128)S(1)} %collective-permute-done.9.refs_6_.refs_4_) | copy-start | bytes 3145732
  112.1 17.8 %collective-permute-start.18 = (f32[2048,128]{1,0:T(8,128)}, f32[2048,128]{1,0:T(8,128)}, u32[]{:S(2)}, u32[]{:S(2)}) collective-permute-start(f32[2048,128]{1,0:T(8,128)} %collective-permute-done.17.refs_15_.refs_13_), channel_id=1, source_target_pairs={{0,1},{1,0},{2,3},{3,2},{4,5},{5,4},{6,7},{7,6},{8,9},{9,8},{10,11... | collective-permute-start | bytes 3145736 | tf_op jit(solution)/shard_map/t_cYG/ppermute | solution.py:38
  123.7 6.2 %collective-permute-start.12 = (f32[2048,128]{1,0:T(8,128)}, f32[2048,128]{1,0:T(8,128)}, u32[]{:S(2)}, u32[]{:S(2)}) collective-permute-start(f32[2048,128]{1,0:T(8,128)} %collective-permute-done.11.refs_9_.refs_7_), channel_id=1, source_target_pairs={{0,1},{1,0},{2,3},{3,2},{4,5},{5,4},{6,7},{7,6},{8,9},{9,8},{10,11... | collective-permute-start | bytes 3145736 | tf_op jit(solution)/shard_map/t_cH/ppermute | solution.py:38
  123.7 6.1 %collective-permute-start.20 = (f32[2048,128]{1,0:T(8,128)S(1)}, f32[2048,128]{1,0:T(8,128)}, u32[]{:S(2)}, u32[]{:S(2)}) collective-permute-start(f32[2048,128]{1,0:T(8,128)S(1)} %collective-permute-done.19.refs_17_.refs_15_), channel_id=1, source_target_pairs={{0,1},{1,0},{2,3},{3,2},{4,5},{5,4},{6,7},{7,6},{8,9},{9,8},{10,11... | collective-permute-start | bytes 3145736 | tf_op jit(solution)/shard_map/t_cYH/ppermute | solution.py:38
  126.7 21.1 %collective-permute-start.7 = (f32[512,512]{1,0:T(8,128)}, f32[512,512]{1,0:T(8,128)}, u32[]{:S(2)}, u32[]{:S(2)}) collective-permute-start(f32[512,512]{1,0:T(8,128)} %collective-permute-done.5.refs_1_), channel_id=1, source_target_pairs={{0,16},{1,49},{2,18},{3,51},{4,20},{5,53},{6,22},{7,55},{8,24},{9,... | collective-permute-start | bytes 3145736 | tf_op jit(solution)/shard_map/t_bH/ppermute | solution.py:54
  (4 other events, 17.4 us)

commit v5 on v4

--- a/solution.py
+++ b/solution.py
@@ -248,7 +248,7 @@
     return ks
 
 
-TM = 512
+TM, TM_LAST = 512, 1024
 
 
 def product_kernel(last, mask, *refs):
@@ -258,6 +258,7 @@
     before = refs.pop(0) if last else None
     out, rows, panel, stack, a_sems, b_sems = refs
     tile, tiles = pl.program_id(0), pl.num_programs(0)
+    tm = out.shape[0]
     depth = len(b_pieces) * KZ * BS
     z_now, step = place()[0], place()[4]
 
@@ -267,7 +268,7 @@
             hop = lax.rem((z_now - lax.div(k, KZ)) * step + 2 * NZ, NZ)
             slot = lax.rem(k, KZ) + (0 if last else KZ * jnp.minimum(hop, 2))
             copy = pltpu.make_async_copy(
-                piece.at[pl.ds(pl.multiple_of(at * TM, TM), TM)],
+                piece.at[pl.ds(pl.multiple_of(at * tm, tm), tm)],
                 rows.at[buffer, :, pl.ds(pl.multiple_of(slot * BS, BS), BS)],
                 a_sems.at[buffer, slot],
             )
@@ -297,9 +298,9 @@
     total += jnp.dot(low, stack[pl.ds(0, depth), :], preferred_element_type=F32)
     if last:
         total += before[...]
-        for r in range(TM // BS):
+        for r in range(tm // BS):
             for c in range(CB):
-                keep = mask[tile * (TM // BS) + r, c].astype(F32)
+                keep = mask[tile * (tm // BS) + r, c].astype(F32)
                 piece = total[r * BS : (r + 1) * BS, c * BS : (c + 1) * BS]
                 out[pl.ds(r * BS, BS), pl.ds(c * BS, BS)] = piece * keep
     else:
@@ -310,16 +311,17 @@
 def product(mask, b_pieces, a_pieces, before=None):
     height, cols = RB * BS, CB * BS
     depth = len(b_pieces) * KZ * BS
-    c_spec = pl.BlockSpec((TM, cols), lambda t: (t, 0))
     last = before is not None
+    tm = TM_LAST if last else TM
+    c_spec = pl.BlockSpec((tm, cols), lambda t: (t, 0))
     return pl.pallas_call(
         functools.partial(product_kernel, last),
-        grid=(height // TM,),
+        grid=(height // tm,),
         out_shape=jax.ShapeDtypeStruct((height, cols), F32),
         in_specs=[SMEM] + [HBM] * (len(b_pieces) + KB) + [c_spec] * last,
         out_specs=c_spec,
         scratch_shapes=[
-            pltpu.VMEM((2, TM, depth), F32),
+            pltpu.VMEM((2, tm, depth), F32),
             pltpu.VMEM((depth, cols), F32),
             pltpu.VMEM((2 * depth, cols), jnp.bfloat16),
             pltpu.SemaphoreType.DMA((2, depth // BS)),

time: 159 us -> 159 us (level)
  no operation moved by 1% of the time
where the time goes in v5:
time: 159 us; the launch traced here: 158 us
  waiting for transfers between devices  72.9 us (46%)
  Pallas kernels  42.4 us (27%)
  starting transfers between devices  37.9 us (24%)
  local copies, waits for them, and re-layouts  3.02 us (2%)
  other arithmetic  1.74 us (1%)
    pallas_call x2, Pallas kernels, product(): pl.pallas_call(functools.partial(product_kernel, last), grid=(height // t...  27.8 us
    ppermute x15, waiting for transfers between devices, col_shift(): return lax.ppermute(value, 'col', route)  22 us
    all_to_all x1, waiting for transfers between devices, per_device(): lax.all_to_all(a_send, 'col', split_axis=0, concat_axis=0, tiled=True)  19.5 us
    ppermute x4, waiting for transfers between devices, row_shift(): return lax.ppermute(value, 'row', route)  18.3 us
    ppermute x15, starting transfers between devices, col_shift(): return lax.ppermute(value, 'col', route)  16.5 us
    ppermute x3, waiting for transfers between devices, row_shift_by_core(): return lax.ppermute(value, ('row', 'col'), route)  13.1 us
    ppermute x4, starting transfers between devices, row_shift(): return lax.ppermute(value, 'row', route)  8.08 us
    all_to_all x1, starting transfers between devices, per_device(): lax.all_to_all(a_send, 'col', split_axis=0, concat_axis=0, tiled=True)  6.82 us
  transfers between devices with their start and end apart: 23, of which 6 were waited for; matrix products, arithmetic and copies ran while one was open for 2% of the time, Pallas kernels for 18%

profile of v5, /device:TPU:1, one launch (start us, length us, event | category | flops | bytes accessed | tf_op | source)
XLA Modules:
  0.0 158.2 jit_solution(14030065483493796515)
XLA Ops:
  0.0 3.6 %pack_a.1 = f32[16,264,128]{2,1,0:T(8,128)} custom-call(s32[16]{0:T(128)} %bitcast.8, s32[32]{0:T(128)} %bitcast.9, f32[32,128,128]{2,1,0:T(8,128)} %bitcast.6), custom_call_target="tpu_custom_call" | custom-call | tf_op jit(solution)/shard_map/pack_a/pallas_call | solution.py:101
  3.6 6.8 %all-to-all-start = ((f32[16,264,128]{2,1,0:T(8,128)}), f32[16,264,128]{2,1,0:T(8,128)S(1)}, u32[]{:S(2)}, u32[]{:S(2)}) async-start(f32[16,264,128]{2,1,0:T(8,128)} %pack_a.1), calls=%async_computation | async-start | bytes 4325376 | tf_op jit(solution)/shard_map/all_to_all | solution.py:342
  10.4 3.4 %pack_b.1 = (f32[1056,128]{1,0:T(8,128)}, f32[1056,128]{1,0:T(8,128)}, f32[1056,128]{1,0:T(8,128)}, f32[1056,128]{1,0:T(8,128)}) custom-call(s32[16]{0:T(128)} %bitcast.10, s32[32]{0:T(128)} %bitcast.11, f32[32,128,128]{2,1,0:T(8,128)} %bitcast.7), custom_call_target="tpu_custom_call" | custom-call | tf_op jit(solution)/shard_map/pack_b/pallas_call | solution.py:140
  13.8 1.8 %collective-permute-start = (f32[1056,128]{1,0:T(8,128)}, f32[1056,128]{1,0:T(8,128)}, u32[]{:S(2)}, u32[]{:S(2)}) collective-permute-start(f32[1056,128]{1,0:T(8,128)} %get-tuple-element.19), channel_id=1, source_target_pairs={{0,16},{16,32},{32,48},{48,0},{64,80},{80,96},{96,112},{112,64},{1... | collective-permute-start | bytes 1622024 | tf_op jit(solution)/shard_map/ppermute | solution.py:45
  15.6 3.3 %collective-permute-start.1 = (f32[1056,128]{1,0:T(8,128)}, f32[1056,128]{1,0:T(8,128)}, u32[]{:S(2)}, u32[]{:S(2)}) collective-permute-start(f32[1056,128]{1,0:T(8,128)} %get-tuple-element.20), channel_id=1, source_target_pairs={{0,32},{16,48},{32,0},{48,16},{64,96},{80,112},{96,64},{112,80},{1... | collective-permute-start | bytes 1622024 | tf_op jit(solution)/shard_map/ppermute | solution.py:45
  18.9 0.5 collective-permute-start.2
  19.4 19.5 %all-to-all-done.got = f32[16,264,128]{2,1,0:T(8,128)S(1)} async-done(((f32[16,264,128]{2,1,0:T(8,128)}), f32[16,264,128]{2,1,0:T(8,128)S(1)}, u32[]{:S(2)}, u32[]{:S(2)}) %all-to-all-start) | async-done | bytes 2162720 | tf_op jit(solution)/shard_map/all_to_all | solution.py:342
  38.9 1.3 copy-done
  40.3 3.4 %unpack_a.1.refs_3_.refs_1_ = f32[2048,128]{1,0:T(8,128)} custom-call(f32[16,264,128]{2,1,0:T(8,128)} %copy-done), custom_call_target="tpu_custom_call" | custom-call | tf_op jit(solution)/shard_map/unpack_a/pallas_call | solution.py:174
  43.7 0.8 collective-permute-start.13
  44.5 2.2 %collective-permute-start.6 = (f32[2048,128]{1,0:T(8,128)}, f32[2048,128]{1,0:T(8,128)S(1)}, u32[]{:S(2)}, u32[]{:S(2)}) collective-permute-start(f32[2048,128]{1,0:T(8,128)} %unpack_a.1.refs_3_.refs_1_), channel_id=1, source_target_pairs={{0,6},{1,3},{2,0},{3,5},{4,2},{5,7},{6,4},{7,1},{8,14},{9,11},{10,... | collective-permute-start | bytes 3145736 | tf_op jit(solution)/shard_map/t_G/ppermute | solution.py:38
  46.7 4.2 %unpack_b.1 = f32[512,512]{1,0:T(8,128)} custom-call(f32[1056,128]{1,0:T(8,128)} %get-tuple-element.18.refs_0_, f32[1056,128]{1,0:T(8,128)} %collective-permute-done.refs_1_, f32[1056,128]{1,0:T(8,128)} %collective-permute-done.1.refs_2_, f32[1056,128]{1,0:T(8,128)} %collective-permute-done.2.refs_3_), custom_call_target="tpu_custom_call" | custom-call | tf_op jit(solution)/shard_map/unpack_b/pallas_call | solution.py:220
  51.0 2.5 %collective-permute-start.3 = (f32[512,512]{1,0:T(8,128)}, f32[512,512]{1,0:T(8,128)S(1)}, u32[]{:S(2)}, u32[]{:S(2)}) collective-permute-start(f32[512,512]{1,0:T(8,128)} %unpack_b.1), channel_id=1, source_target_pairs={{0,64},{16,80},{32,96},{48,112},{64,0},{80,16},{96,32},{112,48},{1... | collective-permute-start | bytes 3145736 | tf_op jit(solution)/shard_map/t_S/ppermute | solution.py:45
  53.4 0.6 collective-permute-start.4
  54.0 14.2 %collective-permute-done.13.refs_11_.refs_9_ = f32[2048,128]{1,0:T(8,128)S(1)} collective-permute-done((f32[2048,128]{1,0:T(8,128)}, f32[2048,128]{1,0:T(8,128)S(1)}, u32[]{:S(2)}, u32[]{:S(2)}) %collective-permute-start.13) | collective-permute-done | bytes 1048608 | tf_op jit(solution)/shard_map/t_Y/ppermute | solution.py:38
  68.5 2.0 %collective-permute-start.17 = (f32[2048,128]{1,0:T(8,128)S(1)}, f32[2048,128]{1,0:T(8,128)}, u32[]{:S(2)}, u32[]{:S(2)}) collective-permute-start(f32[2048,128]{1,0:T(8,128)S(1)} %collective-permute-done.13.refs_11_.refs_9_), channel_id=1, source_target_pairs={{0,6},{1,3},{2,0},{3,5},{4,2},{5,7},{6,4},{7,1},{8,14},{9,11},{10,... | collective-permute-start | bytes 3145736 | tf_op jit(solution)/shard_map/t_YG/ppermute | solution.py:38
  70.5 3.3 %collective-permute-start.8 = (f32[2048,128]{1,0:T(8,128)S(1)}, f32[2048,128]{1,0:T(8,128)S(1)}, u32[]{:S(2)}, u32[]{:S(2)}) collective-permute-start(f32[2048,128]{1,0:T(8,128)S(1)} %copy-done.1), channel_id=1, source_target_pairs={{0,1},{1,0},{2,3},{3,2},{4,5},{5,4},{6,7},{7,6},{8,9},{9,8},{10,11... | collective-permute-start | bytes 3145736 | tf_op jit(solution)/shard_map/t_cown/ppermute | solution.py:38
  73.8 18.3 %collective-permute-done.3 = f32[512,512]{1,0:T(8,128)S(1)} collective-permute-done((f32[512,512]{1,0:T(8,128)}, f32[512,512]{1,0:T(8,128)S(1)}, u32[]{:S(2)}, u32[]{:S(2)}) %collective-permute-start.3) | collective-permute-done | bytes 1048608 | tf_op jit(solution)/shard_map/t_S/ppermute | solution.py:45
  92.1 1.8 %collective-permute-start.14 = (f32[2048,128]{1,0:T(8,128)S(1)}, f32[2048,128]{1,0:T(8,128)S(1)}, u32[]{:S(2)}, u32[]{:S(2)}) collective-permute-start(f32[2048,128]{1,0:T(8,128)S(1)} %collective-permute-done.13.refs_11_.refs_9_), channel_id=1, source_target_pairs={{0,1},{1,0},{2,3},{3,2},{4,5},{5,4},{6,7},{7,6},{8,9},{9,8},{10,11... | collective-permute-start | bytes 3145736 | tf_op jit(solution)/shard_map/t_cY/ppermute | solution.py:38
  94.0 1.7 %add.3.refs_0_ = f32[512,512]{1,0:T(8,128)S(1)} add(f32[512,512]{1,0:T(8,128)} %unpack_b.1, f32[512,512]{1,0:T(8,128)S(1)} %collective-permute-done.3) | non-fusion elementwise | flops 262144 | bytes 3145728 | tf_op jit(solution)/shard_map/add | solution.py:385
  96.2 2.2 %collective-permute-start.9 = (f32[2048,128]{1,0:T(8,128)S(1)}, f32[2048,128]{1,0:T(8,128)S(1)}, u32[]{:S(2)}, u32[]{:S(2)}) collective-permute-start(f32[2048,128]{1,0:T(8,128)S(1)} %collective-permute-done.4.refs_5_.refs_3_), channel_id=1, source_target_pairs={{0,1},{1,0},{2,3},{3,2},{4,5},{5,4},{6,7},{7,6},{8,9},{9,8},{10,11... | collective-permute-start | bytes 3145736 | tf_op jit(solution)/shard_map/t_cF/ppermute | solution.py:38
  98.4 3.8 %collective-permute-start.5 = (f32[512,512]{1,0:T(8,128)S(1)}, f32[512,512]{1,0:T(8,128)}, u32[]{:S(2)}, u32[]{:S(2)}) collective-permute-start(f32[512,512]{1,0:T(8,128)S(1)} %add.3.refs_0_), channel_id=1, source_target_pairs={{0,16},{1,49},{2,18},{3,51},{4,20},{5,53},{6,22},{7,55},{8,24},{9,... | collective-permute-start | bytes 3145736 | tf_op jit(solution)/shard_map/t_bF/ppermute | solution.py:54
  102.8 7.8 %collective-permute-done.11.refs_9_.refs_7_ = f32[2048,128]{1,0:T(8,128)} collective-permute-done((f32[2048,128]{1,0:T(8,128)S(1)}, f32[2048,128]{1,0:T(8,128)}, u32[]{:S(2)}, u32[]{:S(2)}) %collective-permute-start.11) | collective-permute-done | bytes 1048608 | tf_op jit(solution)/shard_map/t_H/ppermute | solution.py:38
  110.6 1.5 collective-permute-start.16
  112.2 11.8 %collective-permute-done.5.refs_1_ = f32[512,512]{1,0:T(8,128)} collective-permute-done((f32[512,512]{1,0:T(8,128)S(1)}, f32[512,512]{1,0:T(8,128)}, u32[]{:S(2)}, u32[]{:S(2)}) %collective-permute-start.5) | collective-permute-done | bytes 1048608 | tf_op jit(solution)/shard_map/t_bF/ppermute | solution.py:54
  124.0 0.6 collective-permute-start.20
  124.6 1.3 collective-permute-done.21.refs_2_
  125.9 1.0 copy-done.12
  126.9 2.6 %collective-permute-start.7 = (f32[512,512]{1,0:T(8,128)}, f32[512,512]{1,0:T(8,128)}, u32[]{:S(2)}, u32[]{:S(2)}) collective-permute-start(f32[512,512]{1,0:T(8,128)} %collective-permute-done.5.refs_1_), channel_id=1, source_target_pairs={{0,16},{1,49},{2,18},{3,51},{4,20},{5,53},{6,22},{7,55},{8,24},{9,... | collective-permute-start | bytes 3145736 | tf_op jit(solution)/shard_map/t_bH/ppermute | solution.py:54
  129.5 0.7 copy.9.mask
  130.3 17.9 %product.2.refs_17_ = f32[2048,512]{1,0:T(8,128)} custom-call(s32[16,4]{1,0:T(8,128)} %copy.9.mask, f32[512,512]{1,0:T(8,128)} %copy-done.9, f32[512,512]{1,0:T(8,128)} %collective-permute-done.5.refs_1_, f32[512,512]{1,0:T(8,128)} %copy-done.12, f32[2048,128]{1,0:T(8,128)} %unpack_a.1.refs_3_.refs_1_, f32[2048,128]{1,0:T(8,128)} %copy-done.5, ...), custom_call_target="tpu_custom_call" | custom-call | flops 9663676416 | bytes 24117248 | tf_op jit(solution)/shard_map/product/pallas_call | solution.py:317
  148.2 9.9 %product.3 = f32[2048,512]{1,0:T(8,128)} custom-call(s32[16,4]{1,0:T(8,128)} %copy.9.mask, f32[512,512]{1,0:T(8,128)} %collective-permute-done.7.refs_0_, f32[2048,128]{1,0:T(8,128)} %unpack_a.1.refs_3_.refs_1_, f32[2048,128]{1,0:T(8,128)} %copy-done.5, f32[2048,128]{1,0:T(8,128)} %copy-done.4, f32[2048,128]{1,0:T(8,128)} %copy-done.8, ...), custom_call_target="tpu_custom_call" | custom-call | flops 3221225472 | bytes 13631488 | tf_op jit(solution)/shard_map/product/pallas_call | solution.py:317
  (48 shorter events, 1.6 us)
Async XLA Ops:
  3.6 35.3 %all-to-all-start = ((f32[16,264,128]{2,1,0:T(8,128)}), f32[16,264,128]{2,1,0:T(8,128)S(1)}, u32[]{:S(2)}, u32[]{:S(2)}) async-start(f32[16,264,128]{2,1,0:T(8,128)} %pack_a.1), calls=%async_computation | async-start | bytes 4325376 | tf_op jit(solution)/shard_map/all_to_all | solution.py:342
  13.8 32.9 %collective-permute-start = (f32[1056,128]{1,0:T(8,128)}, f32[1056,128]{1,0:T(8,128)}, u32[]{:S(2)}, u32[]{:S(2)}) collective-permute-start(f32[1056,128]{1,0:T(8,128)} %get-tuple-element.19), channel_id=1, source_target_pairs={{0,16},{16,32},{32,48},{48,0},{64,80},{80,96},{96,112},{112,64},{1... | collective-permute-start | bytes 1622024 | tf_op jit(solution)/shard_map/ppermute | solution.py:45
  15.6 31.1 %collective-permute-start.1 = (f32[1056,128]{1,0:T(8,128)}, f32[1056,128]{1,0:T(8,128)}, u32[]{:S(2)}, u32[]{:S(2)}) collective-permute-start(f32[1056,128]{1,0:T(8,128)} %get-tuple-element.20), channel_id=1, source_target_pairs={{0,32},{16,48},{32,0},{48,16},{64,96},{80,112},{96,64},{112,80},{1... | collective-permute-start | bytes 1622024 | tf_op jit(solution)/shard_map/ppermute | solution.py:45
  18.9 27.8 %collective-permute-start.2 = (f32[1056,128]{1,0:T(8,128)}, f32[1056,128]{1,0:T(8,128)}, u32[]{:S(2)}, u32[]{:S(2)}) collective-permute-start(f32[1056,128]{1,0:T(8,128)} %get-tuple-element.21), channel_id=1, source_target_pairs={{0,48},{16,0},{32,16},{48,32},{64,112},{80,64},{96,80},{112,96},{1... | collective-permute-start | bytes 1622024 | tf_op jit(solution)/shard_map/ppermute | solution.py:45
  43.7 9.8 %copy-start.1 = (f32[2048,128]{1,0:T(8,128)S(1)}, f32[2048,128]{1,0:T(8,128)}, u32[]{:S(2)}) copy-start(f32[2048,128]{1,0:T(8,128)} %unpack_a.1.refs_3_.refs_1_) | copy-start | bytes 3145732
  43.7 24.5 %collective-permute-start.13 = (f32[2048,128]{1,0:T(8,128)}, f32[2048,128]{1,0:T(8,128)S(1)}, u32[]{:S(2)}, u32[]{:S(2)}) collective-permute-start(f32[2048,128]{1,0:T(8,128)} %unpack_a.1.refs_3_.refs_1_), channel_id=1, source_target_pairs={{0,8},{1,9},{2,10},{3,11},{4,12},{5,13},{6,14},{7,15},{8,0},{9,1},... | collective-permute-start | bytes 3145736 | tf_op jit(solution)/shard_map/t_Y/ppermute | solution.py:38
  44.5 23.7 %collective-permute-start.6 = (f32[2048,128]{1,0:T(8,128)}, f32[2048,128]{1,0:T(8,128)S(1)}, u32[]{:S(2)}, u32[]{:S(2)}) collective-permute-start(f32[2048,128]{1,0:T(8,128)} %unpack_a.1.refs_3_.refs_1_), channel_id=1, source_target_pairs={{0,6},{1,3},{2,0},{3,5},{4,2},{5,7},{6,4},{7,1},{8,14},{9,11},{10,... | collective-permute-start | bytes 3145736 | tf_op jit(solution)/shard_map/t_G/ppermute | solution.py:38
  51.0 78.6 %copy-start.11 = (s32[16,4]{0,1:T(4,128)S(1)}, s32[16,4]{0,1:T(4,128)}, u32[]{:S(2)}) copy-start(s32[16,4]{0,1:T(4,128)} %param.15) | copy-start | bytes 772
  51.0 41.1 %collective-permute-start.3 = (f32[512,512]{1,0:T(8,128)}, f32[512,512]{1,0:T(8,128)S(1)}, u32[]{:S(2)}, u32[]{:S(2)}) collective-permute-start(f32[512,512]{1,0:T(8,128)} %unpack_b.1), channel_id=1, source_target_pairs={{0,64},{16,80},{32,96},{48,112},{64,0},{80,16},{96,32},{112,48},{1... | collective-permute-start | bytes 3145736 | tf_op jit(solution)/shard_map/t_S/ppermute | solution.py:45
  53.4 40.4 %collective-permute-start.4 = (f32[2048,128]{1,0:T(8,128)S(1)}, f32[2048,128]{1,0:T(8,128)S(1)}, u32[]{:S(2)}, u32[]{:S(2)}) collective-permute-start(f32[2048,128]{1,0:T(8,128)S(1)} %copy-done.1), channel_id=1, source_target_pairs={{0,2},{1,7},{2,4},{3,1},{4,6},{5,3},{6,0},{7,5},{8,10},{9,15},{10,... | collective-permute-start | bytes 3145736 | tf_op jit(solution)/shard_map/t_F/ppermute | solution.py:38
  68.2 62.1 %copy-start.2 = (f32[2048,128]{1,0:T(8,128)}, f32[2048,128]{1,0:T(8,128)S(1)}, u32[]{:S(2)}) copy-start(f32[2048,128]{1,0:T(8,128)S(1)} %collective-permute-done.13.refs_11_.refs_9_) | copy-start | bytes 3145732
  68.2 62.1 %copy-start.3 = (f32[2048,128]{1,0:T(8,128)}, f32[2048,128]{1,0:T(8,128)S(1)}, u32[]{:S(2)}) copy-start(f32[2048,128]{1,0:T(8,128)S(1)} %collective-permute-done.6.refs_7_.refs_5_) | copy-start | bytes 3145732
  68.2 27.5 %collective-permute-start.15 = (f32[2048,128]{1,0:T(8,128)S(1)}, f32[2048,128]{1,0:T(8,128)}, u32[]{:S(2)}, u32[]{:S(2)}) collective-permute-start(f32[2048,128]{1,0:T(8,128)S(1)} %collective-permute-done.13.refs_11_.refs_9_), channel_id=1, source_target_pairs={{0,2},{1,7},{2,4},{3,1},{4,6},{5,3},{6,0},{7,5},{8,10},{9,15},{10,... | collective-permute-start | bytes 3145736 | tf_op jit(solution)/shard_map/t_YF/ppermute | solution.py:38
  68.5 27.7 %collective-permute-start.17 = (f32[2048,128]{1,0:T(8,128)S(1)}, f32[2048,128]{1,0:T(8,128)}, u32[]{:S(2)}, u32[]{:S(2)}) collective-permute-start(f32[2048,128]{1,0:T(8,128)S(1)} %collective-permute-done.13.refs_11_.refs_9_), channel_id=1, source_target_pairs={{0,6},{1,3},{2,0},{3,5},{4,2},{5,7},{6,4},{7,1},{8,14},{9,11},{10,... | collective-permute-start | bytes 3145736 | tf_op jit(solution)/shard_map/t_YG/ppermute | solution.py:38
  70.5 27.9 %collective-permute-start.8 = (f32[2048,128]{1,0:T(8,128)S(1)}, f32[2048,128]{1,0:T(8,128)S(1)}, u32[]{:S(2)}, u32[]{:S(2)}) collective-permute-start(f32[2048,128]{1,0:T(8,128)S(1)} %copy-done.1), channel_id=1, source_target_pairs={{0,1},{1,0},{2,3},{3,2},{4,5},{5,4},{6,7},{7,6},{8,9},{9,8},{10,11... | collective-permute-start | bytes 3145736 | tf_op jit(solution)/shard_map/t_cown/ppermute | solution.py:38
  92.1 10.2 %collective-permute-start.14 = (f32[2048,128]{1,0:T(8,128)S(1)}, f32[2048,128]{1,0:T(8,128)S(1)}, u32[]{:S(2)}, u32[]{:S(2)}) collective-permute-start(f32[2048,128]{1,0:T(8,128)S(1)} %collective-permute-done.13.refs_11_.refs_9_), channel_id=1, source_target_pairs={{0,1},{1,0},{2,3},{3,2},{4,5},{5,4},{6,7},{7,6},{8,9},{9,8},{10,11... | collective-permute-start | bytes 3145736 | tf_op jit(solution)/shard_map/t_cY/ppermute | solution.py:38
  93.9 8.9 %collective-permute-start.10 = (f32[2048,128]{1,0:T(8,128)S(1)}, f32[2048,128]{1,0:T(8,128)S(1)}, u32[]{:S(2)}, u32[]{:S(2)}) collective-permute-start(f32[2048,128]{1,0:T(8,128)S(1)} %collective-permute-done.6.refs_7_.refs_5_), channel_id=1, source_target_pairs={{0,1},{1,0},{2,3},{3,2},{4,5},{5,4},{6,7},{7,6},{8,9},{9,8},{10,11... | collective-permute-start | bytes 3145736 | tf_op jit(solution)/shard_map/t_cG/ppermute | solution.py:38
  95.7 28.3 %copy-start.9 = (f32[512,512]{1,0:T(8,128)}, f32[512,512]{1,0:T(8,128)S(1)}, u32[]{:S(2)}) copy-start(f32[512,512]{1,0:T(8,128)S(1)} %add.3.refs_0_) | copy-start | bytes 3145732
  95.7 14.9 %collective-permute-start.11 = (f32[2048,128]{1,0:T(8,128)S(1)}, f32[2048,128]{1,0:T(8,128)}, u32[]{:S(2)}, u32[]{:S(2)}) collective-permute-start(f32[2048,128]{1,0:T(8,128)S(1)} %collective-permute-done.4.refs_5_.refs_3_), channel_id=1, source_target_pairs={{0,2},{1,7},{2,4},{3,1},{4,6},{5,3},{6,0},{7,5},{8,10},{9,15},{10,... | collective-permute-start | bytes 3145736 | tf_op jit(solution)/shard_map/t_H/ppermute | solution.py:38
  96.2 15.9 %collective-permute-start.9 = (f32[2048,128]{1,0:T(8,128)S(1)}, f32[2048,128]{1,0:T(8,128)S(1)}, u32[]{:S(2)}, u32[]{:S(2)}) collective-permute-start(f32[2048,128]{1,0:T(8,128)S(1)} %collective-permute-done.4.refs_5_.refs_3_), channel_id=1, source_target_pairs={{0,1},{1,0},{2,3},{3,2},{4,5},{5,4},{6,7},{7,6},{8,9},{9,8},{10,11... | collective-permute-start | bytes 3145736 | tf_op jit(solution)/shard_map/t_cF/ppermute | solution.py:38
  98.4 13.7 %copy-start.5 = (f32[2048,128]{1,0:T(8,128)}, f32[2048,128]{1,0:T(8,128)S(1)}, u32[]{:S(2)}) copy-start(f32[2048,128]{1,0:T(8,128)S(1)} %collective-permute-done.8.refs_4_.refs_2_) | copy-start | bytes 3145732
  98.4 25.6 %collective-permute-start.5 = (f32[512,512]{1,0:T(8,128)S(1)}, f32[512,512]{1,0:T(8,128)}, u32[]{:S(2)}, u32[]{:S(2)}) collective-permute-start(f32[512,512]{1,0:T(8,128)S(1)} %add.3.refs_0_), channel_id=1, source_target_pairs={{0,16},{1,49},{2,18},{3,51},{4,20},{5,53},{6,22},{7,55},{8,24},{9,... | collective-permute-start | bytes 3145736 | tf_op jit(solution)/shard_map/t_bF/ppermute | solution.py:54
  102.2 10.0 %copy-start.6 = (f32[2048,128]{1,0:T(8,128)}, f32[2048,128]{1,0:T(8,128)S(1)}, u32[]{:S(2)}) copy-start(f32[2048,128]{1,0:T(8,128)S(1)} %collective-permute-done.14.refs_12_.refs_10_) | copy-start | bytes 3145732
  102.3 21.8 %collective-permute-start.19 = (f32[2048,128]{1,0:T(8,128)}, f32[2048,128]{1,0:T(8,128)S(1)}, u32[]{:S(2)}, u32[]{:S(2)}) collective-permute-start(f32[2048,128]{1,0:T(8,128)} %collective-permute-done.15.refs_13_.refs_11_), channel_id=1, source_target_pairs={{0,2},{1,7},{2,4},{3,1},{4,6},{5,3},{6,0},{7,5},{8,10},{9,15},{10,... | collective-permute-start | bytes 3145736 | tf_op jit(solution)/shard_map/t_YH/ppermute | solution.py:38
  102.7 21.3 %copy-start.7 = (f32[2048,128]{1,0:T(8,128)}, f32[2048,128]{1,0:T(8,128)S(1)}, u32[]{:S(2)}) copy-start(f32[2048,128]{1,0:T(8,128)S(1)} %collective-permute-done.10.refs_8_.refs_6_) | copy-start | bytes 3145732
  102.7 23.2 %collective-permute-start.21 = (f32[512,512]{1,0:T(8,128)S(1)}, f32[512,512]{1,0:T(8,128)S(1)}, u32[]{:S(2)}, u32[]{:S(2)}) collective-permute-start(f32[512,512]{1,0:T(8,128)S(1)} %add.3.refs_0_), channel_id=1, source_target_pairs={{0,48},{1,17},{2,50},{3,19},{4,52},{5,21},{6,54},{7,23},{8,56},{9,... | collective-permute-start | bytes 3145736 | tf_op jit(solution)/shard_map/t_bG/ppermute | solution.py:54
  110.6 19.6 %collective-permute-start.16 = (f32[2048,128]{1,0:T(8,128)}, f32[2048,128]{1,0:T(8,128)}, u32[]{:S(2)}, u32[]{:S(2)}) collective-permute-start(f32[2048,128]{1,0:T(8,128)} %collective-permute-done.15.refs_13_.refs_11_), channel_id=1, source_target_pairs={{0,1},{1,0},{2,3},{3,2},{4,5},{5,4},{6,7},{7,6},{8,9},{9,8},{10,11... | collective-permute-start | bytes 3145736 | tf_op jit(solution)/shard_map/t_cYF/ppermute | solution.py:38
  112.1 11.9 %copy-start.8 = (f32[2048,128]{1,0:T(8,128)}, f32[2048,128]{1,0:T(8,128)S(1)}, u32[]{:S(2)}) copy-start(f32[2048,128]{1,0:T(8,128)S(1)} %collective-permute-done.9.refs_6_.refs_4_) | copy-start | bytes 3145732
  112.1 18.1 %collective-permute-start.18 = (f32[2048,128]{1,0:T(8,128)}, f32[2048,128]{1,0:T(8,128)}, u32[]{:S(2)}, u32[]{:S(2)}) collective-permute-start(f32[2048,128]{1,0:T(8,128)} %collective-permute-done.17.refs_15_.refs_13_), channel_id=1, source_target_pairs={{0,1},{1,0},{2,3},{3,2},{4,5},{5,4},{6,7},{7,6},{8,9},{9,8},{10,11... | collective-permute-start | bytes 3145736 | tf_op jit(solution)/shard_map/t_cYG/ppermute | solution.py:38
  124.0 6.2 %collective-permute-start.12 = (f32[2048,128]{1,0:T(8,128)}, f32[2048,128]{1,0:T(8,128)}, u32[]{:S(2)}, u32[]{:S(2)}) collective-permute-start(f32[2048,128]{1,0:T(8,128)} %collective-permute-done.11.refs_9_.refs_7_), channel_id=1, source_target_pairs={{0,1},{1,0},{2,3},{3,2},{4,5},{5,4},{6,7},{7,6},{8,9},{9,8},{10,11... | collective-permute-start | bytes 3145736 | tf_op jit(solution)/shard_map/t_cH/ppermute | solution.py:38
  124.0 6.2 %collective-permute-start.20 = (f32[2048,128]{1,0:T(8,128)S(1)}, f32[2048,128]{1,0:T(8,128)}, u32[]{:S(2)}, u32[]{:S(2)}) collective-permute-start(f32[2048,128]{1,0:T(8,128)S(1)} %collective-permute-done.19.refs_17_.refs_15_), channel_id=1, source_target_pairs={{0,1},{1,0},{2,3},{3,2},{4,5},{5,4},{6,7},{7,6},{8,9},{9,8},{10,11... | collective-permute-start | bytes 3145736 | tf_op jit(solution)/shard_map/t_cYH/ppermute | solution.py:38
  126.9 21.3 %collective-permute-start.7 = (f32[512,512]{1,0:T(8,128)}, f32[512,512]{1,0:T(8,128)}, u32[]{:S(2)}, u32[]{:S(2)}) collective-permute-start(f32[512,512]{1,0:T(8,128)} %collective-permute-done.5.refs_1_), channel_id=1, source_target_pairs={{0,16},{1,49},{2,18},{3,51},{4,20},{5,53},{6,22},{7,55},{8,24},{9,... | collective-permute-start | bytes 3145736 | tf_op jit(solution)/shard_map/t_bH/ppermute | solution.py:54
  (4 other events, 17.4 us)
